TPU v7x, 256 devices: a whole 4x4x8 slice. The times are simulated.
256 devices in a mesh: leaf: 128 (over x, y, z), vec: 2 (over core).
Axes of the slice: x: 4, y: 4, z: 8, core: 2. Of those that a mesh axis runs over, the one named last changes fastest.
Arguments:
- points: bfloat16 [3, 1048576], P(None, 'leaf'), may hold values from -4 to 4
- vectors: bfloat16 [16, 1048576], P('vec', 'leaf'), may hold values from -6 to 6
- leaf_order: int32 [128, 8192], P('leaf'), may hold values from 0 to 8191, each once within a row
- leaf_bases: bfloat16 [2048, 64, 512], P('leaf'), may hold values from -0.25 to 0.25
- transfers: bfloat16 [3840, 64, 64], P('leaf'), may hold values from -0.5 to 0.5
- coupling_blocks: bfloat16 [32768, 64, 64], P('leaf'), may hold values from -0.75 to 0.75
- block_source: int32 [32768], P('leaf'), may hold values from 0 to 30, as said below
- block_owner: int32 [32768, 1], P('leaf'), may hold values from 0 to 127; in each aligned block of 256 rows (0 to 255, 256 to 511, ...) at most 4 rows name the same one
- block_target: int32 [32768], P('leaf'), may hold values from 0 to 30, as said below
- up_transfer: bfloat16 [254, 64, 64], replicated, may hold values from -0.5 to 0.5
- up_coupling: bfloat16 [254, 64, 64], replicated, as said below
Outputs:
- product: bfloat16 [16, 1048576], P('vec', 'leaf')
Inputs may be any that keep to these rules, and one draw needn't show every extreme that they name: `leaf_order`: within each row, each point of the device once. `block_source`: A cluster of the subtree of the device that stores the block, numbered leaves first and level by level up to the root. `block_target`: A cluster of the subtree of the device block_owner names, in the same numbering, on the same level as the block's source cluster. `block_owner`: of the 256 blocks stored on one device, at most 4 name the same device, and exactly 4 name some device; every device is named by some block. `up_coupling`: coupling matrices of sibling clusters of the upper tree, finite.
All inputs are finite; a program needn't handle non-finite values.
Results may differ from a plain program's by a relative error of at most 0.0065.
Values may be sent and summed in bfloat16 or wider, within the bound.
No kernel may reach another device: no remote copies, remote signals or barrier semaphores. Data moves between devices by JAX's collectives and lax.ppermute only.
A program may use at most 128 MiB of HBM per device.

v0:
```python
import jax
import jax.numpy as jnp
from jax import lax
from jax.sharding import PartitionSpec as P

NEAR = 2


near_scale = 8.0
smooth_sq = 0.0025
highest = lax.Precision.HIGHEST


def extended(shard, sides, width):
    for axis, dim in sides:
        peers, length = (lax.axis_size(axis), shard.shape[dim])
        up = [(i, (i + 1) % peers) for i in range(peers - 1)]
        down = [(j, i) for i, j in up]
        last = lax.slice_in_dim(shard, length - width, length, axis=dim)
        first = lax.slice_in_dim(shard, 0, width, axis=dim)
        before = lax.ppermute(last, axis, up)
        after = lax.ppermute(first, axis, down)
        shard = jnp.concatenate([before, shard, after], axis=dim)
    return shard


def partner_2(value, axis, distance):
    mask = 2**distance
    pairs = [(source, source ^ mask) for source in range(lax.axis_size(axis))]
    return lax.ppermute(value, axis, pairs)


def kernel_block(sources, targets):
    source_f = sources.astype(jnp.float32)
    target_f = targets.astype(jnp.float32)
    distance = (source_f[0][:, None] - target_f[0][None, :]) ** 2
    distance = distance + (source_f[1][:, None] - target_f[1][None, :]) ** 2
    distance = distance + (source_f[2][:, None] - target_f[2][None, :]) ** 2
    return lax.rsqrt(distance + smooth_sq).astype(jnp.bfloat16)


def near_block(padded, first_leaf, number, leaf_len):
    reach = NEAR * leaf_len
    window_len = (2 * NEAR + 1) * leaf_len

    def one_leaf(leaf_no):
        start_col = (first_leaf + leaf_no) * leaf_len
        targets = lax.dynamic_slice_in_dim(padded, start_col + reach, leaf_len, 1)
        window = lax.dynamic_slice_in_dim(padded, start_col, window_len, 1)
        kernel = kernel_block(window[:3], targets[:3])
        return jnp.dot(window[3:], kernel, preferred_element_type=jnp.float32) * (
            near_scale / leaf_len
        )

    per_leaf = lax.map(one_leaf, jnp.arange(number, dtype=jnp.int32))
    return jnp.transpose(per_leaf, (1, 0, 2)).reshape(per_leaf.shape[1], number * leaf_len)


def climb(children, matrices):
    moved_rows = jnp.einsum(
        "...jvk,...jkp->...jvp", children, matrices.astype(jnp.float32), precision=highest
    )
    return moved_rows[..., 0::2, :, :] + moved_rows[..., 1::2, :, :]


def descend(parent, matrices):
    spread = jnp.repeat(parent, 2, axis=-3)
    return jnp.einsum(
        "...jvp,...jkp->...jvk", spread, matrices.astype(jnp.float32), precision=highest
    )


def permute_columns(data, permute, forward):
    count = permute.shape[0]
    block_len = min(512, count)
    all_ids = jnp.arange(count, dtype=jnp.int32)

    def one_block(start):
        if forward:
            picks = lax.dynamic_slice_in_dim(permute, start, block_len, 0)
            select = (all_ids[:, None] == picks[None, :]).astype(jnp.bfloat16)
        else:
            wanted = start + jnp.arange(block_len, dtype=jnp.int32)
            select = (permute[:, None] == wanted[None, :]).astype(jnp.bfloat16)
        return jnp.dot(data, select, preferred_element_type=jnp.float32)

    starts = jnp.arange(count // block_len, dtype=jnp.int32) * block_len
    blocks = lax.map(one_block, starts)
    return jnp.transpose(blocks, (1, 0, 2)).reshape(data.shape[0], count).astype(jnp.bfloat16)


def shards(
    points,
    vectors,
    leaf_order,
    leaf_bases,
    transfers,
    coupling_blocks,
    block_source,
    block_owner,
    block_target,
    up_transfer,
    up_coupling,
):
    leaf_dev, rank_width, leaf_len = leaf_bases.shape
    local_cols = vectors.shape[0]
    tree_perm = leaf_order[0]
    both_tree = permute_columns(jnp.concatenate([points, vectors], axis=0), tree_perm, True)
    points_tree = both_tree[:3]
    vectors_tree = both_tree[3:]
    reach = NEAR * leaf_len
    all_columns = lax.all_gather(vectors_tree, "vec", axis=0, tiled=True)
    joined = jnp.concatenate([points_tree, all_columns], axis=0)
    padded = extended(joined, (("leaf", 1),), reach)
    half_leaves = leaf_dev // lax.axis_size("vec")
    first_leaf = lax.axis_index("vec") * half_leaves
    near_all = near_block(padded, first_leaf, half_leaves, leaf_len)
    near_part = lax.all_to_all(near_all, "vec", split_axis=0, concat_axis=1, tiled=True)
    shaped = vectors_tree.reshape(local_cols, leaf_dev, leaf_len)
    leaf_coeff = jnp.einsum("vlp,lkp->lvk", shaped, leaf_bases, preferred_element_type=jnp.float32)
    levels = [leaf_coeff]
    offset = 0
    number = leaf_dev
    while number > 1:
        levels.append(climb(levels[-1], transfers[offset : offset + number]))
        offset += number
        number //= 2
    all_coeff = jnp.concatenate(levels, axis=0)
    root_coeff = levels[-1][0]
    device = lax.axis_index("leaf")
    peer_count = lax.axis_size("leaf")
    current = root_coeff
    gain_list = []
    offset = 0
    number = peer_count
    for level_no in range(peer_count.bit_length() - 1):
        partner = partner_2(current, "leaf", level_no)
        node_index = jnp.right_shift(device, level_no)
        is_odd = node_index % 2 == 1
        pair_start = offset + node_index - node_index % 2
        pair_mats = lax.dynamic_slice_in_dim(up_transfer, pair_start, 2, 0).astype(jnp.float32)
        own_coupling = lax.dynamic_index_in_dim(
            up_coupling, offset + node_index, 0, keepdims=False
        ).astype(jnp.float32)
        even_part = jnp.where(is_odd, partner, current)
        odd_part = jnp.where(is_odd, current, partner)
        own_matrix = jnp.where(is_odd, pair_mats[1], pair_mats[0])
        gain_list.append((own_matrix, jnp.dot(partner, own_coupling, precision=highest)))
        current = jnp.dot(even_part, pair_mats[0], precision=highest) + jnp.dot(
            odd_part, pair_mats[1], precision=highest
        )
        offset += number
        number //= 2
    top_down = jnp.zeros_like(current)
    for own_matrix, gain_term in reversed(gain_list):
        top_down = jnp.dot(top_down, own_matrix.T, precision=highest) + gain_term
    coeff_bf = all_coeff.astype(jnp.bfloat16)
    clusters = all_coeff.shape[0]
    blocks_dev = coupling_blocks.shape[0]
    capacity = max(2, 2 * blocks_dev // peer_count)
    flat_len = local_cols * rank_width
    source_hot = (block_source[:, None] == jnp.arange(clusters, dtype=jnp.int32)[None, :]).astype(
        jnp.bfloat16
    )
    picked = (
        jnp.dot(
            source_hot, coeff_bf.reshape(clusters, flat_len), preferred_element_type=jnp.float32
        )
        .astype(jnp.bfloat16)
        .reshape(blocks_dev, local_cols, rank_width)
    )
    dest_dev = block_owner[:, 0]
    matches = (dest_dev[:, None] == jnp.arange(peer_count, dtype=jnp.int32)[None, :]).astype(
        jnp.float32
    )
    block_ids = jnp.arange(blocks_dev, dtype=jnp.int32)
    earlier = (block_ids[None, :] < block_ids[:, None]).astype(jnp.float32)
    before_count = jnp.dot(earlier, matches, precision=highest)
    slot_rank = jnp.sum(before_count * matches, axis=1).astype(jnp.int32)
    slots = dest_dev * capacity + slot_rank
    slot_total = peer_count * capacity
    slot_hot_int = (jnp.arange(slot_total, dtype=jnp.int32)[:, None] == slots[None, :]).astype(
        jnp.int32
    )
    slot_used = jnp.sum(slot_hot_int, axis=1)
    labels = jnp.sum(slot_hot_int * block_target[None, :], axis=1) + clusters * (1 - slot_used)
    products = jnp.einsum(
        "bvk,bkp->bvp", picked, coupling_blocks, preferred_element_type=jnp.float32
    )
    send_rows = jnp.dot(
        slot_hot_int.astype(jnp.float32), products.reshape(blocks_dev, flat_len), precision=highest
    )
    received, got_labels = (
        lax.all_to_all(send_rows, "leaf", split_axis=0, concat_axis=0, tiled=True),
        lax.all_to_all(labels, "leaf", split_axis=0, concat_axis=0, tiled=True),
    )
    one_hot = (got_labels[:, None] == jnp.arange(clusters, dtype=jnp.int32)[None, :]).astype(
        jnp.float32
    )
    coupled = jnp.einsum("sc,sf->cf", one_hot, received, precision=highest).reshape(
        clusters, local_cols, rank_width
    )
    current = (top_down + coupled[clusters - 1])[None]
    number = 1
    while number < leaf_dev:
        number *= 2
        offset = 2 * leaf_dev - 2 * number
        current = (
            descend(current, transfers[offset : offset + number])
            + coupled[offset : offset + number]
        )
    down_leaf = current.astype(jnp.bfloat16)
    far_part = jnp.einsum(
        "lvk,lkp->vlp", down_leaf, leaf_bases, preferred_element_type=jnp.float32
    ).reshape(local_cols, leaf_dev * leaf_len)
    tree_out = (far_part + near_part).astype(jnp.bfloat16)
    return permute_columns(tree_out, tree_perm, False)


def solution(mesh):
    return jax.shard_map(
        shards,
        mesh=mesh,
        in_specs=(
            P(None, "leaf"),
            P("vec", "leaf"),
            P("leaf", None),
            P("leaf", None, None),
            P("leaf", None, None),
            P("leaf", None, None),
            P("leaf"),
            P("leaf", None),
            P("leaf"),
            P(),
            P(),
        ),
        out_specs=P("vec", "leaf"),
        check_vma=False,
    )
```

profile of v0, /device:TPU:8, one launch (start us, length us, event | category | flops | bytes accessed | tf_op | source)
XLA Modules:
  0.0 395.2 jit_solution(16733925718658472927)
XLA Ops:
  1.6 106.3 %while.35 = (s32[]{:T(128)}, bf16[16,11,512]{2,1,0:T(8,128)(2,1)S(1)}, s32[16]{0:T(128)}, s32[8192]{0:T(1024)}, bf16[11,8192]{1,0:T(8,128)(2,1)S(1)}, /*index=5*/s32[]{:T(128)}, s32[]{:T(128)}, s32[]{:T(128)}) while((s32[]{:T(128)}, bf16[16,11,512]{2,1,0:T(8,128)(2,1)S(1)}, s32[16]{0:T(128)}, s32[8192]{0:T(1024)}, ...), condition=%wide.region_1.2_spmd.clone, body=%wide.region_0.1_spmd.clone.sunk | while | flops 96468992 | bytes 301195 | solution.py:88
  119.0 14.9 %all-to-all-start = ((s32[128,4,1]{1,2,0:T(1,128)}), s32[128,4,1]{1,2,0:T(1,128)}, u32[]{:S(2)}, u32[]{:S(2)}) async-start(s32[128,4,1]{1,2,0:T(1,128)} %bitcast.39), calls=%async_computation | async-start | bytes 131072 | tf_op jit(solution)/shard_map/all_to_all | solution.py:195
  136.7 3.4 collective-permute-start.7
  140.1 4.6 %collective-permute-start.8 = (bf16[19,1024]{1,0:T(8,128)(2,1)}, bf16[19,1024]{1,0:T(8,128)(2,1)}, u32[]{:S(2)}, u32[]{:S(2)}) collective-permute-start(bf16[19,1024]{1,0:T(8,128)(2,1)} %get-tuple-element.197), channel_id=1, source_target_pairs={{2,0},{4,2},{6,4},{8,6},{10,8},{12,10},{14,12},{16,14},{18,16},{20... | collective-permute-start | bytes 116744 | tf_op jit(solution)/shard_map/ppermute | solution.py:22
  146.7 5.5 %constant_dynamic-slice_fusion.12 = (bf16[2,64,64]{0,2,1:T(8,128)(2,1)}, bf16[2,64,64]{0,2,1:T(8,128)(2,1)}, bf16[2,64,64]{0,2,1:T(8,128)(2,1)}, bf16[2,64,64]{0...) fusion(bf16[254,64,64]{0,2,1:T(8,128)(2,1)S(1)} %copy-done.1, ...), kind=kLoop, calls=%fused_computation.173 | loop fusion | bytes 229404 | tf_op jit(solution)/shard_map/dynamic_slice | solution.py:141
  170.7 6.6 %copy.73 = bf16[256,64,64]{2,1,0:T(8,128)(2,1)} copy(bf16[256,64,64]{0,2,1:T(8,128)(2,1)S(1)} %copy-done.7) | data formatting | bytes 4194304 | tf_op args[5]
  177.6 4.3 %collective-permute-start.2 = (f32[8,64]{1,0:T(8,128)S(1)}, f32[8,64]{1,0:T(8,128)S(1)}, u32[]{:S(2)}, u32[]{:S(2)}) collective-permute-start(f32[8,64]{1,0:T(8,128)S(1)} %convolution_add_fusion.15), channel_id=1, source_target_pairs={{0,8},{2,10},{4,12},{6,14},{8,0},{10,2},{12,4},{14,6},{16,24},{18,... | collective-permute-start | bytes 6152 | tf_op jit(solution)/shard_map/ppermute | solution.py:30
  181.8 4.5 %fusion.131 = f32[256,8,64]{2,1,0:T(8,128)} fusion(bf16[256,8,64]{2,1,0:T(8,128)(2,1)} %copy.72, bf16[256,64,64]{2,1,0:T(8,128)(2,1)} %copy.73), kind=kOutput, calls=%fused_computation.201 | convolution fusion | flops 16777216 | bytes 2883584 | tf_op jit(solution)/shard_map/bvk,bkp->bvp/dot_general | solution.py:187
  191.0 5.2 %constant_dynamic-slice_fusion = (bf16[1,64,64]{0,2,1:T(8,128)(2,1)}, bf16[1,64,64]{0,2,1:T(8,128)(2,1)}, bf16[1,64,64]{0,2,1:T(8,128)(2,1)}, bf16[1,64,64]{0,2,...) fusion(bf16[254,64,64]{0,2,1:T(8,128)(2,1)S(1)} %copy-done.2, ...), kind=kLoop, calls=%fused_computation.161 | loop fusion | bytes 114716 | tf_op jit(solution)/shard_map/jit(dynamic_index_in_dim)/dynamic_slice | solution.py:142
  246.5 8.4 %all-to-all-start.1 = ((f32[128,4,512]{2,1,0:T(4,128)}), f32[128,4,512]{2,1,0:T(4,128)S(1)}, u32[]{:S(2)}, u32[]{:S(2)}) async-start(f32[128,4,512]{2,1,0:T(4,128)} %copy.76), calls=%async_computation.1 | async-start | bytes 2097152 | tf_op jit(solution)/shard_map/all_to_all | solution.py:194
  268.7 31.6 %while.33 = (s32[]{:T(128)}, f32[8,16,512]{2,1,0:T(8,128)}, s32[8]{0:T(128)S(1)}, s32[]{:T(128)}, bf16[19,10240]{1,0:T(8,128)(2,1)S(1)}, /*index=5*/s32[]{:T(128...) while((s32[]{:T(128)}, f32[8,16,512]{2,1,0:T(8,128)}, s32[8]{0:T(128)S(1)}, ...), condition=%wide.region_6.7_spmd, body=%wide.region_5.6_spmd.sunk | while | flops 55067660 | bytes 287493 | solution.py:55
  302.2 3.7 all-to-all-start.2
  313.1 82.2 %while.34 = (s32[]{:T(128)}, bf16[16,8,512]{2,1,0:T(8,128)(2,1)}, s32[1,8192]{1,0:T(1,128)S(1)}, s32[16]{0:T(128)}, bf16[8,8192]{1,0:T(8,128)(2,1)S(1)}, /*index=5*/s32[]{:T(128)}) while((s32[]{:T(128)}, bf16[16,8,512]{2,1,0:T(8,128)(2,1)}, s32[1,8192]{1,0:T(1,128)S(1)}, s32[16]{0:T(128)}, bf16[8,8192]{1,0:T(8,128)(2,1)S(1)}, ...), condition=%wide.region_8.9_spmd, body=%wide.region_7.8_spmd.sunk | while | flops 71303680 | bytes 184917 | solution.py:88
  315.0 3.2 fusion.173
  320.1 3.2 fusion.173
  325.3 3.2 fusion.173
  330.4 3.2 fusion.173
  335.5 3.2 fusion.173
  340.7 3.2 fusion.173
  345.8 3.2 fusion.173
  350.9 3.2 fusion.173
  361.2 3.2 fusion.173
  371.5 3.2 fusion.173
  381.8 3.2 fusion.173
  (302 shorter events, 262.8 us)
Async XLA Ops:
  0.0 107.8 %copy-start = (bf16[16,64,512]{2,1,0:T(8,128)(2,1)S(1)}, bf16[16,64,512]{2,1,0:T(8,128)(2,1)}, u32[]{:S(2)}) copy-start(bf16[16,64,512]{2,1,0:T(8,128)(2,1)} %param.20) | copy-start | bytes 3145732
  107.8 38.8 %copy-start.1 = (bf16[254,64,64]{0,2,1:T(8,128)(2,1)S(1)}, bf16[254,64,64]{0,2,1:T(8,128)(2,1)}, u32[]{:S(2)}) copy-start(bf16[254,64,64]{0,2,1:T(8,128)(2,1)} %param.26) | copy-start | bytes 6242308
  111.2 22.7 %copy-start.8 = (f32[8,8,64]{2,1,0:T(8,128)}, f32[8,8,64]{2,1,0:T(8,128)S(1)}, u32[]{:S(2)}) copy-start(f32[8,8,64]{2,1,0:T(8,128)S(1)} %fusion.37) | copy-start | bytes 49156
  113.8 47.7 %collective-permute-start = (f32[8,64]{1,0:T(8,128)}, f32[8,64]{1,0:T(8,128)}, u32[]{:S(2)}, u32[]{:S(2)}) collective-permute-start(f32[8,64]{1,0:T(8,128)} %get-tuple-element.198), channel_id=1, source_target_pairs={{0,2},{2,0},{4,6},{6,4},{8,10},{10,8},{12,14},{14,12},{16,18},{18,... | collective-permute-start | bytes 6152 | tf_op jit(solution)/shard_map/ppermute | solution.py:30
  119.0 127.5 %all-to-all-start = ((s32[128,4,1]{1,2,0:T(1,128)}), s32[128,4,1]{1,2,0:T(1,128)}, u32[]{:S(2)}, u32[]{:S(2)}) async-start(s32[128,4,1]{1,2,0:T(1,128)} %bitcast.39), calls=%async_computation | async-start | bytes 131072 | tf_op jit(solution)/shard_map/all_to_all | solution.py:195
  136.7 131.0 %collective-permute-start.7 = (bf16[19,1024]{1,0:T(8,128)(2,1)}, bf16[19,1024]{1,0:T(8,128)(2,1)}, u32[]{:S(2)}, u32[]{:S(2)}) collective-permute-start(bf16[19,1024]{1,0:T(8,128)(2,1)} %get-tuple-element.196), channel_id=1, source_target_pairs={{0,2},{2,4},{4,6},{6,8},{8,10},{10,12},{12,14},{14,16},{16,18},{18... | collective-permute-start | bytes 116744 | tf_op jit(solution)/shard_map/ppermute | solution.py:21
  140.1 127.6 %collective-permute-start.8 = (bf16[19,1024]{1,0:T(8,128)(2,1)}, bf16[19,1024]{1,0:T(8,128)(2,1)}, u32[]{:S(2)}, u32[]{:S(2)}) collective-permute-start(bf16[19,1024]{1,0:T(8,128)(2,1)} %get-tuple-element.197), channel_id=1, source_target_pairs={{2,0},{4,2},{6,4},{8,6},{10,8},{12,10},{14,12},{16,14},{18,16},{20... | collective-permute-start | bytes 116744 | tf_op jit(solution)/shard_map/ppermute | solution.py:22
  152.2 18.5 %copy-start.7 = (bf16[256,64,64]{0,2,1:T(8,128)(2,1)S(1)}, bf16[256,64,64]{0,2,1:T(8,128)(2,1)}, u32[]{:S(2)}) copy-start(bf16[256,64,64]{0,2,1:T(8,128)(2,1)} %param.22) | copy-start | bytes 6291460
  163.1 14.3 %collective-permute-start.1 = (f32[8,64]{1,0:T(8,128)S(1)}, f32[8,64]{1,0:T(8,128)S(1)}, u32[]{:S(2)}, u32[]{:S(2)}) collective-permute-start(f32[8,64]{1,0:T(8,128)S(1)} %convolution_add_fusion.16), channel_id=1, source_target_pairs={{0,4},{2,6},{4,0},{6,2},{8,12},{10,14},{12,8},{14,10},{16,20},{18,... | collective-permute-start | bytes 6152 | tf_op jit(solution)/shard_map/ppermute | solution.py:30
  177.3 18.9 %copy-start.12 = (f32[8,64]{1,0:T(8,128)}, f32[8,64]{1,0:T(8,128)S(1)}, u32[]{:S(2)}) copy-start(f32[8,64]{1,0:T(8,128)S(1)} %collective-permute-done.1) | copy-start | bytes 6148
  177.6 11.1 %collective-permute-start.2 = (f32[8,64]{1,0:T(8,128)S(1)}, f32[8,64]{1,0:T(8,128)S(1)}, u32[]{:S(2)}, u32[]{:S(2)}) collective-permute-start(f32[8,64]{1,0:T(8,128)S(1)} %convolution_add_fusion.15), channel_id=1, source_target_pairs={{0,8},{2,10},{4,12},{6,14},{8,0},{10,2},{12,4},{14,6},{16,24},{18,... | collective-permute-start | bytes 6152 | tf_op jit(solution)/shard_map/ppermute | solution.py:30
  190.4 8.3 %collective-permute-start.3 = (f32[8,64]{1,0:T(8,128)S(1)}, f32[8,64]{1,0:T(8,128)S(1)}, u32[]{:S(2)}, u32[]{:S(2)}) collective-permute-start(f32[8,64]{1,0:T(8,128)S(1)} %convolution_add_fusion.14), channel_id=1, source_target_pairs={{0,16},{2,18},{4,20},{6,22},{8,24},{10,26},{12,28},{14,30},{16,0},... | collective-permute-start | bytes 6152 | tf_op jit(solution)/shard_map/ppermute | solution.py:30
  196.2 19.4 %copy-start.3 = (bf16[2,64,64]{0,2,1:T(8,128)(2,1)S(1)}, bf16[2,64,64]{0,2,1:T(8,128)(2,1)}, u32[]{:S(2)}) copy-start(bf16[2,64,64]{0,2,1:T(8,128)(2,1)} %get-tuple-element.194) | copy-start | bytes 49156
  198.7 34.2 %copy-start.14 = (f32[8,64]{1,0:T(8,128)}, f32[8,64]{1,0:T(8,128)S(1)}, u32[]{:S(2)}) copy-start(f32[8,64]{1,0:T(8,128)S(1)} %collective-permute-done.3) | copy-start | bytes 6148
  200.4 7.6 %collective-permute-start.4 = (f32[8,64]{1,0:T(8,128)S(1)}, f32[8,64]{1,0:T(8,128)S(1)}, u32[]{:S(2)}, u32[]{:S(2)}) collective-permute-start(f32[8,64]{1,0:T(8,128)S(1)} %convolution_add_fusion.13), channel_id=1, source_target_pairs={{0,32},{2,34},{4,36},{6,38},{8,40},{10,42},{12,44},{14,46},{16,48}... | collective-permute-start | bytes 6152 | tf_op jit(solution)/shard_map/ppermute | solution.py:30
  208.1 31.7 %copy-start.15 = (f32[8,64]{1,0:T(8,128)}, f32[8,64]{1,0:T(8,128)S(1)}, u32[]{:S(2)}) copy-start(f32[8,64]{1,0:T(8,128)S(1)} %collective-permute-done.4) | copy-start | bytes 6148
  209.8 7.8 %collective-permute-start.5 = (f32[8,64]{1,0:T(8,128)S(1)}, f32[8,64]{1,0:T(8,128)S(1)}, u32[]{:S(2)}, u32[]{:S(2)}) collective-permute-start(f32[8,64]{1,0:T(8,128)S(1)} %convolution_add_fusion.12), channel_id=1, source_target_pairs={{0,64},{2,66},{4,68},{6,70},{8,72},{10,74},{12,76},{14,78},{16,80}... | collective-permute-start | bytes 6152 | tf_op jit(solution)/shard_map/ppermute | solution.py:30
  215.7 26.4 %copy-start.6 = (bf16[1,64,64]{0,2,1:T(8,128)(2,1)S(1)}, bf16[1,64,64]{0,2,1:T(8,128)(2,1)}, u32[]{:S(2)}) copy-start(bf16[1,64,64]{0,2,1:T(8,128)(2,1)} %get-tuple-element.183) | copy-start | bytes 24580
  217.6 24.5 %copy-start.16 = (f32[8,64]{1,0:T(8,128)}, f32[8,64]{1,0:T(8,128)S(1)}, u32[]{:S(2)}) copy-start(f32[8,64]{1,0:T(8,128)S(1)} %collective-permute-done.5) | copy-start | bytes 6148
  219.9 37.8 %collective-permute-start.6 = (f32[8,64]{1,0:T(8,128)}, f32[8,64]{1,0:T(8,128)}, u32[]{:S(2)}, u32[]{:S(2)}) collective-permute-start(f32[8,64]{1,0:T(8,128)} %convolution_add_fusion.11), channel_id=1, source_target_pairs={{0,128},{2,130},{4,132},{6,134},{8,136},{10,138},{12,140},{14,142}... | collective-permute-start | bytes 6152 | tf_op jit(solution)/shard_map/ppermute | solution.py:30
  239.8 27.7 %copy-start.9 = (f32[2,64,64]{2,1,0:T(8,128)S(1)}, f32[2,64,64]{2,1,0:T(8,128)}, u32[]{:S(2)}) copy-start(f32[2,64,64]{2,1,0:T(8,128)} %convert_element_type.120) | copy-start | bytes 98308
  246.5 55.6 %all-to-all-start.1 = ((f32[128,4,512]{2,1,0:T(4,128)}), f32[128,4,512]{2,1,0:T(4,128)S(1)}, u32[]{:S(2)}, u32[]{:S(2)}) async-start(f32[128,4,512]{2,1,0:T(4,128)} %copy.76), calls=%async_computation.1 | async-start | bytes 2097152 | tf_op jit(solution)/shard_map/all_to_all | solution.py:194
  268.7 37.6 %copy-start.18 = (s32[512]{0:T(512)S(1)}, s32[512]{0:T(512)}, u32[]{:S(2)}) copy-start(s32[512]{0:T(512)} %eq.148) | copy-start | bytes 6148
  302.2 10.9 %all-to-all-start.2 = ((f32[2,8,4096]{2,1,0:T(8,128)}), f32[2,8,4096]{2,1,0:T(8,128)S(1)}, u32[]{:S(2)}, u32[]{:S(2)}) async-start(f32[2,8,4096]{2,1,0:T(8,128)} %all_to_all.27), calls=%async_computation.2 | async-start | bytes 524288 | tf_op jit(solution)/shard_map/all_to_all | solution.py:118
  (8 other events, 104.0 us)
where the time goes:
time: 402 us; the launch traced here: 395 us
  matrix products  158 us (39%)
  local copies, waits for them, and re-layouts  122 us (30%)
  starting transfers between devices  49.3 us (12%)
  loops' own time  35.5 us (9%)
  other arithmetic  28 us (7%)
    dot_general x32, matrix products, one_block(): return jnp.dot(data, select, preferred_element_type=jnp.float32)  94.8 us
    dynamic_slice x32, local copies, waits for them, and re-layouts, permute_columns(): blocks = lax.map(one_block, starts)  40.7 us
    unnamed x55, local copies, waits for them, and re-layouts  32.5 us
    another operation x2, loops' own time, permute_columns(): blocks = lax.map(one_block, starts)  30.4 us
    dot_general x8, matrix products, one_leaf(): jnp.dot(window[3:], kernel, preferred_element_type=jnp.float32)  21 us
    all_to_all x1, starting transfers between devices, shards(): lax.all_to_all(labels, 'leaf', split_axis=0, concat_axis=0, tiled=True)  14.9 us
    ppermute x7, starting transfers between devices, partner_2(): return lax.ppermute(value, axis, pairs)  14.4 us
    dynamic_slice x16, local copies, waits for them, and re-layouts, one_block(): picks = lax.dynamic_slice_in_dim(permute, start, block_len, 0)  12.4 us
  transfers between devices with their start and end apart: 12, of which 0 were waited for; matrix products, arithmetic and copies ran while one was open for 36% of the time, Pallas kernels for 0%

commit v1 on v0

v1 whole, which is shorter than its diff:
```python
import jax
import jax.numpy as jnp
import ml_dtypes
from jax import lax
from jax.experimental import pallas as pl
from jax.experimental.pallas import tpu as pltpu
from jax.sharding import PartitionSpec as P

f32 = jnp.float32
bf16 = jnp.bfloat16
i32 = jnp.int32

LEAF = 512
COLS = 8192
HALO = 1024
LOCAL = 5120
HALF = 4096
NT = (((1,), (1,)), ((), ()))
TN = (((0,), (0,)), ((), ()))
SMOOTH_HI = float(ml_dtypes.bfloat16(0.0025))
SMOOTH_LO = float(ml_dtypes.bfloat16(0.0025 - SMOOTH_HI))
VM = pl.BlockSpec(memory_space=pltpu.VMEM)


def dot(a, b, dims=(((1,), (0,)), ((), ()))):
    return lax.dot_general(a, b, dims, preferred_element_type=f32)


def iota(shape, dim):
    return lax.broadcasted_iota(i32, shape, dim)


def hot(mask):
    return jnp.where(mask, 1.0, 0.0).astype(bf16)


def halves(x):
    hi = x.astype(bf16)
    lo = (x - hi.astype(f32)).astype(bf16)
    return jnp.concatenate([hi, lo], axis=0)


def wide(x):
    return jnp.concatenate([x, jnp.zeros_like(x)], axis=1)


def dot_pair(x, w, dims=(((1,), (0,)), ((), ()))):
    y = dot(halves(x), w, dims)
    n = x.shape[0]
    return y[:n] + y[n:]


def call(kernel, outs, scratch, args, flops, nbytes, vmem=48):
    return pl.pallas_call(
        kernel,
        out_shape=[jax.ShapeDtypeStruct(s, d) for s, d in outs],
        in_specs=[VM] * len(args),
        out_specs=[VM] * len(outs),
        scratch_shapes=scratch,
        compiler_params=pltpu.CompilerParams(vmem_limit_bytes=vmem << 20),
        cost_estimate=pl.CostEstimate(flops=flops, bytes_accessed=nbytes, transcendentals=0),
    )(*args)


def gather_kernel(pts, vec, perm, vt, pt, send_a, send_b, send_c, dv, dp):
    core = lax.axis_index("vec")
    for m in range(16):
        a, b = 512 * m, 512 * m + 256
        dv[16 * m : 16 * m + 16, :] = jnp.concatenate(
            [vec[:, a : a + 256], vec[:, b : b + 256]], axis=0
        )
        three = pts[:, a : a + 512].astype(f32)
        four = jnp.concatenate([three, jnp.zeros((1, 512), f32)], axis=0)
        dp[8 * m : 8 * m + 8, :] = jnp.concatenate([four[:, :256], four[:, 256:]], axis=0)
    data_v = dv[...]
    data_p = dp[...].astype(bf16)
    width = 512
    for n in range(COLS // width):
        cols = slice(n * width, (n + 1) * width)
        index = perm[:, cols]
        low = index & 255
        high = jnp.broadcast_to(lax.shift_right_logical(index, 8), (8, width))
        select = hot(iota((256, width), 0) == low)
        got = dot(data_v, select)
        out = got[:8]
        for q in range(1, 32):
            out = jnp.where(high == q, got[8 * q : 8 * q + 8], out)
        vt[:, cols] = out.astype(bf16)
        got = dot(data_p, select)
        pair = high - iota((8, width), 0) // 4
        out = jnp.zeros((8, width), f32)
        for m in range(16):
            out = jnp.where(pair == 2 * m, got[8 * m : 8 * m + 8], out)
        out = out[:4] + out[4:]
        pt[:, cols] = jnp.concatenate([out, jnp.zeros((4, width), f32)], axis=0).astype(bf16)
    first, last = slice(0, HALO), slice(COLS - HALO, COLS)

    @pl.when(core == 0)
    def _():
        send_a[0:8, :] = vt[:, first]
        send_a[8:16, :] = pt[:, first]
        send_b[...] = vt[:, last]
        send_c[...] = vt[:, COLS - LOCAL :]

    @pl.when(core == 1)
    def _():
        send_a[0:8, :] = vt[:, last]
        send_a[8:16, :] = pt[:, last]
        send_b[...] = vt[:, first]
        send_c[...] = vt[:, :LOCAL]


def coeff_kernel(vt, bases, tr, cp, bsrc, bown, btgt, send, cf, pick, prod):
    cf[248:256, :] = jnp.zeros((8, 128), f32)
    for leaf in range(16):
        cf[8 * leaf : 8 * leaf + 8, :64] = dot(
            vt[:, LEAF * leaf : LEAF * leaf + LEAF], bases[leaf], NT
        )
    off, n = 0, 16
    while n > 1:
        for m in range(n // 2):
            r = 8 * (off + 2 * m)
            pair = jnp.concatenate([cf[r : r + 8, :64], cf[r + 8 : r + 16, :64]], axis=1)
            w = tr[off + 2 * m : off + 2 * m + 2].reshape(128, 64)
            t = 8 * (off + n + m)
            cf[t : t + 8, :64] = dot_pair(pair, w)
        off += n
        n //= 2
    source = hot(iota((32, 256), 0) == bsrc[...])
    for v in range(8):
        mine = cf[pl.ds(v, 32, stride=8), :][:, :64].astype(bf16)
        chosen = dot(mine, source, TN)
        pick[pl.ds(v, 64, stride=8), :] = chosen[:, :128]
        pick[pl.ds(512 + v, 64, stride=8), :] = chosen[:, 128:]
    for half in range(2):
        lanes = slice(128 * half, 128 * half + 128)
        for pb in range(4):
            rows = slice(16 * pb, 16 * pb + 16)

            def step(k, acc):
                block = cp[k, rows, lanes].astype(f32)
                picked = pick[pl.ds(pl.multiple_of(512 * half + 8 * k, 8), 8), :]
                return tuple(acc[v] + picked[v : v + 1] * block for v in range(8))

            acc = lax.fori_loop(0, 64, step, (jnp.zeros((16, 128), f32),) * 8, unroll=8)
            for v in range(8):
                top = 64 * (v % 4) + 16 * pb
                left = 256 * (v // 4) + 128 * half
                prod[top : top + 16, left : left + 128] = acc[v].astype(bf16)
    prod[256:384, 0:256] = jnp.zeros((128, 256), bf16)
    prod[256:384, 256:512] = jnp.broadcast_to((btgt[...] + 1).astype(f32), (128, 256)).astype(bf16)
    owner = bown[...]
    owner_f = owner.astype(f32)
    column = jnp.transpose(jnp.broadcast_to(owner_f, (128, 256)))
    ranks = []
    for half in range(2):
        row = owner_f[:, 128 * half : 128 * half + 128]
        before = iota((256, 128), 0) < iota((256, 128), 1) + 128 * half
        same = jnp.where((column == row) & before, 1.0, 0.0)
        ranks.append(jnp.sum(same, axis=0, keepdims=True))
    place = owner * 8 + jnp.concatenate(ranks, axis=1).astype(i32)
    place = jnp.concatenate([place, place + 4], axis=1)
    even = cf[pl.ds(240, 4, stride=2), :][:, :64]
    odd = cf[pl.ds(241, 4, stride=2), :][:, :64]
    root = jnp.concatenate([even, odd], axis=1)
    root = jnp.concatenate([root, jnp.zeros((4, 128), f32)], axis=0)
    payload = prod[...]
    for part in range(4):
        rows = slice(256 * part, 256 * part + 256)
        slots = hot(iota((256, 512), 0) + 256 * part == place)
        out = dot(slots, payload, NT)
        send[rows, 0:256] = out[:, :256].astype(bf16)
        extra = out[:, 256:].reshape(32, 8, 128) + root[None]
        send[rows, 256:384] = extra.reshape(256, 128).astype(bf16)


def split3(x):
    a = x.astype(bf16).astype(f32)
    b = (x - a).astype(bf16).astype(f32)
    return a, b, x - a - b


def near_kernel(vt, pt, rec_a, rec_b, rec_c, mine, other, vw, pw, fs, ft, acc):
    core = lax.axis_index("vec")

    @pl.when(core == 0)
    def _():
        vw[0:8, HALO:] = vt[:, :LOCAL]
        vw[8:16, HALO:] = rec_c[...]
        vw[0:8, :HALO] = rec_b[...]
        vw[8:16, :HALO] = rec_a[0:8, :]
        pw[:, HALO:] = pt[:, :LOCAL].astype(f32)
        pw[:, :HALO] = rec_a[8:16, :].astype(f32)

    @pl.when(core == 1)
    def _():
        vw[0:8, :LOCAL] = vt[:, COLS - LOCAL :]
        vw[8:16, :LOCAL] = rec_c[...]
        vw[0:8, LOCAL:] = rec_b[...]
        vw[8:16, LOCAL:] = rec_a[0:8, :]
        pw[:, :LOCAL] = pt[:, COLS - LOCAL :].astype(f32)
        pw[:, LOCAL:] = rec_a[8:16, :].astype(f32)

    for leaf in range(12):
        cols = slice(LEAF * leaf, LEAF * leaf + LEAF)
        p = pw[0:3, cols]
        norm = p[0:1] * p[0:1] + p[1:2] * p[1:2] + p[2:3] * p[2:3]
        parts = jnp.concatenate(split3(norm), axis=0)
        one = jnp.ones((3, LEAF), f32)
        two = jnp.ones((2, LEAF), f32)
        pad = jnp.zeros((5, LEAF), f32)
        source = jnp.concatenate([p, parts, one, two, pad], axis=0)
        smooth = jnp.where(iota((2, LEAF), 0) == 0, SMOOTH_HI, SMOOTH_LO)
        target = jnp.concatenate([-2.0 * p, one, parts, smooth, pad], axis=0)
        fs[cols, :] = jnp.transpose(source).astype(bf16)
        ft[:, cols] = target.astype(bf16)
    acc[...] = jnp.zeros_like(acc)
    for t in range(2, 10):
        tc = slice(LEAF * t, LEAF * t + LEAF)
        to = slice(LEAF * (t - 2), LEAF * (t - 1))
        total = jnp.zeros((16, LEAF), f32)
        for s in range(t - 2, t + 3):
            if 2 <= s < t:
                continue
            sc = slice(LEAF * s, LEAF * s + LEAF)
            kernel = lax.rsqrt(dot(fs[sc, :], ft[:, tc])).astype(bf16)
            total = total + dot(vw[:, sc], kernel)
            if t < s < 10:
                so = slice(LEAF * (s - 2), LEAF * (s - 1))
                acc[:, so] += dot(vw[:, tc], kernel, NT)
        acc[:, to] += total
    mine[...] = acc[0:8, :] * (8.0 / LEAF)
    other[...] = acc[8:16, :] * (8.0 / LEAF)


LEVEL_START = [256 - (256 >> u) for u in range(7)]


def matrices_kernel(ut, uc, et, eu):
    device = lax.axis_index("leaf")
    row, lane = iota((80, 254), 0), iota((80, 254), 1)
    own = jnp.zeros((80, 254), i32) - 1
    for u in range(7):
        own = jnp.where(row == 64 + u, LEVEL_START[u] + lax.shift_right_logical(device, u), own)
    pick_t = hot(((row < 62) & (lane == row + 192)) | (lane == own))
    pick_c = pick_t[64:80]

    def step(k, carry):
        et[pl.ds(pl.multiple_of(80 * k, 8), 80), :64] = dot(pick_t, ut[k], NT)
        eu[pl.ds(pl.multiple_of(16 * k, 8), 16), :64] = dot(pick_c, uc[k], NT)
        return carry

    lax.fori_loop(0, 64, step, 0, unroll=8)


def final_kernel(
    recv, near_mine, near_other, ut, et, eu, tr, bases, perm, out,
    ext, xt, y0, y1, xs, gain, cpl, dn, tree,
):
    device = lax.axis_index("leaf")
    core = lax.axis_index("vec")
    ext[...] = recv[:, 256:384].astype(f32)

    for s in range(4):
        turned = jnp.transpose(ext[pl.ds(s, 128, stride=8), :])
        xt[pl.ds(2 * s, 64, stride=8), :] = turned[:64]
        xt[pl.ds(2 * s + 1, 64, stride=8), :] = turned[64:]

    def climb_lanes(left, width, dest):
        for pb in range(4):
            rows = slice(16 * pb, 16 * pb + 16)

            def step(k, acc):
                block = ut[k, rows, left : left + width].astype(f32)
                values = xt[pl.ds(pl.multiple_of(8 * k, 8), 8), 0:width]
                return tuple(acc[v] + values[v : v + 1] * block for v in range(8))

            acc = lax.fori_loop(0, 64, step, (jnp.zeros((16, width), f32),) * 8, unroll=8)
            for v in range(8):
                dest[64 * v + 16 * pb : 64 * v + 16 * pb + 16, :] = acc[v]

    def to_rows(values, count, base):
        for v in range(8):
            xs[pl.ds(base * 8 + v, count, stride=8), :] = wide(values[:count, 64 * v : 64 * v + 64])

    sibling0 = lax.bitwise_xor(device, 1)
    lines = ext[pl.ds(pl.multiple_of(sibling0 * 8, 8), 8), :]
    for s in range(4):
        line = lines[s : s + 1]
        xs[2 * s : 2 * s + 1, :64] = line[:, :64]
        xs[2 * s + 1 : 2 * s + 2, :64] = line[:, 64:]
    climb_lanes(0, 128, y0)
    hi = y0[...].astype(bf16)
    lo = (y0[...] - hi.astype(f32)).astype(bf16)
    join = hot(iota((128, 128), 0) // 2 == iota((128, 128), 1))
    joined = dot(hi, join) + dot(lo, join)
    for v in range(8):
        xt[pl.ds(v, 64, stride=8), :] = joined[64 * v : 64 * v + 64]
    sibling1 = lax.bitwise_xor(lax.shift_right_logical(device, 1), 1)
    pick = hot((iota((8, 128), 1) // 2 == sibling1) & (iota((8, 128), 0) == 0))
    to_rows(dot(pick, hi, NT) + dot(pick, lo, NT), 1, 1)
    climb_lanes(128, 64, y1)
    hi = y1[...].astype(bf16)
    lo = (y1[...] - hi.astype(f32)).astype(bf16)
    join = hot(iota((32, 64), 1) // 2 == iota((32, 64), 0))
    to_rows(dot(join, hi, NT) + dot(join, lo, NT), 32, 2)
    first, n = 2, 32
    firsts = {2: 2}
    for u in range(2, 6):
        for m in range(n // 2):
            r = 8 * (first + 2 * m)
            e = LEVEL_START[u] - 192 + 2 * m
            pair = jnp.concatenate([xs[r : r + 8, :64], xs[r + 8 : r + 16, :64]], axis=1)
            w = jnp.concatenate(
                [et[pl.ds(e, 64, stride=80), :], et[pl.ds(e + 1, 64, stride=80), :]], axis=0
            )[:, :64].astype(bf16)
            t = 8 * (first + n + m)
            xs[t : t + 8, :64] = dot_pair(pair, w)
        first += n
        n //= 2
        firsts[u + 1] = first

    for u in range(7):
        if u < 2:
            partner = xs[8 * u : 8 * u + 8, :64]
        else:
            sib = lax.bitwise_xor(lax.shift_right_logical(device, u), 1)
            partner = xs[pl.ds(pl.multiple_of((firsts[u] + sib) * 8, 8), 8), :64]
        gain[8 * u : 8 * u + 8, :] = dot_pair(
            partner, eu[pl.ds(u, 64, stride=16), :][:, :64].astype(bf16)
        )
    down = gain[48:56, :]
    for u in range(5, -1, -1):
        w = et[pl.ds(64 + u, 64, stride=80), :][:, :64].astype(bf16)
        down = dot_pair(down, w, NT) + gain[8 * u : 8 * u + 8, :]

    late = (iota((128, 8, 128), 1) >= 4)
    lab = ext[...].reshape(128, 8, 128)
    early_lab = jnp.where(late, 0.0, pltpu.roll(lab, 4, 1)).reshape(1024, 128)
    late_lab = jnp.where(late, lab, 0.0).reshape(1024, 128)
    name = (iota((1024, 128), 1) + 1).astype(f32)
    for h, label in enumerate((early_lab, late_lab)):
        sums = dot(hot(label == name), recv[:, 0:256], TN)
        for v in range(4):
            cpl[pl.ds(4 * h + v, 32, stride=8), :] = wide(sums[:32, 64 * v : 64 * v + 64])

    dn[240:248, :] = down + cpl[240:248, :64]
    n = 1
    while n < 16:
        off_parent = 32 - 2 * n
        n *= 2
        off = 32 - 2 * n
        for m in range(n // 2):
            r = 8 * (off_parent + m)
            w = tr[off + 2 * m : off + 2 * m + 2].reshape(128, 64)
            both = dot_pair(dn[r : r + 8, :], w, NT)
            t = 8 * (off + 2 * m)
            dn[t : t + 8, :] = both[:, :64] + cpl[t : t + 8, :64]
            dn[t + 8 : t + 16, :] = both[:, 64:] + cpl[t + 8 : t + 16, :64]
    for leaf in range(16):
        tree[:, LEAF * leaf : LEAF * leaf + LEAF] = dot(
            dn[8 * leaf : 8 * leaf + 8, :].astype(bf16), bases[leaf]
        )

    @pl.when(core == 0)
    def _():
        tree[:, :HALF] += near_mine[...]
        tree[:, HALF:] += near_other[...]

    @pl.when(core == 1)
    def _():
        tree[:, :HALF] += near_other[...]
        tree[:, HALF:] += near_mine[...]

    width = 512
    total = jnp.zeros((256, 256), f32)
    for b in range(COLS // width):
        cols = slice(b * width, (b + 1) * width)
        index = perm[:, cols]
        select = hot(iota((256, width), 0) == (index & 255))
        high = jnp.broadcast_to(lax.shift_right_logical(index, 8), (8, width))
        values = tree[:, cols]
        spread = jnp.concatenate(
            [jnp.where(high == q, values, 0.0) for q in range(32)], axis=0
        ).astype(bf16)
        total = total + dot(spread, select, NT)
    for q in range(32):
        out[:, 256 * q : 256 * q + 256] = total[8 * q : 8 * q + 8].astype(bf16)


def shards(
    points, vectors, leaf_order, leaf_bases, transfers, coupling_blocks,
    block_source, block_owner, block_target, up_transfer, up_coupling,
):
    peers = lax.axis_size("leaf")
    axes = ("leaf", "vec")
    vt, pt, send_a, send_b, send_c = call(
        gather_kernel,
        [((8, COLS), bf16), ((8, COLS), bf16), ((16, HALO), bf16), ((8, HALO), bf16), ((8, LOCAL), bf16)],
        [pltpu.VMEM((256, 256), bf16), pltpu.VMEM((128, 256), f32)],
        (points, vectors, leaf_order),
        2 * 384 * 256 * COLS, 1 << 20,
    )
    pairs_a, pairs_b, pairs_c = [], [], []
    for d in range(peers):
        pairs_c += [(2 * d, 2 * d + 1), (2 * d + 1, 2 * d)]
        if d + 1 < peers:
            pairs_a += [(2 * d + 1, 2 * d + 2), (2 * d + 2, 2 * d + 1)]
            pairs_b += [(2 * d, 2 * d + 2), (2 * d + 3, 2 * d + 1)]
    rec_c = lax.ppermute(send_c, axes, pairs_c)
    rec_a = lax.ppermute(send_a, axes, pairs_a)
    rec_b = lax.ppermute(send_b, axes, pairs_b)
    (send,) = call(
        coeff_kernel,
        [((1024, 384), bf16)],
        [pltpu.VMEM((256, 128), f32), pltpu.VMEM((1024, 128), f32), pltpu.VMEM((384, 512), bf16)],
        (
            vt, leaf_bases, transfers, jnp.transpose(coupling_blocks, (1, 2, 0)),
            block_source.reshape(1, -1), block_owner.reshape(1, -1), block_target.reshape(1, -1),
        ),
        2 * 1024 * 512 * 384, 4 << 20,
    )
    recv = lax.all_to_all(send, "leaf", split_axis=0, concat_axis=0, tiled=True)
    near_mine, near_send = call(
        near_kernel,
        [((8, HALF), f32), ((8, HALF), f32)],
        [
            pltpu.VMEM((16, 6144), bf16), pltpu.VMEM((8, 6144), f32), pltpu.VMEM((6144, 16), bf16),
            pltpu.VMEM((16, 6144), bf16), pltpu.VMEM((16, HALF), f32),
        ],
        (vt, pt, rec_a, rec_b, rec_c),
        2 * 67 * 512 * 512 * 256, 1 << 20,
    )
    near_other = lax.ppermute(near_send, axes, pairs_c)
    ut = jnp.transpose(up_transfer, (1, 2, 0))
    uc = jnp.transpose(up_coupling, (1, 2, 0))
    et, eu = call(
        matrices_kernel,
        [((64 * 80, 128), f32), ((64 * 16, 128), f32)],
        [],
        (ut, uc),
        2 * 8192 * 256 * 96, 8 << 20,
    )
    (out,) = call(
        final_kernel,
        [((8, COLS), bf16)],
        [
            pltpu.VMEM((1024, 128), f32), pltpu.VMEM((512, 128), f32), pltpu.VMEM((512, 128), f32),
            pltpu.VMEM((512, 64), f32), pltpu.VMEM((576, 128), f32), pltpu.VMEM((56, 64), f32),
            pltpu.VMEM((256, 128), f32), pltpu.VMEM((248, 64), f32), pltpu.VMEM((8, COLS), f32),
        ],
        (recv, near_mine, near_other, ut, et, eu, transfers, leaf_bases, leaf_order),
        2 * 256 * 256 * COLS, 8 << 20,
    )
    return out


def solution(mesh):
    return jax.shard_map(
        shards,
        mesh=mesh,
        in_specs=(
            P(None, "leaf"),
            P("vec", "leaf"),
            P("leaf", None),
            P("leaf", None, None),
            P("leaf", None, None),
            P("leaf", None, None),
            P("leaf"),
            P("leaf", None),
            P("leaf"),
            P(),
            P(),
        ),
        out_specs=P("vec", "leaf"),
        check_vma=False,
    )
```

time: 402 us -> 76 us (0.19)
  the two profiles are of different devices: /device:TPU:8 before, /device:TPU:7 now
where the time goes in v1:
time: 76 us; the launch traced here: 75.6 us
  Pallas kernels  32.3 us (42%)
  starting transfers between devices  29.3 us (39%)
  waiting for transfers between devices  8.12 us (11%)
  local copies, waits for them, and re-layouts  5.74 us (8%)
    pallas_call x5, Pallas kernels, call(): pl.pallas_call(kernel, out_shape=[jax.ShapeDtypeStruct(s, d) for s, d in...  32.3 us
    all_to_all x1, starting transfers between devices, shards(): recv = lax.all_to_all(send, 'leaf', split_axis=0, concat_axis=0, tiled=True)  15.8 us
    ppermute x1, starting transfers between devices, shards(): rec_b = lax.ppermute(send_b, axes, pairs_b)  6.4 us
    ppermute x1, waiting for transfers between devices, shards(): rec_b = lax.ppermute(send_b, axes, pairs_b)  5.88 us
    unnamed x30, local copies, waits for them, and re-layouts  5.74 us
    ppermute x1, starting transfers between devices, shards(): rec_a = lax.ppermute(send_a, axes, pairs_a)  3 us
    ppermute x1, starting transfers between devices, shards(): near_other = lax.ppermute(near_send, axes, pairs_c)  2.84 us
    ppermute x1, waiting for transfers between devices, shards(): rec_a = lax.ppermute(send_a, axes, pairs_a)  2.24 us
  transfers between devices with their start and end apart: 5, of which 2 were waited for; matrix products, arithmetic and copies ran while one was open for 0% of the time, Pallas kernels for 17%

profile of v1, /device:TPU:7, one launch (start us, length us, event | category | flops | bytes accessed | tf_op | source)
XLA Modules:
  0.0 75.6 jit_solution(4267095248723226644)
XLA Ops:
  0.0 0.0 copy-start.8
  0.0 0.9 %copy-done.8 = s32[1,8192]{1,0:T(1,128)S(1)} copy-done((s32[1,8192]{1,0:T(1,128)S(1)}, s32[1,8192]{1,0:T(1,128)}, u32[]{:S(2)}) %copy-start.8) | copy-done | bytes 32792
  0.9 1.1 %copy-done.13 = bf16[8,8192]{1,0:T(8,128)(2,1)S(1)} copy-done((bf16[8,8192]{1,0:T(8,128)(2,1)S(1)}, bf16[8,8192]{1,0:T(8,128)(2,1)}, u32[]{:S(2)}) %copy-start.13) | copy-done | bytes 131096
  2.0 0.8 %copy-done.14 = bf16[3,8192]{1,0:T(4,128)(2,1)S(1)} copy-done((bf16[3,8192]{1,0:T(4,128)(2,1)S(1)}, bf16[3,8192]{1,0:T(4,128)(2,1)}, u32[]{:S(2)}) %copy-start.14) | copy-done | bytes 49176
  2.9 3.0 %shard_map.109 = (bf16[8,8192]{1,0:T(8,128)(2,1)S(1)}, bf16[8,8192]{1,0:T(8,128)(2,1)S(1)}, bf16[16,1024]{1,0:T(8,128)(2,1)S(1)}, bf16[8,1024]{1,0:T(8,128)(2,1)S(1)}, bf16[8,5120]{1,0:T(8,128)(2,1)S(1)}) custom-call(bf16[3,8192]{1,0:T(4,128)(2,1)S(1)} %copy-done.14, bf16[8,8192]{1,0:T(8,128)(2,1)S(1)} %copy-done.13, s32[1,8192]{1,0:T(1,128)S(1)} %copy-done.8), custom_call_target="tpu_custom_call" | custom-call | flops 1610612736 | bytes 1048576 | tf_op jit(solution)/shard_map/pallas_call | solution.py:54
  5.9 5.8 %shard_map.110 = bf16[1024,384]{1,0:T(8,128)(2,1)} custom-call(bf16[8,8192]{1,0:T(8,128)(2,1)S(1)} %get-tuple-element.14.vt, bf16[16,64,512]{2,1,0:T(8,128)(2,1)S(1)} %copy-done.1, bf16[30,64,64]{2,1,0:T(8,128)(2,1)S(1)} %copy-done.4, bf16[64,64,256]{2,1,0:T(8,128)(2,1)S(1)} %bitcast.10, s32[1,256]{1,0:T(1,128)S(1)} %bitcast.12, s32[1,256]{1,0:T(1,128)S(1)} %bitcast.13, ...), custom_call_target="tpu_custom_call" | custom-call | flops 402653184 | bytes 4194304 | tf_op jit(solution)/shard_map/pallas_call | solution.py:54
  11.7 15.8 %all-to-all-start = ((bf16[128,8,384]{2,1,0:T(8,128)(2,1)}), bf16[128,8,384]{2,1,0:T(8,128)(2,1)}, u32[]{:S(2)}, u32[]{:S(2)}) async-start(bf16[128,8,384]{2,1,0:T(8,128)(2,1)} %bitcast.4), calls=%async_computation | async-start | bytes 1572864 | tf_op jit(solution)/shard_map/all_to_all | solution.py:423
  27.5 1.3 %collective-permute-start.2 = (bf16[8,5120]{1,0:T(8,128)(2,1)S(1)}, bf16[8,5120]{1,0:T(8,128)(2,1)S(1)}, u32[]{:S(2)}, u32[]{:S(2)}) collective-permute-start(bf16[8,5120]{1,0:T(8,128)(2,1)S(1)} %get-tuple-element.18), channel_id=1, source_target_pairs={{0,1},{1,0},{2,3},{3,2},{4,5},{5,4},{6,7},{7,6},{8,9},{9,8},{10,11... | collective-permute-start | bytes 245768 | tf_op jit(solution)/shard_map/ppermute | solution.py:410
  28.8 3.0 %collective-permute-start = (bf16[16,1024]{1,0:T(8,128)(2,1)S(1)}, bf16[16,1024]{1,0:T(8,128)(2,1)S(1)}, u32[]{:S(2)}, u32[]{:S(2)}) collective-permute-start(bf16[16,1024]{1,0:T(8,128)(2,1)S(1)} %get-tuple-element.16), channel_id=1, source_target_pairs={{1,2},{2,1},{3,4},{4,3},{5,6},{6,5},{7,8},{8,7},{9,10},{10,9},{11,... | collective-permute-start | bytes 98312 | tf_op jit(solution)/shard_map/ppermute | solution.py:411
  31.8 6.4 %collective-permute-start.1 = (bf16[8,1024]{1,0:T(8,128)(2,1)S(1)}, bf16[8,1024]{1,0:T(8,128)(2,1)S(1)}, u32[]{:S(2)}, u32[]{:S(2)}) collective-permute-start(bf16[8,1024]{1,0:T(8,128)(2,1)S(1)} %get-tuple-element.17), channel_id=1, source_target_pairs={{0,2},{3,1},{2,4},{5,3},{4,6},{7,5},{6,8},{9,7},{8,10},{11,9},{10,... | collective-permute-start | bytes 49160 | tf_op jit(solution)/shard_map/ppermute | solution.py:412
  38.2 5.9 %collective-permute-done.1.rec_b = bf16[8,1024]{1,0:T(8,128)(2,1)S(1)} collective-permute-done((bf16[8,1024]{1,0:T(8,128)(2,1)S(1)}, bf16[8,1024]{1,0:T(8,128)(2,1)S(1)}, u32[]{:S(2)}, u32[]{:S(2)}) %collective-permute-start.1) | collective-permute-done | bytes 16416 | tf_op jit(solution)/shard_map/ppermute | solution.py:412
  44.1 2.2 %collective-permute-done.rec_a = bf16[16,1024]{1,0:T(8,128)(2,1)S(1)} collective-permute-done((bf16[16,1024]{1,0:T(8,128)(2,1)S(1)}, bf16[16,1024]{1,0:T(8,128)(2,1)S(1)}, u32[]{:S(2)}, u32[]{:S(2)}) %collective-permute-start) | collective-permute-done | bytes 32800 | tf_op jit(solution)/shard_map/ppermute | solution.py:411
  46.3 0.0 collective-permute-done.2.rec_c
  46.4 9.2 %shard_map.111 = (f32[8,4096]{1,0:T(8,128)S(1)}, f32[8,4096]{1,0:T(8,128)S(1)}) custom-call(bf16[8,8192]{1,0:T(8,128)(2,1)S(1)} %get-tuple-element.14.vt, bf16[8,8192]{1,0:T(8,128)(2,1)S(1)} %get-tuple-element.15.pt, bf16[16,1024]{1,0:T(8,128)(2,1)S(1)} %collective-permute-done.rec_a, bf16[8,1024]{1,0:T(8,128)(2,1)S(1)} %collective-permute-done.1.rec_b, ...), custom_call_target="tpu_custom_call" | custom-call | flops 8992587776 | bytes 1048576 | tf_op jit(solution)/shard_map/pallas_call | solution.py:54
  55.6 2.8 %collective-permute-start.3 = (f32[8,4096]{1,0:T(8,128)S(1)}, f32[8,4096]{1,0:T(8,128)S(1)}, u32[]{:S(2)}, u32[]{:S(2)}) collective-permute-start(f32[8,4096]{1,0:T(8,128)S(1)} %get-tuple-element.20), channel_id=1, source_target_pairs={{0,1},{1,0},{2,3},{3,2},{4,5},{5,4},{6,7},{7,6},{8,9},{9,8},{10,11... | collective-permute-start | bytes 393224 | tf_op jit(solution)/shard_map/ppermute | solution.py:434
  58.4 3.8 %shard_map.112 = (f32[5120,128]{1,0:T(8,128)}, f32[1024,128]{1,0:T(8,128)S(1)}) custom-call(bf16[64,64,254]{2,1,0:T(8,128)(2,1)S(1)} %bitcast.8, bf16[64,64,254]{2,1,0:T(8,128)(2,1)S(1)} %bitcast.11), custom_call_target="tpu_custom_call" | custom-call | flops 402653184 | bytes 8388608 | tf_op jit(solution)/shard_map/pallas_call | solution.py:54
  62.2 0.8 %copy-done.6 = f32[1024,128]{1,0:T(8,128)} copy-done((f32[1024,128]{1,0:T(8,128)}, f32[1024,128]{1,0:T(8,128)S(1)}, u32[]{:S(2)}) %copy-start.6) | copy-done | bytes 524312
  63.0 0.0 collective-permute-done.3.near_other
  63.0 0.0 all-to-all-done
  63.0 0.0 copy-done.9
  63.0 0.0 copy-start.5
  63.1 1.0 %copy-done.5 = bf16[30,64,64]{2,1,0:T(8,128)(2,1)S(1)} copy-done((bf16[30,64,64]{2,1,0:T(8,128)(2,1)S(1)}, bf16[30,64,64]{2,1,0:T(8,128)(2,1)}, u32[]{:S(2)}) %copy-start.5) | copy-done | bytes 245784
  64.1 1.0 %copy-done.7 = f32[1024,128]{1,0:T(8,128)S(1)} copy-done((f32[1024,128]{1,0:T(8,128)S(1)}, f32[1024,128]{1,0:T(8,128)}, u32[]{:S(2)}) %copy-start.7) | copy-done | bytes 524312
  65.1 10.5 %shard_map.113 = bf16[8,8192]{1,0:T(8,128)(2,1)} custom-call(bf16[1024,384]{1,0:T(8,128)(2,1)} %bitcast.5.recv, f32[8,4096]{1,0:T(8,128)S(1)} %get-tuple-element.19.near_mine, f32[8,4096]{1,0:T(8,128)S(1)} %collective-permute-done.3.near_other, bf16[64,64,254]{2,1,0:T(8,128)(2,1)S(1)} %bitcast.9, f32[5120,128]{1,0:T(8,128)} %get-tuple-element.21.et, ...), custom_call_target="tpu_custom_call" | custom-call | flops 1073741824 | bytes 8388608 | tf_op jit(solution)/shard_map/pallas_call | solution.py:54
  (21 shorter events, 0.0 us)
Async XLA Ops:
  0.0 5.8 %copy-start.4 = (bf16[30,64,64]{2,1,0:T(8,128)(2,1)S(1)}, bf16[30,64,64]{2,1,0:T(8,128)(2,1)}, u32[]{:S(2)}) copy-start(bf16[30,64,64]{2,1,0:T(8,128)(2,1)} %tr.3) | copy-start | bytes 737284
  0.0 5.8 %copy-start.1 = (bf16[16,64,512]{2,1,0:T(8,128)(2,1)S(1)}, bf16[16,64,512]{2,1,0:T(8,128)(2,1)}, u32[]{:S(2)}) copy-start(bf16[16,64,512]{2,1,0:T(8,128)(2,1)} %bases.3) | copy-start | bytes 3145732
  0.0 5.8 %copy-start.2 = (bf16[256,64,64]{0,2,1:T(8,128)(2,1)S(1)}, bf16[256,64,64]{0,2,1:T(8,128)(2,1)}, u32[]{:S(2)}) copy-start(bf16[256,64,64]{0,2,1:T(8,128)(2,1)} %param.16) | copy-start | bytes 6291460
  0.0 0.9 %copy-start.8 = (s32[1,8192]{1,0:T(1,128)S(1)}, s32[1,8192]{1,0:T(1,128)}, u32[]{:S(2)}) copy-start(s32[1,8192]{1,0:T(1,128)} %perm.3) | copy-start | bytes 98308
  0.9 1.1 %copy-start.13 = (bf16[8,8192]{1,0:T(8,128)(2,1)S(1)}, bf16[8,8192]{1,0:T(8,128)(2,1)}, u32[]{:S(2)}) copy-start(bf16[8,8192]{1,0:T(8,128)(2,1)} %vec.1) | copy-start | bytes 393220
  2.0 0.8 %copy-start.14 = (bf16[3,8192]{1,0:T(4,128)(2,1)S(1)}, bf16[3,8192]{1,0:T(4,128)(2,1)}, u32[]{:S(2)}) copy-start(bf16[3,8192]{1,0:T(4,128)(2,1)} %pts.1) | copy-start | bytes 147460
  2.9 3.0 %copy-start.10 = (s32[256]{0:T(256)S(1)}, s32[256]{0:T(256)}, u32[]{:S(2)}) copy-start(s32[256]{0:T(256)} %param.17) | copy-start | bytes 3076
  2.9 3.0 %copy-start.11 = (s32[256,1]{0,1:T(1,128)S(1)}, s32[256,1]{0,1:T(1,128)}, u32[]{:S(2)}) copy-start(s32[256,1]{0,1:T(1,128)} %param.18) | copy-start | bytes 3076
  2.9 3.0 %copy-start.12 = (s32[256]{0:T(256)S(1)}, s32[256]{0:T(256)}, u32[]{:S(2)}) copy-start(s32[256]{0:T(256)} %param.19) | copy-start | bytes 3076
  11.7 51.3 %all-to-all-start = ((bf16[128,8,384]{2,1,0:T(8,128)(2,1)}), bf16[128,8,384]{2,1,0:T(8,128)(2,1)}, u32[]{:S(2)}, u32[]{:S(2)}) async-start(bf16[128,8,384]{2,1,0:T(8,128)(2,1)} %bitcast.4), calls=%async_computation | async-start | bytes 1572864 | tf_op jit(solution)/shard_map/all_to_all | solution.py:423
  27.5 18.9 %collective-permute-start.2 = (bf16[8,5120]{1,0:T(8,128)(2,1)S(1)}, bf16[8,5120]{1,0:T(8,128)(2,1)S(1)}, u32[]{:S(2)}, u32[]{:S(2)}) collective-permute-start(bf16[8,5120]{1,0:T(8,128)(2,1)S(1)} %get-tuple-element.18), channel_id=1, source_target_pairs={{0,1},{1,0},{2,3},{3,2},{4,5},{5,4},{6,7},{7,6},{8,9},{9,8},{10,11... | collective-permute-start | bytes 245768 | tf_op jit(solution)/shard_map/ppermute | solution.py:410
  28.8 17.5 %collective-permute-start = (bf16[16,1024]{1,0:T(8,128)(2,1)S(1)}, bf16[16,1024]{1,0:T(8,128)(2,1)S(1)}, u32[]{:S(2)}, u32[]{:S(2)}) collective-permute-start(bf16[16,1024]{1,0:T(8,128)(2,1)S(1)} %get-tuple-element.16), channel_id=1, source_target_pairs={{1,2},{2,1},{3,4},{4,3},{5,6},{6,5},{7,8},{8,7},{9,10},{10,9},{11,... | collective-permute-start | bytes 98312 | tf_op jit(solution)/shard_map/ppermute | solution.py:411
  31.8 12.3 %collective-permute-start.1 = (bf16[8,1024]{1,0:T(8,128)(2,1)S(1)}, bf16[8,1024]{1,0:T(8,128)(2,1)S(1)}, u32[]{:S(2)}, u32[]{:S(2)}) collective-permute-start(bf16[8,1024]{1,0:T(8,128)(2,1)S(1)} %get-tuple-element.17), channel_id=1, source_target_pairs={{0,2},{3,1},{2,4},{5,3},{4,6},{7,5},{6,8},{9,7},{8,10},{11,9},{10,... | collective-permute-start | bytes 49160 | tf_op jit(solution)/shard_map/ppermute | solution.py:412
  46.3 12.0 %copy-start = (bf16[254,64,64]{0,2,1:T(8,128)(2,1)S(1)}, bf16[254,64,64]{0,2,1:T(8,128)(2,1)}, u32[]{:S(2)}) copy-start(bf16[254,64,64]{0,2,1:T(8,128)(2,1)} %param.20) | copy-start | bytes 6242308
  46.4 12.0 %copy-start.3 = (bf16[254,64,64]{0,2,1:T(8,128)(2,1)S(1)}, bf16[254,64,64]{0,2,1:T(8,128)(2,1)}, u32[]{:S(2)}) copy-start(bf16[254,64,64]{0,2,1:T(8,128)(2,1)} %param.21) | copy-start | bytes 6242308
  55.6 7.5 %collective-permute-start.3 = (f32[8,4096]{1,0:T(8,128)S(1)}, f32[8,4096]{1,0:T(8,128)S(1)}, u32[]{:S(2)}, u32[]{:S(2)}) collective-permute-start(f32[8,4096]{1,0:T(8,128)S(1)} %get-tuple-element.20), channel_id=1, source_target_pairs={{0,1},{1,0},{2,3},{3,2},{4,5},{5,4},{6,7},{7,6},{8,9},{9,8},{10,11... | collective-permute-start | bytes 393224 | tf_op jit(solution)/shard_map/ppermute | solution.py:434
  58.4 4.6 %copy-start.9 = (s32[1,8192]{1,0:T(1,128)S(1)}, s32[1,8192]{1,0:T(1,128)}, u32[]{:S(2)}) copy-start(s32[1,8192]{1,0:T(1,128)} %perm.3) | copy-start | bytes 98308
  62.2 0.8 %copy-start.6 = (f32[1024,128]{1,0:T(8,128)}, f32[1024,128]{1,0:T(8,128)S(1)}, u32[]{:S(2)}) copy-start(f32[1024,128]{1,0:T(8,128)S(1)} %get-tuple-element.22.eu) | copy-start | bytes 1572868
  63.0 1.0 %copy-start.5 = (bf16[30,64,64]{2,1,0:T(8,128)(2,1)S(1)}, bf16[30,64,64]{2,1,0:T(8,128)(2,1)}, u32[]{:S(2)}) copy-start(bf16[30,64,64]{2,1,0:T(8,128)(2,1)} %tr.3) | copy-start | bytes 737284
  64.1 1.0 %copy-start.7 = (f32[1024,128]{1,0:T(8,128)S(1)}, f32[1024,128]{1,0:T(8,128)}, u32[]{:S(2)}) copy-start(f32[1024,128]{1,0:T(8,128)} %copy-done.6) | copy-start | bytes 1572868

commit v2 on v1

--- a/solution.py
+++ b/solution.py
@@ -50,11 +50,11 @@
     return y[:n] + y[n:]
 
 
-def call(kernel, outs, scratch, args, flops, nbytes, vmem=48):
+def call(kernel, outs, scratch, args, flops, nbytes, vmem=16, anywhere=0):
     return pl.pallas_call(
         kernel,
         out_shape=[jax.ShapeDtypeStruct(s, d) for s, d in outs],
-        in_specs=[VM] * len(args),
+        in_specs=[VM] * (len(args) - anywhere) + [pl.BlockSpec(memory_space=pl.ANY)] * anywhere,
         out_specs=[VM] * len(outs),
         scratch_shapes=scratch,
         compiler_params=pltpu.CompilerParams(vmem_limit_bytes=vmem << 20),
@@ -110,7 +110,7 @@
         send_c[...] = vt[:, :LOCAL]
 
 
-def coeff_kernel(vt, bases, tr, cp, bsrc, bown, btgt, send, cf, pick, prod):
+def coeff_kernel(vt, bases, tr, et, cf, path):
     cf[248:256, :] = jnp.zeros((8, 128), f32)
     for leaf in range(16):
         cf[8 * leaf : 8 * leaf + 8, :64] = dot(
@@ -126,6 +126,18 @@
             cf[t : t + 8, :64] = dot_pair(pair, w)
         off += n
         n //= 2
+    value = cf[240:248, :64]
+    for u in range(3):
+        path[8 * u : 8 * u + 8, :] = value
+        value = dot_pair(value, own_matrix(et, OWN + u, T_ROWS))
+    path[24:32, :] = value
+
+
+def own_matrix(ref, row, rows):
+    return ref[pl.ds(row, 64, stride=rows), :][:, :64].astype(bf16)
+
+
+def product_kernel(cf, path, cp, bsrc, bown, btgt, seen_a, seen_b, seen_c, send, pick, prod):
     source = hot(iota((32, 256), 0) == bsrc[...])
     for v in range(8):
         mine = cf[pl.ds(v, 32, stride=8), :][:, :64].astype(bf16)
@@ -144,11 +156,10 @@
 
             acc = lax.fori_loop(0, 64, step, (jnp.zeros((16, 128), f32),) * 8, unroll=8)
             for v in range(8):
-                top = 64 * (v % 4) + 16 * pb
-                left = 256 * (v // 4) + 128 * half
-                prod[top : top + 16, left : left + 128] = acc[v].astype(bf16)
-    prod[256:384, 0:256] = jnp.zeros((128, 256), bf16)
-    prod[256:384, 256:512] = jnp.broadcast_to((btgt[...] + 1).astype(f32), (128, 256)).astype(bf16)
+                top = 64 * v + 16 * pb
+                prod[top : top + 16, lanes] = acc[v].astype(bf16)
+    prod[512:576, :] = jnp.zeros((64, 256), bf16)
+    prod[576:640, :] = jnp.broadcast_to((btgt[...] + 1).astype(f32), (64, 256)).astype(bf16)
     owner = bown[...]
     owner_f = owner.astype(f32)
     column = jnp.transpose(jnp.broadcast_to(owner_f, (128, 256)))
@@ -158,20 +169,19 @@
         before = iota((256, 128), 0) < iota((256, 128), 1) + 128 * half
         same = jnp.where((column == row) & before, 1.0, 0.0)
         ranks.append(jnp.sum(same, axis=0, keepdims=True))
-    place = owner * 8 + jnp.concatenate(ranks, axis=1).astype(i32)
-    place = jnp.concatenate([place, place + 4], axis=1)
-    even = cf[pl.ds(240, 4, stride=2), :][:, :64]
-    odd = cf[pl.ds(241, 4, stride=2), :][:, :64]
-    root = jnp.concatenate([even, odd], axis=1)
-    root = jnp.concatenate([root, jnp.zeros((4, 128), f32)], axis=0)
+    place = owner * 4 + jnp.concatenate(ranks, axis=1).astype(i32)
+    top = path[24:32, :]
+    high = top.astype(bf16).astype(f32)
+    extra = jnp.concatenate([high, top - high, jnp.zeros((16, 64), f32)], axis=0)
+    extra = wide(extra)
     payload = prod[...]
-    for part in range(4):
+    for part in range(2):
         rows = slice(256 * part, 256 * part + 256)
-        slots = hot(iota((256, 512), 0) + 256 * part == place)
+        slots = hot(iota((256, 256), 0) + 256 * part == place)
         out = dot(slots, payload, NT)
-        send[rows, 0:256] = out[:, :256].astype(bf16)
-        extra = out[:, 256:].reshape(32, 8, 128) + root[None]
-        send[rows, 256:384] = extra.reshape(256, 128).astype(bf16)
+        send[rows, 0:512] = out[:, :512].astype(bf16)
+        tail = out[:, 512:].reshape(8, 32, 128) + extra[None]
+        send[rows, 512:640] = tail.reshape(256, 128).astype(bf16)
 
 
 def split3(x):
@@ -180,7 +190,7 @@
     return a, b, x - a - b
 
 
-def near_kernel(vt, pt, rec_a, rec_b, rec_c, mine, other, vw, pw, fs, ft, acc):
+def near_setup_kernel(vt, pt, rec_a, rec_b, rec_c, vw, fs, ft, acc, pw):
     core = lax.axis_index("vec")
 
     @pl.when(core == 0)
@@ -215,7 +225,11 @@
         fs[cols, :] = jnp.transpose(source).astype(bf16)
         ft[:, cols] = target.astype(bf16)
     acc[...] = jnp.zeros_like(acc)
-    for t in range(2, 10):
+    near_blocks(range(2, 6), vw, fs, ft, acc)
+
+
+def near_blocks(targets, vw, fs, ft, acc):
+    for t in targets:
         tc = slice(LEAF * t, LEAF * t + LEAF)
         to = slice(LEAF * (t - 2), LEAF * (t - 1))
         total = jnp.zeros((16, LEAF), f32)
@@ -229,120 +243,138 @@
                 so = slice(LEAF * (s - 2), LEAF * (s - 1))
                 acc[:, so] += dot(vw[:, tc], kernel, NT)
         acc[:, to] += total
+
+
+def near_rest_kernel(vw, fs, ft, begun, mine, other, acc):
+    acc[...] = begun[...]
+    near_blocks(range(6, 10), vw, fs, ft, acc)
     mine[...] = acc[0:8, :] * (8.0 / LEAF)
     other[...] = acc[8:16, :] * (8.0 / LEAF)
 
 
 LEVEL_START = [256 - (256 >> u) for u in range(7)]
+UPPER = 224
+OWN = 30
+SIBLING = 33
+OWN_UPPER = 36
+T_ROWS = 40
+C_ROWS = 8
 
 
 def matrices_kernel(ut, uc, et, eu):
     device = lax.axis_index("leaf")
-    row, lane = iota((80, 254), 0), iota((80, 254), 1)
-    own = jnp.zeros((80, 254), i32) - 1
+
+    def node(u, other=False):
+        n = lax.shift_right_logical(device, u)
+        return LEVEL_START[u] + (lax.bitwise_xor(n, 1) if other else n)
+
+    row, lane = iota((T_ROWS, 254), 0), iota((T_ROWS, 254), 1)
+    want = jnp.where(row < 30, row + UPPER, -1)
+    for u in range(3):
+        want = jnp.where(row == OWN + u, node(u), want)
+        want = jnp.where(row == SIBLING + u, node(u, True), want)
+        want = jnp.where(row == OWN_UPPER + u, node(u + 3), want)
+    pick_t = hot(lane == want)
+    row, lane = iota((C_ROWS, 254), 0), iota((C_ROWS, 254), 1)
+    want = jnp.zeros((C_ROWS, 254), i32) - 1
     for u in range(7):
-        own = jnp.where(row == 64 + u, LEVEL_START[u] + lax.shift_right_logical(device, u), own)
-    pick_t = hot(((row < 62) & (lane == row + 192)) | (lane == own))
-    pick_c = pick_t[64:80]
-
-    def step(k, carry):
-        et[pl.ds(pl.multiple_of(80 * k, 8), 80), :64] = dot(pick_t, ut[k], NT)
-        eu[pl.ds(pl.multiple_of(16 * k, 8), 16), :64] = dot(pick_c, uc[k], NT)
+        want = jnp.where(row == u, node(u, u < 3), want)
+    pick_c = hot(lane == want)
+
+    def step(g, carry):
+        for ref, pick, dest, rows in ((ut, pick_t, et, T_ROWS), (uc, pick_c, eu, C_ROWS)):
+            block = ref[pl.ds(4 * g, 4)].reshape(256, 254)
+            out = dot(pick, block, NT)
+            for j in range(4):
+                at = pl.multiple_of((4 * g + j) * rows, 8)
+                dest[pl.ds(at, rows), :64] = out[:, 64 * j : 64 * j + 64]
         return carry
 
-    lax.fori_loop(0, 64, step, 0, unroll=8)
-
-
-def final_kernel(
-    recv, near_mine, near_other, ut, et, eu, tr, bases, perm, out,
-    ext, xt, y0, y1, xs, gain, cpl, dn, tree,
-):
+    lax.fori_loop(0, 16, step, 0, unroll=4)
+
+
+def middle_kernel(recv, path, et, eu, send, ext, xs, gain):
     device = lax.axis_index("leaf")
-    core = lax.axis_index("vec")
-    ext[...] = recv[:, 256:384].astype(f32)
-
-    for s in range(4):
-        turned = jnp.transpose(ext[pl.ds(s, 128, stride=8), :])
-        xt[pl.ds(2 * s, 64, stride=8), :] = turned[:64]
-        xt[pl.ds(2 * s + 1, 64, stride=8), :] = turned[64:]
-
-    def climb_lanes(left, width, dest):
-        for pb in range(4):
-            rows = slice(16 * pb, 16 * pb + 16)
-
-            def step(k, acc):
-                block = ut[k, rows, left : left + width].astype(f32)
-                values = xt[pl.ds(pl.multiple_of(8 * k, 8), 8), 0:width]
-                return tuple(acc[v] + values[v : v + 1] * block for v in range(8))
-
-            acc = lax.fori_loop(0, 64, step, (jnp.zeros((16, width), f32),) * 8, unroll=8)
-            for v in range(8):
-                dest[64 * v + 16 * pb : 64 * v + 16 * pb + 16, :] = acc[v]
-
-    def to_rows(values, count, base):
-        for v in range(8):
-            xs[pl.ds(base * 8 + v, count, stride=8), :] = wide(values[:count, 64 * v : 64 * v + 64])
-
-    sibling0 = lax.bitwise_xor(device, 1)
-    lines = ext[pl.ds(pl.multiple_of(sibling0 * 8, 8), 8), :]
-    for s in range(4):
-        line = lines[s : s + 1]
-        xs[2 * s : 2 * s + 1, :64] = line[:, :64]
-        xs[2 * s + 1 : 2 * s + 2, :64] = line[:, 64:]
-    climb_lanes(0, 128, y0)
-    hi = y0[...].astype(bf16)
-    lo = (y0[...] - hi.astype(f32)).astype(bf16)
-    join = hot(iota((128, 128), 0) // 2 == iota((128, 128), 1))
-    joined = dot(hi, join) + dot(lo, join)
-    for v in range(8):
-        xt[pl.ds(v, 64, stride=8), :] = joined[64 * v : 64 * v + 64]
-    sibling1 = lax.bitwise_xor(lax.shift_right_logical(device, 1), 1)
-    pick = hot((iota((8, 128), 1) // 2 == sibling1) & (iota((8, 128), 0) == 0))
-    to_rows(dot(pick, hi, NT) + dot(pick, lo, NT), 1, 1)
-    climb_lanes(128, 64, y1)
-    hi = y1[...].astype(bf16)
-    lo = (y1[...] - hi.astype(f32)).astype(bf16)
-    join = hot(iota((32, 64), 1) // 2 == iota((32, 64), 0))
-    to_rows(dot(join, hi, NT) + dot(join, lo, NT), 32, 2)
-    first, n = 2, 32
-    firsts = {2: 2}
-    for u in range(2, 6):
+    ext[...] = recv[:, 512:640].astype(f32)
+
+    labels = jnp.concatenate(
+        [jnp.transpose(ext[128 * i : 128 * i + 128, :])[64:65, :] for i in range(4)], axis=1
+    )
+    row, lane = iota((256, 512), 0), iota((256, 512), 1)
+    wanted = ((row & 31) + 1).astype(f32)
+    fits = lax.shift_right_logical(row, 5) == (lax.shift_right_logical(lane, 2) & 7)
+    sums = dot(hot((labels == wanted) & fits), recv[:, 0:512])
+
+    for g in range(16):
+        rows = ext[32 * g : 32 * g + 16, :64]
+        xs[8 * g : 8 * g + 8, :] = rows[:8] + rows[8:]
+    first, n = 0, 16
+    firsts = {3: 0}
+    for u in range(3, 6):
         for m in range(n // 2):
             r = 8 * (first + 2 * m)
-            e = LEVEL_START[u] - 192 + 2 * m
-            pair = jnp.concatenate([xs[r : r + 8, :64], xs[r + 8 : r + 16, :64]], axis=1)
-            w = jnp.concatenate(
-                [et[pl.ds(e, 64, stride=80), :], et[pl.ds(e + 1, 64, stride=80), :]], axis=0
-            )[:, :64].astype(bf16)
+            e = LEVEL_START[u] - UPPER + 2 * m
+            pair = jnp.concatenate([xs[r : r + 8, :], xs[r + 8 : r + 16, :]], axis=1)
+            w = jnp.concatenate([own_matrix(et, e, T_ROWS), own_matrix(et, e + 1, T_ROWS)], axis=0)
             t = 8 * (first + n + m)
-            xs[t : t + 8, :64] = dot_pair(pair, w)
+            xs[t : t + 8, :] = dot_pair(pair, w)
         first += n
         n //= 2
         firsts[u + 1] = first
-
     for u in range(7):
-        if u < 2:
-            partner = xs[8 * u : 8 * u + 8, :64]
+        if u < 3:
+            partner = path[8 * u : 8 * u + 8, :]
         else:
             sib = lax.bitwise_xor(lax.shift_right_logical(device, u), 1)
-            partner = xs[pl.ds(pl.multiple_of((firsts[u] + sib) * 8, 8), 8), :64]
-        gain[8 * u : 8 * u + 8, :] = dot_pair(
-            partner, eu[pl.ds(u, 64, stride=16), :][:, :64].astype(bf16)
+            partner = xs[pl.ds(pl.multiple_of((firsts[u] + sib) * 8, 8), 8), :]
+        gain[8 * u : 8 * u + 8, :] = dot_pair(partner, own_matrix(eu, u, C_ROWS))
+    down = gain[48:56, :]
+    for u in (5, 4, 3):
+        w = own_matrix(et, OWN_UPPER + u - 3, T_ROWS)
+        down = dot_pair(down, w, NT) + gain[8 * u : 8 * u + 8, :]
+    lines = {}
+    for u in (2, 1, 0):
+        both = jnp.concatenate(
+            [own_matrix(et, OWN + u, T_ROWS), own_matrix(et, SIBLING + u, T_ROWS)], axis=0
         )
-    down = gain[48:56, :]
-    for u in range(5, -1, -1):
-        w = et[pl.ds(64 + u, 64, stride=80), :][:, :64].astype(bf16)
-        down = dot_pair(down, w, NT) + gain[8 * u : 8 * u + 8, :]
-
-    late = (iota((128, 8, 128), 1) >= 4)
-    lab = ext[...].reshape(128, 8, 128)
-    early_lab = jnp.where(late, 0.0, pltpu.roll(lab, 4, 1)).reshape(1024, 128)
-    late_lab = jnp.where(late, lab, 0.0).reshape(1024, 128)
-    name = (iota((1024, 128), 1) + 1).astype(f32)
-    for h, label in enumerate((early_lab, late_lab)):
-        sums = dot(hot(label == name), recv[:, 0:256], TN)
-        for v in range(4):
-            cpl[pl.ds(4 * h + v, 32, stride=8), :] = wide(sums[:32, 64 * v : 64 * v + 64])
+        spread = dot_pair(down, both, NT)
+        lines[u] = flat(spread[:, 64:] + gain[8 * u : 8 * u + 8, :])
+        down = spread[:, :64]
+    own_line = flat(down)
+    z = device & 7
+    last = iota((32, 512), 0) == 31
+    for peer in range(8):
+        x = lax.bitwise_xor(z, peer)
+        line = jnp.where(x == 0, own_line, lines[0])
+        line = jnp.where(x >= 2, lines[1], line)
+        line = jnp.where(x >= 4, lines[2], line)
+        block = jnp.where(last, line, sums[32 * peer : 32 * peer + 32])
+        send[32 * peer : 32 * peer + 32, :] = block.astype(bf16)
+
+
+def flat(x):
+    return jnp.concatenate([x[v : v + 1] for v in range(8)], axis=1)
+
+
+def final_kernel(recv, near_mine, near_other, et, tr, bases, perm, out, cpl, dwn, dn, tree):
+    device = lax.axis_index("leaf")
+    core = lax.axis_index("vec")
+    z = device & 7
+    total = jnp.zeros((32, 512), f32)
+    levels = [jnp.zeros((1, 512), f32)] * 3
+    for peer in range(8):
+        block = recv[32 * peer : 32 * peer + 32, :].astype(f32)
+        total = total + block
+        x = lax.bitwise_xor(z, peer)
+        line = block[31:32]
+        for i, use in enumerate((x >= 4, (x >= 2) & (x < 4), x < 2)):
+            levels[i] = levels[i] + jnp.where(use, line, 0.0)
+    levels = jnp.concatenate(levels + [jnp.zeros((5, 512), f32)], axis=0)
+    for v in range(8):
+        cpl[pl.ds(v, 32, stride=8), :] = wide(total[:, 64 * v : 64 * v + 64])
+        dwn[pl.ds(v, 8, stride=8), :] = wide(levels[:, 64 * v : 64 * v + 64])
+    down = dot_pair(dwn[0:8, :64], own_matrix(et, OWN + 1, T_ROWS), NT) + dwn[8:16, :64]
+    down = dot_pair(down, own_matrix(et, OWN, T_ROWS), NT) + dwn[16:24, :64]
 
     dn[240:248, :] = down + cpl[240:248, :64]
     n = 1
@@ -410,46 +442,72 @@
     rec_c = lax.ppermute(send_c, axes, pairs_c)
     rec_a = lax.ppermute(send_a, axes, pairs_a)
     rec_b = lax.ppermute(send_b, axes, pairs_b)
-    (send,) = call(
-        coeff_kernel,
-        [((1024, 384), bf16)],
-        [pltpu.VMEM((256, 128), f32), pltpu.VMEM((1024, 128), f32), pltpu.VMEM((384, 512), bf16)],
-        (
-            vt, leaf_bases, transfers, jnp.transpose(coupling_blocks, (1, 2, 0)),
-            block_source.reshape(1, -1), block_owner.reshape(1, -1), block_target.reshape(1, -1),
-        ),
-        2 * 1024 * 512 * 384, 4 << 20,
-    )
-    recv = lax.all_to_all(send, "leaf", split_axis=0, concat_axis=0, tiled=True)
-    near_mine, near_send = call(
-        near_kernel,
-        [((8, HALF), f32), ((8, HALF), f32)],
-        [
-            pltpu.VMEM((16, 6144), bf16), pltpu.VMEM((8, 6144), f32), pltpu.VMEM((6144, 16), bf16),
-            pltpu.VMEM((16, 6144), bf16), pltpu.VMEM((16, HALF), f32),
-        ],
-        (vt, pt, rec_a, rec_b, rec_c),
-        2 * 67 * 512 * 512 * 256, 1 << 20,
-    )
-    near_other = lax.ppermute(near_send, axes, pairs_c)
     ut = jnp.transpose(up_transfer, (1, 2, 0))
     uc = jnp.transpose(up_coupling, (1, 2, 0))
     et, eu = call(
         matrices_kernel,
-        [((64 * 80, 128), f32), ((64 * 16, 128), f32)],
+        [((64 * T_ROWS, 128), f32), ((64 * C_ROWS, 128), f32)],
         [],
         (ut, uc),
-        2 * 8192 * 256 * 96, 8 << 20,
-    )
+        2 * 8192 * 256 * 48, 8 << 20,
+    )
+    cf, path = call(
+        coeff_kernel,
+        [((256, 128), f32), ((32, 64), f32)],
+        [],
+        (vt, leaf_bases, transfers, et),
+        2 * 512 * 512 * 256, 2 << 20,
+    )
+    (send,) = call(
+        product_kernel,
+        [((512, 640), bf16)],
+        [pltpu.VMEM((1024, 128), f32), pltpu.VMEM((640, 256), bf16)],
+        (
+            cf, path, jnp.transpose(coupling_blocks, (1, 2, 0)),
+            block_source.reshape(1, -1), block_owner.reshape(1, -1), block_target.reshape(1, -1),
+            rec_a, rec_b, rec_c,
+        ),
+        2 * 512 * 256 * 640, 4 << 20,
+        anywhere=3,
+    )
+    near_groups = [[xy * 8 + z for z in range(8)] for xy in range(peers // 8)]
+    far_groups = [[xy * 8 + z for xy in range(peers // 8)] for z in range(8)]
+    recv = lax.all_to_all(
+        send, "leaf", split_axis=0, concat_axis=0, tiled=True, axis_index_groups=far_groups
+    )
+    vw, fs, ft, begun = call(
+        near_setup_kernel,
+        [((16, 6144), bf16), ((6144, 16), bf16), ((16, 6144), bf16), ((16, HALF), f32)],
+        [pltpu.VMEM((8, 6144), f32)],
+        (vt, pt, rec_a, rec_b, rec_c),
+        2 * 40 * 512 * 512 * 256, 1 << 20, vmem=24,
+    )
+    (send,) = call(
+        middle_kernel,
+        [((256, 512), bf16)],
+        [pltpu.VMEM((512, 128), f32), pltpu.VMEM((256, 64), f32), pltpu.VMEM((56, 64), f32)],
+        (recv, path, et, eu),
+        2 * 256 * 512 * 512, 2 << 20,
+    )
+    recv = lax.all_to_all(
+        send, "leaf", split_axis=0, concat_axis=0, tiled=True, axis_index_groups=near_groups
+    )
+    near_mine, near_send = call(
+        near_rest_kernel,
+        [((8, HALF), f32), ((8, HALF), f32)],
+        [pltpu.VMEM((16, HALF), f32)],
+        (vw, fs, ft, begun),
+        2 * 27 * 512 * 512 * 256, 1 << 20, vmem=24,
+    )
+    near_other = lax.ppermute(near_send, axes, pairs_c)
     (out,) = call(
         final_kernel,
         [((8, COLS), bf16)],
         [
-            pltpu.VMEM((1024, 128), f32), pltpu.VMEM((512, 128), f32), pltpu.VMEM((512, 128), f32),
-            pltpu.VMEM((512, 64), f32), pltpu.VMEM((576, 128), f32), pltpu.VMEM((56, 64), f32),
-            pltpu.VMEM((256, 128), f32), pltpu.VMEM((248, 64), f32), pltpu.VMEM((8, COLS), f32),
+            pltpu.VMEM((256, 128), f32), pltpu.VMEM((64, 128), f32),
+            pltpu.VMEM((248, 64), f32), pltpu.VMEM((8, COLS), f32),
         ],
-        (recv, near_mine, near_other, ut, et, eu, transfers, leaf_bases, leaf_order),
+        (recv, near_mine, near_other, et, transfers, leaf_bases, leaf_order),
         2 * 256 * 256 * COLS, 8 << 20,
     )
     return out

time: 76 us -> 70.4 us (0.926)
  the two profiles are of different devices: /device:TPU:7 before, /device:TPU:8 now
where the time goes in v2:
time: 70.4 us; the launch traced here: 69.3 us
  Pallas kernels  25.6 us (36%)
  starting transfers between devices  23.1 us (33%)
  local copies, waits for them, and re-layouts  17 us (24%)
  waiting for transfers between devices  3.32 us (5%)
    pallas_call x8, Pallas kernels, call(): pl.pallas_call(kernel, out_shape=[jax.ShapeDtypeStruct(s, d) for s, d in...  25.6 us
    unnamed x64, local copies, waits for them, and re-layouts  17 us
    all_to_all x2, starting transfers between devices, shards(): lax.all_to_all(send, 'leaf', split_axis=0, concat_axis=0, tiled=True, axi...  13.3 us
    ppermute x1, starting transfers between devices, shards(): rec_a = lax.ppermute(send_a, axes, pairs_a)  7.74 us
    ppermute x1, starting transfers between devices, shards(): rec_b = lax.ppermute(send_b, axes, pairs_b)  1.92 us
    ppermute x1, waiting for transfers between devices, shards(): rec_b = lax.ppermute(send_b, axes, pairs_b)  1.53 us
  transfers between devices with their start and end apart: 6, of which 3 were waited for; matrix products, arithmetic and copies ran while one was open for 0% of the time, Pallas kernels for 18%

profile of v2, /device:TPU:8, one launch (start us, length us, event | category | flops | bytes accessed | tf_op | source)
XLA Modules:
  0.0 69.3 jit_solution(11699533926700303619)
XLA Ops:
  0.0 1.0 %copy-done.16 = bf16[8,8192]{1,0:T(8,128)(2,1)S(1)} copy-done((bf16[8,8192]{1,0:T(8,128)(2,1)S(1)}, bf16[8,8192]{1,0:T(8,128)(2,1)}, u32[]{:S(2)}) %copy-start.16) | copy-done | bytes 131096
  1.1 1.1 %copy-done.17 = bf16[3,8192]{1,0:T(4,128)(2,1)S(1)} copy-done((bf16[3,8192]{1,0:T(4,128)(2,1)S(1)}, bf16[3,8192]{1,0:T(4,128)(2,1)}, u32[]{:S(2)}) %copy-start.17) | copy-done | bytes 49176
  2.9 3.0 %shard_map.109 = (bf16[8,8192]{1,0:T(8,128)(2,1)S(1)}, bf16[8,8192]{1,0:T(8,128)(2,1)S(1)}, bf16[16,1024]{1,0:T(8,128)(2,1)S(1)}, bf16[8,1024]{1,0:T(8,128)(2,1)S(1)}, bf16[8,5120]{1,0:T(8,128)(2,1)S(1)}) custom-call(bf16[3,8192]{1,0:T(4,128)(2,1)S(1)} %copy-done.17, bf16[8,8192]{1,0:T(8,128)(2,1)S(1)} %copy-done.16, s32[1,8192]{1,0:T(1,128)S(1)} %copy-done.18), custom_call_target="tpu_custom_call" | custom-call | flops 1610612736 | bytes 1048576 | tf_op jit(solution)/shard_map/pallas_call | solution.py:54
  6.0 7.7 %collective-permute-start = (bf16[16,1024]{1,0:T(8,128)(2,1)S(1)}, bf16[16,1024]{1,0:T(8,128)(2,1)S(1)}, u32[]{:S(2)}, u32[]{:S(2)}) collective-permute-start(bf16[16,1024]{1,0:T(8,128)(2,1)S(1)} %get-tuple-element.24), channel_id=1, source_target_pairs={{1,2},{2,1},{3,4},{4,3},{5,6},{6,5},{7,8},{8,7},{9,10},{10,9},{11,... | collective-permute-start | bytes 98312 | tf_op jit(solution)/shard_map/ppermute | solution.py:443
  13.8 1.9 %collective-permute-start.1 = (bf16[8,1024]{1,0:T(8,128)(2,1)S(1)}, bf16[8,1024]{1,0:T(8,128)(2,1)S(1)}, u32[]{:S(2)}, u32[]{:S(2)}) collective-permute-start(bf16[8,1024]{1,0:T(8,128)(2,1)S(1)} %get-tuple-element.25), channel_id=1, source_target_pairs={{0,2},{3,1},{2,4},{5,3},{4,6},{7,5},{6,8},{9,7},{8,10},{11,9},{10,... | collective-permute-start | bytes 49160 | tf_op jit(solution)/shard_map/ppermute | solution.py:444
  15.7 1.9 %shard_map.110 = (f32[2560,128]{1,0:T(8,128)S(1)}, f32[512,128]{1,0:T(8,128)S(1)}) custom-call(bf16[64,64,254]{2,1,0:T(8,128)(2,1)S(1)} %bitcast.12, bf16[64,64,254]{2,1,0:T(8,128)(2,1)S(1)} %bitcast.13), custom_call_target="tpu_custom_call" | custom-call | flops 201326592 | bytes 8388608 | tf_op jit(solution)/shard_map/pallas_call | solution.py:54
  18.4 1.5 %shard_map.111 = (f32[256,128]{1,0:T(8,128)S(1)}, f32[32,64]{1,0:T(8,128)S(1)}) custom-call(bf16[8,8192]{1,0:T(8,128)(2,1)S(1)} %get-tuple-element.20.vt, bf16[16,64,512]{2,1,0:T(8,128)(2,1)S(1)} %copy-done.3, bf16[30,64,64]{2,1,0:T(8,128)(2,1)S(1)} %copy-done.4, f32[2560,128]{1,0:T(8,128)S(1)} %get-tuple-element.21.et), custom_call_target="tpu_custom_call" | custom-call | flops 134217728 | bytes 2097152 | tf_op jit(solution)/shard_map/pallas_call | solution.py:54
  20.0 1.5 %collective-permute-done.1.seen_b.rec_b = bf16[8,1024]{1,0:T(8,128)(2,1)S(1)} collective-permute-done((bf16[8,1024]{1,0:T(8,128)(2,1)S(1)}, bf16[8,1024]{1,0:T(8,128)(2,1)S(1)}, u32[]{:S(2)}, u32[]{:S(2)}) %collective-permute-start.1) | collective-permute-done | bytes 16416 | tf_op jit(solution)/shard_map/ppermute | solution.py:444
  21.6 4.2 %shard_map.112 = bf16[512,640]{1,0:T(8,128)(2,1)} custom-call(f32[256,128]{1,0:T(8,128)S(1)} %get-tuple-element.22.cf, f32[32,64]{1,0:T(8,128)S(1)} %get-tuple-element.23.path, bf16[64,64,256]{2,1,0:T(8,128)(2,1)S(1)} %bitcast.11, s32[1,256]{1,0:T(1,128)S(1)} %bitcast.15, s32[1,256]{1,0:T(1,128)S(1)} %bitcast.16, s32[1,256]{1,0:T(1,128)S(1)} %bitcast.17, ...), custom_call_target="tpu_custom_call" | custom-call | flops 167772160 | bytes 4194304 | tf_op jit(solution)/shard_map/pallas_call | solution.py:54
  25.8 9.4 %all-to-all-start = ((bf16[16,32,640]{2,1,0:T(8,128)(2,1)}), bf16[16,32,640]{2,1,0:T(8,128)(2,1)S(1)}, u32[]{:S(2)}, u32[]{:S(2)}) async-start(bf16[16,32,640]{2,1,0:T(8,128)(2,1)} %bitcast.6), calls=%async_computation | async-start | bytes 1310720 | tf_op jit(solution)/shard_map/all_to_all | solution.py:475
  37.7 0.9 %copy-done.25 = bf16[8,8192]{1,0:T(8,128)(2,1)S(1)} copy-done((bf16[8,8192]{1,0:T(8,128)(2,1)S(1)}, bf16[8,8192]{1,0:T(8,128)(2,1)}, u32[]{:S(2)}) %copy-start.25) | copy-done | bytes 131096
  38.6 5.3 %shard_map.114 = (bf16[16,6144]{1,0:T(8,128)(2,1)S(1)}, bf16[6144,16]{1,0:T(8,128)(2,1)S(1)}, bf16[16,6144]{1,0:T(8,128)(2,1)S(1)}, f32[16,4096]{1,0:T(8,128)S(1)}) custom-call(bf16[8,8192]{1,0:T(8,128)(2,1)S(1)} %copy-done.8, bf16[8,8192]{1,0:T(8,128)(2,1)S(1)} %copy-done.25, bf16[16,1024]{1,0:T(8,128)(2,1)S(1)} %collective-permute-done.seen_a.rec_a, ...), custom_call_target="tpu_custom_call" | custom-call | flops 5368709120 | bytes 1048576 | tf_op jit(solution)/shard_map/pallas_call | solution.py:54
  43.9 1.2 %copy-done.22 = bf16[6144,16]{1,0:T(8,128)(2,1)} copy-done((bf16[6144,16]{1,0:T(8,128)(2,1)}, bf16[6144,16]{1,0:T(8,128)(2,1)S(1)}, u32[]{:S(2)}) %copy-start.22) | copy-done | bytes 196632
  47.2 0.9 %copy-done.6 = f32[512,128]{1,0:T(8,128)S(1)} copy-done((f32[512,128]{1,0:T(8,128)S(1)}, f32[512,128]{1,0:T(8,128)}, u32[]{:S(2)}) %copy-start.6) | copy-done | bytes 262168
  48.1 2.5 %shard_map.113 = bf16[256,512]{1,0:T(8,128)(2,1)} custom-call(bf16[512,640]{1,0:T(8,128)(2,1)S(1)} %bitcast.10, f32[32,64]{1,0:T(8,128)S(1)} %get-tuple-element.23.path, f32[2560,128]{1,0:T(8,128)S(1)} %get-tuple-element.21.et, f32[512,128]{1,0:T(8,128)S(1)} %copy-done.6), custom_call_target="tpu_custom_call" | custom-call | flops 134217728 | bytes 2097152 | tf_op jit(solution)/shard_map/pallas_call | solution.py:54
  50.6 3.9 %all-to-all-start.1 = ((bf16[8,32,512]{2,1,0:T(8,128)(2,1)}), bf16[8,32,512]{2,1,0:T(8,128)(2,1)S(1)}, u32[]{:S(2)}, u32[]{:S(2)}) async-start(bf16[8,32,512]{2,1,0:T(8,128)(2,1)} %bitcast.8), calls=%async_computation.1 | async-start | bytes 524288 | tf_op jit(solution)/shard_map/all_to_all | solution.py:492
  54.5 1.4 %copy-done.23 = bf16[6144,16]{1,0:T(8,128)(2,1)S(1)} copy-done((bf16[6144,16]{1,0:T(8,128)(2,1)S(1)}, bf16[6144,16]{1,0:T(8,128)(2,1)}, u32[]{:S(2)}) %copy-start.23) | copy-done | bytes 196632
  55.9 0.9 %copy-done.27 = f32[16,4096]{1,0:T(8,128)S(1)} copy-done((f32[16,4096]{1,0:T(8,128)S(1)}, f32[16,4096]{1,0:T(8,128)}, u32[]{:S(2)}) %copy-start.27) | copy-done | bytes 262168
  56.9 0.9 %copy-done.29 = bf16[16,6144]{1,0:T(8,128)(2,1)S(1)} copy-done((bf16[16,6144]{1,0:T(8,128)(2,1)S(1)}, bf16[16,6144]{1,0:T(8,128)(2,1)}, u32[]{:S(2)}) %copy-start.29) | copy-done | bytes 196632
  57.8 0.9 %copy-done.31 = bf16[16,6144]{1,0:T(8,128)(2,1)S(1)} copy-done((bf16[16,6144]{1,0:T(8,128)(2,1)S(1)}, bf16[16,6144]{1,0:T(8,128)(2,1)}, u32[]{:S(2)}) %copy-start.31) | copy-done | bytes 196632
  58.8 3.8 %shard_map.115 = (f32[8,4096]{1,0:T(8,128)S(1)}, f32[8,4096]{1,0:T(8,128)S(1)}) custom-call(bf16[16,6144]{1,0:T(8,128)(2,1)S(1)} %copy-done.29, bf16[6144,16]{1,0:T(8,128)(2,1)S(1)} %copy-done.23, bf16[16,6144]{1,0:T(8,128)(2,1)S(1)} %copy-done.31, f32[16,4096]{1,0:T(8,128)S(1)} %copy-done.27), custom_call_target="tpu_custom_call" | custom-call | flops 3623878656 | bytes 1048576 | tf_op jit(solution)/shard_map/pallas_call | solution.py:54
  63.2 1.3 %collective-permute-done.3.near_other = f32[8,4096]{1,0:T(8,128)S(1)} collective-permute-done((f32[8,4096]{1,0:T(8,128)S(1)}, f32[8,4096]{1,0:T(8,128)S(1)}, u32[]{:S(2)}, u32[]{:S(2)}) %collective-permute-start.3) | collective-permute-done | bytes 131104 | tf_op jit(solution)/shard_map/ppermute | solution.py:502
  65.0 0.9 %copy-done.21 = f32[8,4096]{1,0:T(8,128)S(1)} copy-done((f32[8,4096]{1,0:T(8,128)S(1)}, f32[8,4096]{1,0:T(8,128)}, u32[]{:S(2)}) %copy-start.21) | copy-done | bytes 131096
  65.9 3.3 %shard_map.116 = bf16[8,8192]{1,0:T(8,128)(2,1)} custom-call(bf16[256,512]{1,0:T(8,128)(2,1)S(1)} %bitcast.14, f32[8,4096]{1,0:T(8,128)S(1)} %copy-done.21, f32[8,4096]{1,0:T(8,128)S(1)} %collective-permute-done.3.near_other, f32[2560,128]{1,0:T(8,128)S(1)} %get-tuple-element.21.et, bf16[30,64,64]{2,1,0:T(8,128)(2,1)S(1)} %copy-done.4, ...), custom_call_target="tpu_custom_call" | custom-call | flops 1073741824 | bytes 8388608 | tf_op jit(solution)/shard_map/pallas_call | solution.py:54
  (60 shorter events, 7.3 us)
Async XLA Ops:
  0.0 15.7 %copy-start.1 = (bf16[254,64,64]{0,2,1:T(8,128)(2,1)S(1)}, bf16[254,64,64]{0,2,1:T(8,128)(2,1)}, u32[]{:S(2)}) copy-start(bf16[254,64,64]{0,2,1:T(8,128)(2,1)} %param.20) | copy-start | bytes 6242308
  0.0 15.7 %copy-start.2 = (bf16[254,64,64]{0,2,1:T(8,128)(2,1)S(1)}, bf16[254,64,64]{0,2,1:T(8,128)(2,1)}, u32[]{:S(2)}) copy-start(bf16[254,64,64]{0,2,1:T(8,128)(2,1)} %param.21) | copy-start | bytes 6242308
  0.0 1.1 %copy-start.16 = (bf16[8,8192]{1,0:T(8,128)(2,1)S(1)}, bf16[8,8192]{1,0:T(8,128)(2,1)}, u32[]{:S(2)}) copy-start(bf16[8,8192]{1,0:T(8,128)(2,1)} %vec.1) | copy-start | bytes 393220
  1.1 1.1 %copy-start.17 = (bf16[3,8192]{1,0:T(4,128)(2,1)S(1)}, bf16[3,8192]{1,0:T(4,128)(2,1)}, u32[]{:S(2)}) copy-start(bf16[3,8192]{1,0:T(4,128)(2,1)} %pts.1) | copy-start | bytes 147460
  5.9 11.8 %copy-start.24 = (bf16[8,8192]{1,0:T(8,128)(2,1)}, bf16[8,8192]{1,0:T(8,128)(2,1)S(1)}, u32[]{:S(2)}) copy-start(bf16[8,8192]{1,0:T(8,128)(2,1)S(1)} %get-tuple-element.28.pt) | copy-start | bytes 393220
  5.9 12.5 %copy-start.7 = (bf16[8,8192]{1,0:T(8,128)(2,1)}, bf16[8,8192]{1,0:T(8,128)(2,1)S(1)}, u32[]{:S(2)}) copy-start(bf16[8,8192]{1,0:T(8,128)(2,1)S(1)} %get-tuple-element.20.vt) | copy-start | bytes 393220
  5.9 15.6 %collective-permute-start.2 = (bf16[8,5120]{1,0:T(8,128)(2,1)S(1)}, bf16[8,5120]{1,0:T(8,128)(2,1)S(1)}, u32[]{:S(2)}, u32[]{:S(2)}) collective-permute-start(bf16[8,5120]{1,0:T(8,128)(2,1)S(1)} %get-tuple-element.26), channel_id=1, source_target_pairs={{0,1},{1,0},{2,3},{3,2},{4,5},{5,4},{6,7},{7,6},{8,9},{9,8},{10,11... | collective-permute-start | bytes 245768 | tf_op jit(solution)/shard_map/ppermute | solution.py:442
  6.0 15.5 %collective-permute-start = (bf16[16,1024]{1,0:T(8,128)(2,1)S(1)}, bf16[16,1024]{1,0:T(8,128)(2,1)S(1)}, u32[]{:S(2)}, u32[]{:S(2)}) collective-permute-start(bf16[16,1024]{1,0:T(8,128)(2,1)S(1)} %get-tuple-element.24), channel_id=1, source_target_pairs={{1,2},{2,1},{3,4},{4,3},{5,6},{6,5},{7,8},{8,7},{9,10},{10,9},{11,... | collective-permute-start | bytes 98312 | tf_op jit(solution)/shard_map/ppermute | solution.py:443
  13.8 7.7 %collective-permute-start.1 = (bf16[8,1024]{1,0:T(8,128)(2,1)S(1)}, bf16[8,1024]{1,0:T(8,128)(2,1)S(1)}, u32[]{:S(2)}, u32[]{:S(2)}) collective-permute-start(bf16[8,1024]{1,0:T(8,128)(2,1)S(1)} %get-tuple-element.25), channel_id=1, source_target_pairs={{0,2},{3,1},{2,4},{5,3},{4,6},{7,5},{6,8},{9,7},{8,10},{11,9},{10,... | collective-permute-start | bytes 49160 | tf_op jit(solution)/shard_map/ppermute | solution.py:444
  15.7 2.7 %copy-start.3 = (bf16[16,64,512]{2,1,0:T(8,128)(2,1)S(1)}, bf16[16,64,512]{2,1,0:T(8,128)(2,1)}, u32[]{:S(2)}) copy-start(bf16[16,64,512]{2,1,0:T(8,128)(2,1)} %bases.3) | copy-start | bytes 3145732
  15.7 2.7 %copy-start.4 = (bf16[30,64,64]{2,1,0:T(8,128)(2,1)S(1)}, bf16[30,64,64]{2,1,0:T(8,128)(2,1)}, u32[]{:S(2)}) copy-start(bf16[30,64,64]{2,1,0:T(8,128)(2,1)} %tr.3) | copy-start | bytes 737284
  18.4 3.1 %copy-start = (bf16[256,64,64]{0,2,1:T(8,128)(2,1)S(1)}, bf16[256,64,64]{0,2,1:T(8,128)(2,1)}, u32[]{:S(2)}) copy-start(bf16[256,64,64]{0,2,1:T(8,128)(2,1)} %param.16) | copy-start | bytes 6291460
  18.4 3.1 %copy-start.13 = (s32[256]{0:T(256)S(1)}, s32[256]{0:T(256)}, u32[]{:S(2)}) copy-start(s32[256]{0:T(256)} %param.17) | copy-start | bytes 3076
  18.4 3.1 %copy-start.14 = (s32[256,1]{0,1:T(1,128)S(1)}, s32[256,1]{0,1:T(1,128)}, u32[]{:S(2)}) copy-start(s32[256,1]{0,1:T(1,128)} %param.18) | copy-start | bytes 3076
  18.4 3.1 %copy-start.15 = (s32[256]{0:T(256)S(1)}, s32[256]{0:T(256)}, u32[]{:S(2)}) copy-start(s32[256]{0:T(256)} %param.19) | copy-start | bytes 3076
  21.5 4.3 %copy-start.11 = (bf16[8,1024]{1,0:T(8,128)(2,1)}, bf16[8,1024]{1,0:T(8,128)(2,1)S(1)}, u32[]{:S(2)}) copy-start(bf16[8,1024]{1,0:T(8,128)(2,1)S(1)} %collective-permute-done.1.seen_b.rec_b) | copy-start | bytes 49156
  21.5 4.3 %copy-start.9 = (bf16[8,5120]{1,0:T(8,128)(2,1)}, bf16[8,5120]{1,0:T(8,128)(2,1)S(1)}, u32[]{:S(2)}) copy-start(bf16[8,5120]{1,0:T(8,128)(2,1)S(1)} %collective-permute-done.2.seen_c.rec_c) | copy-start | bytes 245764
  25.8 21.4 %all-to-all-start = ((bf16[16,32,640]{2,1,0:T(8,128)(2,1)}), bf16[16,32,640]{2,1,0:T(8,128)(2,1)S(1)}, u32[]{:S(2)}, u32[]{:S(2)}) async-start(bf16[16,32,640]{2,1,0:T(8,128)(2,1)} %bitcast.6), calls=%async_computation | async-start | bytes 1310720 | tf_op jit(solution)/shard_map/all_to_all | solution.py:475
  43.9 1.2 %copy-start.22 = (bf16[6144,16]{1,0:T(8,128)(2,1)}, bf16[6144,16]{1,0:T(8,128)(2,1)S(1)}, u32[]{:S(2)}) copy-start(bf16[6144,16]{1,0:T(8,128)(2,1)S(1)} %get-tuple-element.30.fs) | copy-start | bytes 589828
  47.2 1.0 %copy-start.6 = (f32[512,128]{1,0:T(8,128)S(1)}, f32[512,128]{1,0:T(8,128)}, u32[]{:S(2)}) copy-start(f32[512,128]{1,0:T(8,128)} %copy-done.5) | copy-start | bytes 786436
  50.6 14.4 %all-to-all-start.1 = ((bf16[8,32,512]{2,1,0:T(8,128)(2,1)}), bf16[8,32,512]{2,1,0:T(8,128)(2,1)S(1)}, u32[]{:S(2)}, u32[]{:S(2)}) async-start(bf16[8,32,512]{2,1,0:T(8,128)(2,1)} %bitcast.8), calls=%async_computation.1 | async-start | bytes 524288 | tf_op jit(solution)/shard_map/all_to_all | solution.py:492
  54.5 1.4 %copy-start.23 = (bf16[6144,16]{1,0:T(8,128)(2,1)S(1)}, bf16[6144,16]{1,0:T(8,128)(2,1)}, u32[]{:S(2)}) copy-start(bf16[6144,16]{1,0:T(8,128)(2,1)} %copy-done.22) | copy-start | bytes 589828
  58.7 6.3 %copy-start.19 = (s32[1,8192]{1,0:T(1,128)S(1)}, s32[1,8192]{1,0:T(1,128)}, u32[]{:S(2)}) copy-start(s32[1,8192]{1,0:T(1,128)} %perm.3) | copy-start | bytes 98308
  63.2 1.3 %collective-permute-start.3 = (f32[8,4096]{1,0:T(8,128)S(1)}, f32[8,4096]{1,0:T(8,128)S(1)}, u32[]{:S(2)}, u32[]{:S(2)}) collective-permute-start(f32[8,4096]{1,0:T(8,128)S(1)} %get-tuple-element.34), channel_id=1, source_target_pairs={{0,1},{1,0},{2,3},{3,2},{4,5},{5,4},{6,7},{7,6},{8,9},{9,8},{10,11... | collective-permute-start | bytes 393224 | tf_op jit(solution)/shard_map/ppermute | solution.py:502
  (14 other events, 11.3 us)

commit v3 on v2

--- a/solution.py
+++ b/solution.py
@@ -50,20 +50,38 @@
     return y[:n] + y[n:]
 
 
-def call(kernel, outs, scratch, args, flops, nbytes, vmem=16, anywhere=0):
+ANY = pl.BlockSpec(memory_space=pl.ANY)
+SPEC = {"v": VM, "a": ANY, "h": pl.BlockSpec(memory_space=pltpu.HBM)}
+
+
+def call(kernel, outs, scratch, args, kinds, flops, nbytes, vmem=16):
+    ins, results = kinds.split(">")
     return pl.pallas_call(
         kernel,
         out_shape=[jax.ShapeDtypeStruct(s, d) for s, d in outs],
-        in_specs=[VM] * (len(args) - anywhere) + [pl.BlockSpec(memory_space=pl.ANY)] * anywhere,
-        out_specs=[VM] * len(outs),
+        in_specs=[SPEC[k] for k in ins],
+        out_specs=[SPEC[k] for k in results],
         scratch_shapes=scratch,
         compiler_params=pltpu.CompilerParams(vmem_limit_bytes=vmem << 20),
         cost_estimate=pl.CostEstimate(flops=flops, bytes_accessed=nbytes, transcendentals=0),
     )(*args)
 
 
-def gather_kernel(pts, vec, perm, vt, pt, send_a, send_b, send_c, dv, dp):
+def fetch(sems, *pairs):
+    copies = [
+        pltpu.make_async_copy(src, dst, sems.at[i]) for i, (src, dst) in enumerate(pairs)
+    ]
+    for copy in copies:
+        copy.start()
+    return copies
+
+
+def gather_kernel(
+    pts_in, vec_in, perm_in, vt, pt, send_a, send_b, send_c, pts, vec, perm, dv, dp, sems
+):
     core = lax.axis_index("vec")
+    for copy in fetch(sems, (perm_in, perm), (vec_in, vec), (pts_in, pts)):
+        copy.wait()
     for m in range(16):
         a, b = 512 * m, 512 * m + 256
         dv[16 * m : 16 * m + 16, :] = jnp.concatenate(
@@ -110,7 +128,7 @@
         send_c[...] = vt[:, :LOCAL]
 
 
-def coeff_kernel(vt, bases, tr, et, cf, path):
+def coeff_kernel(vt, bases, tr, mats, cf, path):
     cf[248:256, :] = jnp.zeros((8, 128), f32)
     for leaf in range(16):
         cf[8 * leaf : 8 * leaf + 8, :64] = dot(
@@ -129,12 +147,12 @@
     value = cf[240:248, :64]
     for u in range(3):
         path[8 * u : 8 * u + 8, :] = value
-        value = dot_pair(value, own_matrix(et, OWN + u, T_ROWS))
+        value = dot_pair(value, own_matrix(mats, OWN + u))
     path[24:32, :] = value
 
 
-def own_matrix(ref, row, rows):
-    return ref[pl.ds(row, 64, stride=rows), :][:, :64].astype(bf16)
+def own_matrix(mats, row, count=1):
+    return mats[64 * row : 64 * (row + count), :]
 
 
 def product_kernel(cf, path, cp, bsrc, bown, btgt, seen_a, seen_b, seen_c, send, pick, prod):
@@ -190,8 +208,11 @@
     return a, b, x - a - b
 
 
-def near_setup_kernel(vt, pt, rec_a, rec_b, rec_c, vw, fs, ft, acc, pw):
+def near_window(ins, bufs, sems, leaves, vw, fs, ft, pw):
     core = lax.axis_index("vec")
+    for copy in fetch(sems, *zip(ins, bufs)):
+        copy.wait()
+    vt, pt, rec_a, rec_b, rec_c = bufs
 
     @pl.when(core == 0)
     def _():
@@ -211,7 +232,7 @@
         pw[:, :LOCAL] = pt[:, COLS - LOCAL :].astype(f32)
         pw[:, LOCAL:] = rec_a[8:16, :].astype(f32)
 
-    for leaf in range(12):
+    for leaf in leaves:
         cols = slice(LEAF * leaf, LEAF * leaf + LEAF)
         p = pw[0:3, cols]
         norm = p[0:1] * p[0:1] + p[1:2] * p[1:2] + p[2:3] * p[2:3]
@@ -224,30 +245,48 @@
         target = jnp.concatenate([-2.0 * p, one, parts, smooth, pad], axis=0)
         fs[cols, :] = jnp.transpose(source).astype(bf16)
         ft[:, cols] = target.astype(bf16)
+
+
+def near_target(t, vw, fs, ft, acc):
+    tc = slice(LEAF * t, LEAF * t + LEAF)
+    to = slice(LEAF * (t - 2), LEAF * (t - 1))
+    total = jnp.zeros((16, LEAF), f32)
+    for s in range(t - 2, t + 3):
+        if 2 <= s < t:
+            continue
+        sc = slice(LEAF * s, LEAF * s + LEAF)
+        kernel = lax.rsqrt(dot(fs[sc, :], ft[:, tc])).astype(bf16)
+        total = total + dot(vw[:, sc], kernel)
+        if t < s < 10:
+            so = slice(LEAF * (s - 2), LEAF * (s - 1))
+            acc[:, so] += dot(vw[:, tc], kernel, NT)
+    acc[:, to] += total
+
+
+def near_first_kernel(*refs):
+    ins, begun, bufs = refs[:5], refs[5], refs[6:11]
+    vw, fs, ft, pw, acc, sems, out_sems = refs[11:]
+    near_window(ins, bufs, sems, range(0, 8), vw, fs, ft, pw)
     acc[...] = jnp.zeros_like(acc)
-    near_blocks(range(2, 6), vw, fs, ft, acc)
-
-
-def near_blocks(targets, vw, fs, ft, acc):
-    for t in targets:
-        tc = slice(LEAF * t, LEAF * t + LEAF)
-        to = slice(LEAF * (t - 2), LEAF * (t - 1))
-        total = jnp.zeros((16, LEAF), f32)
-        for s in range(t - 2, t + 3):
-            if 2 <= s < t:
-                continue
-            sc = slice(LEAF * s, LEAF * s + LEAF)
-            kernel = lax.rsqrt(dot(fs[sc, :], ft[:, tc])).astype(bf16)
-            total = total + dot(vw[:, sc], kernel)
-            if t < s < 10:
-                so = slice(LEAF * (s - 2), LEAF * (s - 1))
-                acc[:, so] += dot(vw[:, tc], kernel, NT)
-        acc[:, to] += total
-
-
-def near_rest_kernel(vw, fs, ft, begun, mine, other, acc):
-    acc[...] = begun[...]
-    near_blocks(range(6, 10), vw, fs, ft, acc)
+    copies = []
+    for t in range(2, 6):
+        near_target(t, vw, fs, ft, acc)
+        cols = slice(LEAF * (t - 2), LEAF * (t - 1) if t < 5 else HALF)
+        copies += [pltpu.make_async_copy(acc.at[:, cols], begun.at[:, cols], out_sems.at[t - 2])]
+        copies[-1].start()
+    for copy in copies:
+        copy.wait()
+
+
+def near_rest_kernel(*refs):
+    ins, begun, mine, other, bufs = refs[:5], refs[5], refs[6], refs[7], refs[8:13]
+    vw, fs, ft, pw, acc, sems, begun_sem = refs[13:]
+    first = pltpu.make_async_copy(begun, acc, begun_sem)
+    first.start()
+    near_window(ins, bufs, sems, range(6, 12), vw, fs, ft, pw)
+    first.wait()
+    for t in range(6, 10):
+        near_target(t, vw, fs, ft, acc)
     mine[...] = acc[0:8, :] * (8.0 / LEAF)
     other[...] = acc[8:16, :] * (8.0 / LEAF)
 
@@ -257,11 +296,13 @@
 OWN = 30
 SIBLING = 33
 OWN_UPPER = 36
+COUPLING = 40
+MATRICES = 48
 T_ROWS = 40
 C_ROWS = 8
 
 
-def matrices_kernel(ut, uc, et, eu):
+def matrices_kernel(ut, uc, mats, et, eu):
     device = lax.axis_index("leaf")
 
     def node(u, other=False):
@@ -291,10 +332,17 @@
         return carry
 
     lax.fori_loop(0, 16, step, 0, unroll=4)
-
-
-def middle_kernel(recv, path, et, eu, send, ext, xs, gain):
+    for m in range(39):
+        mats[64 * m : 64 * m + 64, :] = et[pl.ds(m, 64, stride=T_ROWS), :][:, :64].astype(bf16)
+    for m in range(7):
+        at = 64 * (COUPLING + m)
+        mats[at : at + 64, :] = eu[pl.ds(m, 64, stride=C_ROWS), :][:, :64].astype(bf16)
+
+
+def middle_kernel(recv_in, path_in, mats_in, send, recv, path, mats, ext, xs, gain, sems):
     device = lax.axis_index("leaf")
+    for copy in fetch(sems, (recv_in, recv), (path_in, path), (mats_in, mats)):
+        copy.wait()
     ext[...] = recv[:, 512:640].astype(f32)
 
     labels = jnp.concatenate(
@@ -315,7 +363,7 @@
             r = 8 * (first + 2 * m)
             e = LEVEL_START[u] - UPPER + 2 * m
             pair = jnp.concatenate([xs[r : r + 8, :], xs[r + 8 : r + 16, :]], axis=1)
-            w = jnp.concatenate([own_matrix(et, e, T_ROWS), own_matrix(et, e + 1, T_ROWS)], axis=0)
+            w = own_matrix(mats, e, 2)
             t = 8 * (first + n + m)
             xs[t : t + 8, :] = dot_pair(pair, w)
         first += n
@@ -327,15 +375,15 @@
         else:
             sib = lax.bitwise_xor(lax.shift_right_logical(device, u), 1)
             partner = xs[pl.ds(pl.multiple_of((firsts[u] + sib) * 8, 8), 8), :]
-        gain[8 * u : 8 * u + 8, :] = dot_pair(partner, own_matrix(eu, u, C_ROWS))
+        gain[8 * u : 8 * u + 8, :] = dot_pair(partner, own_matrix(mats, COUPLING + u))
     down = gain[48:56, :]
     for u in (5, 4, 3):
-        w = own_matrix(et, OWN_UPPER + u - 3, T_ROWS)
+        w = own_matrix(mats, OWN_UPPER + u - 3)
         down = dot_pair(down, w, NT) + gain[8 * u : 8 * u + 8, :]
     lines = {}
     for u in (2, 1, 0):
         both = jnp.concatenate(
-            [own_matrix(et, OWN + u, T_ROWS), own_matrix(et, SIBLING + u, T_ROWS)], axis=0
+            [own_matrix(mats, OWN + u), own_matrix(mats, SIBLING + u)], axis=0
         )
         spread = dot_pair(down, both, NT)
         lines[u] = flat(spread[:, 64:] + gain[8 * u : 8 * u + 8, :])
@@ -356,7 +404,20 @@
     return jnp.concatenate([x[v : v + 1] for v in range(8)], axis=1)
 
 
-def final_kernel(recv, near_mine, near_other, et, tr, bases, perm, out, cpl, dwn, dn, tree):
+def final_kernel(
+    recv_in, mine_in, other_in, mats_in, tr, bases, perm_in, out,
+    recv, near_mine, near_other, mats, perm, cpl, dwn, dn, tree, sems,
+):
+    copies = fetch(
+        sems,
+        (recv_in, recv),
+        (mats_in.at[64 * OWN : 64 * OWN + 128], mats),
+        (mine_in, near_mine),
+        (other_in, near_other),
+        (perm_in, perm),
+    )
+    for copy in copies:
+        copy.wait()
     device = lax.axis_index("leaf")
     core = lax.axis_index("vec")
     z = device & 7
@@ -373,8 +434,8 @@
     for v in range(8):
         cpl[pl.ds(v, 32, stride=8), :] = wide(total[:, 64 * v : 64 * v + 64])
         dwn[pl.ds(v, 8, stride=8), :] = wide(levels[:, 64 * v : 64 * v + 64])
-    down = dot_pair(dwn[0:8, :64], own_matrix(et, OWN + 1, T_ROWS), NT) + dwn[8:16, :64]
-    down = dot_pair(down, own_matrix(et, OWN, T_ROWS), NT) + dwn[16:24, :64]
+    down = dot_pair(dwn[0:8, :64], own_matrix(mats, 1), NT) + dwn[8:16, :64]
+    down = dot_pair(down, own_matrix(mats, 0), NT) + dwn[16:24, :64]
 
     dn[240:248, :] = down + cpl[240:248, :64]
     n = 1
@@ -429,8 +490,11 @@
     vt, pt, send_a, send_b, send_c = call(
         gather_kernel,
         [((8, COLS), bf16), ((8, COLS), bf16), ((16, HALO), bf16), ((8, HALO), bf16), ((8, LOCAL), bf16)],
-        [pltpu.VMEM((256, 256), bf16), pltpu.VMEM((128, 256), f32)],
-        (points, vectors, leaf_order),
+        [
+            pltpu.VMEM((3, COLS), bf16), pltpu.VMEM((8, COLS), bf16), pltpu.VMEM((1, COLS), i32),
+            pltpu.VMEM((256, 256), bf16), pltpu.VMEM((128, 256), f32), pltpu.SemaphoreType.DMA((3,)),
+        ],
+        (points, vectors, leaf_order), "hhh>vvvvv",
         2 * 384 * 256 * COLS, 1 << 20,
     )
     pairs_a, pairs_b, pairs_c = [], [], []
@@ -444,18 +508,18 @@
     rec_b = lax.ppermute(send_b, axes, pairs_b)
     ut = jnp.transpose(up_transfer, (1, 2, 0))
     uc = jnp.transpose(up_coupling, (1, 2, 0))
-    et, eu = call(
+    (mats,) = call(
         matrices_kernel,
-        [((64 * T_ROWS, 128), f32), ((64 * C_ROWS, 128), f32)],
-        [],
-        (ut, uc),
+        [((64 * MATRICES, 64), bf16)],
+        [pltpu.VMEM((64 * T_ROWS, 128), f32), pltpu.VMEM((64 * C_ROWS, 128), f32)],
+        (ut, uc), "vv>v",
         2 * 8192 * 256 * 48, 8 << 20,
     )
     cf, path = call(
         coeff_kernel,
         [((256, 128), f32), ((32, 64), f32)],
         [],
-        (vt, leaf_bases, transfers, et),
+        (vt, leaf_bases, transfers, mats), "vvvv>vv",
         2 * 512 * 512 * 256, 2 << 20,
     )
     (send,) = call(
@@ -466,27 +530,36 @@
             cf, path, jnp.transpose(coupling_blocks, (1, 2, 0)),
             block_source.reshape(1, -1), block_owner.reshape(1, -1), block_target.reshape(1, -1),
             rec_a, rec_b, rec_c,
-        ),
+        ), "vvvvvvaaa>v",
         2 * 512 * 256 * 640, 4 << 20,
-        anywhere=3,
     )
     near_groups = [[xy * 8 + z for z in range(8)] for xy in range(peers // 8)]
     far_groups = [[xy * 8 + z for xy in range(peers // 8)] for z in range(8)]
     recv = lax.all_to_all(
         send, "leaf", split_axis=0, concat_axis=0, tiled=True, axis_index_groups=far_groups
     )
-    vw, fs, ft, begun = call(
-        near_setup_kernel,
-        [((16, 6144), bf16), ((6144, 16), bf16), ((16, 6144), bf16), ((16, HALF), f32)],
-        [pltpu.VMEM((8, 6144), f32)],
-        (vt, pt, rec_a, rec_b, rec_c),
+    buffers = [
+        pltpu.VMEM((8, COLS), bf16), pltpu.VMEM((8, COLS), bf16), pltpu.VMEM((16, HALO), bf16),
+        pltpu.VMEM((8, HALO), bf16), pltpu.VMEM((8, LOCAL), bf16),
+        pltpu.VMEM((16, 6144), bf16), pltpu.VMEM((6144, 16), bf16), pltpu.VMEM((16, 6144), bf16),
+        pltpu.VMEM((8, 6144), f32), pltpu.VMEM((16, HALF), f32), pltpu.SemaphoreType.DMA((5,)),
+    ]
+    (begun,) = call(
+        near_first_kernel,
+        [((16, HALF), f32)],
+        buffers + [pltpu.SemaphoreType.DMA((4,))],
+        (vt, pt, rec_a, rec_b, rec_c), "aaaaa>h",
         2 * 40 * 512 * 512 * 256, 1 << 20, vmem=24,
     )
     (send,) = call(
         middle_kernel,
         [((256, 512), bf16)],
-        [pltpu.VMEM((512, 128), f32), pltpu.VMEM((256, 64), f32), pltpu.VMEM((56, 64), f32)],
-        (recv, path, et, eu),
+        [
+            pltpu.VMEM((512, 640), bf16), pltpu.VMEM((32, 64), f32),
+            pltpu.VMEM((64 * MATRICES, 64), bf16), pltpu.VMEM((512, 128), f32),
+            pltpu.VMEM((256, 64), f32), pltpu.VMEM((56, 64), f32), pltpu.SemaphoreType.DMA((3,)),
+        ],
+        (recv, path, mats), "aaa>v",
         2 * 256 * 512 * 512, 2 << 20,
     )
     recv = lax.all_to_all(
@@ -495,8 +568,8 @@
     near_mine, near_send = call(
         near_rest_kernel,
         [((8, HALF), f32), ((8, HALF), f32)],
-        [pltpu.VMEM((16, HALF), f32)],
-        (vw, fs, ft, begun),
+        buffers + [pltpu.SemaphoreType.DMA(())],
+        (vt, pt, rec_a, rec_b, rec_c, begun), "aaaaah>vv",
         2 * 27 * 512 * 512 * 256, 1 << 20, vmem=24,
     )
     near_other = lax.ppermute(near_send, axes, pairs_c)
@@ -504,10 +577,12 @@
         final_kernel,
         [((8, COLS), bf16)],
         [
+            pltpu.VMEM((256, 512), bf16), pltpu.VMEM((8, HALF), f32), pltpu.VMEM((8, HALF), f32),
+            pltpu.VMEM((128, 64), bf16), pltpu.VMEM((1, COLS), i32),
             pltpu.VMEM((256, 128), f32), pltpu.VMEM((64, 128), f32),
-            pltpu.VMEM((248, 64), f32), pltpu.VMEM((8, COLS), f32),
+            pltpu.VMEM((248, 64), f32), pltpu.VMEM((8, COLS), f32), pltpu.SemaphoreType.DMA((5,)),
         ],
-        (recv, near_mine, near_other, et, transfers, leaf_bases, leaf_order),
+        (recv, near_mine, near_other, mats, transfers, leaf_bases, leaf_order), "aaaavvh>v",
         2 * 256 * 256 * COLS, 8 << 20,
     )
     return out

time: 70.4 us -> 68 us (0.966)
  local copies, waits for them, and re-layouts: 17 us -> 4.61 us
  waiting for transfers between devices: 3.32 us -> 10 us
  Pallas kernels: 25.6 us -> 29.1 us
    unnamed x64 -> x28, local copies, waits for them, and re-layouts: 17 us -> 4.61 us
    all_to_all x2, waiting for transfers between devices: 0.44 us -> 6.72 us  [shards(): lax.all_to_all(send, 'leaf', split_axis=0, concat_axis=0, tiled=True, axi...]
    pallas_call x8, Pallas kernels: 25.6 us -> 29.1 us  [call(): pl.pallas_call(kernel, out_shape=[jax.ShapeDtypeStruct(s, d) for s, d in...]
  transfers between devices with their start and end apart: 6 -> 6, of which waited for: 3 -> 4; matrix products, arithmetic and copies ran while one was open for 0% -> 0% of each run, Pallas kernels for 18% -> 22%
where the time goes in v3:
time: 68 us; the launch traced here: 67.6 us
  Pallas kernels  29.1 us (43%)
  starting transfers between devices  23.5 us (35%)
  waiting for transfers between devices  10 us (15%)
  local copies, waits for them, and re-layouts  4.61 us (7%)
    pallas_call x8, Pallas kernels, call(): pl.pallas_call(kernel, out_shape=[jax.ShapeDtypeStruct(s, d) for s, d in...  29.1 us
    all_to_all x2, starting transfers between devices, shards(): lax.all_to_all(send, 'leaf', split_axis=0, concat_axis=0, tiled=True, axi...  13.6 us
    ppermute x1, starting transfers between devices, shards(): rec_a = lax.ppermute(send_a, axes, pairs_a)  7.75 us
    all_to_all x2, waiting for transfers between devices, shards(): lax.all_to_all(send, 'leaf', split_axis=0, concat_axis=0, tiled=True, axi...  6.72 us
    unnamed x28, local copies, waits for them, and re-layouts  4.61 us
    ppermute x1, waiting for transfers between devices, shards(): rec_b = lax.ppermute(send_b, axes, pairs_b)  1.94 us
    ppermute x1, starting transfers between devices, shards(): rec_b = lax.ppermute(send_b, axes, pairs_b)  1.92 us
  transfers between devices with their start and end apart: 6, of which 4 were waited for; matrix products, arithmetic and copies ran while one was open for 0% of the time, Pallas kernels for 22%

profile of v3, /device:TPU:8, one launch (start us, length us, event | category | flops | bytes accessed | tf_op | source)
XLA Modules:
  0.0 67.6 jit_solution(10338308428288913964)
XLA Ops:
  0.0 1.0 %copy-done.8 = bf16[8,8192]{1,0:T(8,128)(2,1)S(1)} copy-done((bf16[8,8192]{1,0:T(8,128)(2,1)S(1)}, bf16[8,8192]{1,0:T(8,128)(2,1)}, u32[]{:S(2)}) %copy-start.8) | copy-done | bytes 131096
  1.1 1.1 %copy-done.9 = bf16[3,8192]{1,0:T(4,128)(2,1)S(1)} copy-done((bf16[3,8192]{1,0:T(4,128)(2,1)S(1)}, bf16[3,8192]{1,0:T(4,128)(2,1)}, u32[]{:S(2)}) %copy-start.9) | copy-done | bytes 49176
  2.2 0.8 %copy-done.10 = s32[1,8192]{1,0:T(1,128)S(1)} copy-done((s32[1,8192]{1,0:T(1,128)S(1)}, s32[1,8192]{1,0:T(1,128)}, u32[]{:S(2)}) %copy-start.10) | copy-done | bytes 32792
  2.9 3.3 %shard_map.109 = (bf16[8,8192]{1,0:T(8,128)(2,1)S(1)}, bf16[8,8192]{1,0:T(8,128)(2,1)S(1)}, bf16[16,1024]{1,0:T(8,128)(2,1)S(1)}, bf16[8,1024]{1,0:T(8,128)(2,1)S(1)}, bf16[8,5120]{1,0:T(8,128)(2,1)S(1)}) custom-call(bf16[3,8192]{1,0:T(4,128)(2,1)S(1)} %copy-done.9, bf16[8,8192]{1,0:T(8,128)(2,1)S(1)} %copy-done.8, s32[1,8192]{1,0:T(1,128)S(1)} %copy-done.10), custom_call_target="tpu_custom_call" | custom-call | flops 1610612736 | bytes 1048576 | tf_op jit(solution)/shard_map/pallas_call | solution.py:59
  6.2 0.1 collective-permute-start.2
  6.3 7.7 %collective-permute-start = (bf16[16,1024]{1,0:T(8,128)(2,1)S(1)}, bf16[16,1024]{1,0:T(8,128)(2,1)S(1)}, u32[]{:S(2)}, u32[]{:S(2)}) collective-permute-start(bf16[16,1024]{1,0:T(8,128)(2,1)S(1)} %get-tuple-element.17), channel_id=1, source_target_pairs={{1,2},{2,1},{3,4},{4,3},{5,6},{6,5},{7,8},{8,7},{9,10},{10,9},{11,... | collective-permute-start | bytes 98312 | tf_op jit(solution)/shard_map/ppermute | solution.py:507
  14.0 1.9 %collective-permute-start.1 = (bf16[8,1024]{1,0:T(8,128)(2,1)S(1)}, bf16[8,1024]{1,0:T(8,128)(2,1)S(1)}, u32[]{:S(2)}, u32[]{:S(2)}) collective-permute-start(bf16[8,1024]{1,0:T(8,128)(2,1)S(1)} %get-tuple-element.18), channel_id=1, source_target_pairs={{0,2},{3,1},{2,4},{5,3},{4,6},{7,5},{6,8},{9,7},{8,10},{11,9},{10,... | collective-permute-start | bytes 49160 | tf_op jit(solution)/shard_map/ppermute | solution.py:508
  16.0 0.0 copy-start.3
  16.0 2.2 %shard_map.110.mats.mats_in = bf16[3072,64]{1,0:T(8,128)(2,1)S(1)} custom-call(bf16[64,64,254]{2,1,0:T(8,128)(2,1)S(1)} %bitcast.12, bf16[64,64,254]{2,1,0:T(8,128)(2,1)S(1)} %bitcast.13), custom_call_target="tpu_custom_call" | custom-call | flops 201326592 | bytes 8388608 | tf_op jit(solution)/shard_map/pallas_call | solution.py:59
  18.3 1.5 %shard_map.111 = (f32[256,128]{1,0:T(8,128)S(1)}, f32[32,64]{1,0:T(8,128)S(1)}) custom-call(bf16[8,8192]{1,0:T(8,128)(2,1)S(1)} %get-tuple-element.14.vt.refs_0_, bf16[16,64,512]{2,1,0:T(8,128)(2,1)S(1)} %copy-done.3, bf16[30,64,64]{2,1,0:T(8,128)(2,1)S(1)} %copy-done.4, bf16[3072,64]{1,0:T(8,128)(2,1)S(1)} %shard_map.110.mats.mats_in), custom_call_target="tpu_custom_call" | custom-call | flops 134217728 | bytes 2097152 | tf_op jit(solution)/shard_map/pallas_call | solution.py:59
  19.8 1.9 %collective-permute-done.1.seen_b.refs_3_ = bf16[8,1024]{1,0:T(8,128)(2,1)S(1)} collective-permute-done((bf16[8,1024]{1,0:T(8,128)(2,1)S(1)}, bf16[8,1024]{1,0:T(8,128)(2,1)S(1)}, u32[]{:S(2)}, u32[]{:S(2)}) %collective-permute-start.1) | collective-permute-done | bytes 16416 | tf_op jit(solution)/shard_map/ppermute | solution.py:508
  21.8 4.3 %shard_map.112 = bf16[512,640]{1,0:T(8,128)(2,1)} custom-call(f32[256,128]{1,0:T(8,128)S(1)} %get-tuple-element.15.cf, f32[32,64]{1,0:T(8,128)S(1)} %get-tuple-element.16.path.path_in, bf16[64,64,256]{2,1,0:T(8,128)(2,1)S(1)} %bitcast.11, s32[1,256]{1,0:T(1,128)S(1)} %bitcast.15, s32[1,256]{1,0:T(1,128)S(1)} %bitcast.16, s32[1,256]{1,0:T(1,128)S(1)} %bitcast.17, ...), custom_call_target="tpu_custom_call" | custom-call | flops 167772160 | bytes 4194304 | tf_op jit(solution)/shard_map/pallas_call | solution.py:59
  26.1 9.4 %all-to-all-start = ((bf16[16,32,640]{2,1,0:T(8,128)(2,1)}), bf16[16,32,640]{2,1,0:T(8,128)(2,1)S(1)}, u32[]{:S(2)}, u32[]{:S(2)}) async-start(bf16[16,32,640]{2,1,0:T(8,128)(2,1)} %bitcast.6), calls=%async_computation | async-start | bytes 1310720 | tf_op jit(solution)/shard_map/all_to_all | solution.py:538
  35.5 6.3 %shard_map.114.refs_5_ = f32[16,4096]{1,0:T(8,128)S(1)} custom-call(bf16[8,8192]{1,0:T(8,128)(2,1)S(1)} %get-tuple-element.14.vt.refs_0_, bf16[8,8192]{1,0:T(8,128)(2,1)S(1)} %get-tuple-element.20.refs_1_, bf16[16,1024]{1,0:T(8,128)(2,1)S(1)} %collective-permute-done.seen_a.refs_2_, bf16[8,1024]{1,0:T(8,128)(2,1)S(1)} %collective-permute-done.1.seen_b.refs_3_, ...), custom_call_target="tpu_custom_call" | custom-call | flops 5368709120 | bytes 1048576 | tf_op jit(solution)/shard_map/pallas_call | solution.py:59
  41.8 0.7 %copy-done.12 = f32[16,4096]{1,0:T(8,128)} copy-done((f32[16,4096]{1,0:T(8,128)}, f32[16,4096]{1,0:T(8,128)S(1)}, u32[]{:S(2)}) %copy-start.12) | copy-done | bytes 262168
  42.5 2.5 %all-to-all-done = bf16[16,32,640]{2,1,0:T(8,128)(2,1)S(1)} async-done(((bf16[16,32,640]{2,1,0:T(8,128)(2,1)}), bf16[16,32,640]{2,1,0:T(8,128)(2,1)S(1)}, u32[]{:S(2)}, u32[]{:S(2)}) %all-to-all-start) | async-done | bytes 655392 | tf_op jit(solution)/shard_map/all_to_all | solution.py:538
  45.0 2.8 %shard_map.113 = bf16[256,512]{1,0:T(8,128)(2,1)} custom-call(bf16[512,640]{1,0:T(8,128)(2,1)S(1)} %bitcast.10, f32[32,64]{1,0:T(8,128)S(1)} %get-tuple-element.16.path.path_in, bf16[3072,64]{1,0:T(8,128)(2,1)S(1)} %shard_map.110.mats.mats_in), custom_call_target="tpu_custom_call" | custom-call | flops 134217728 | bytes 2097152 | tf_op jit(solution)/shard_map/pallas_call | solution.py:59
  47.8 4.2 %all-to-all-start.1 = ((bf16[8,32,512]{2,1,0:T(8,128)(2,1)}), bf16[8,32,512]{2,1,0:T(8,128)(2,1)S(1)}, u32[]{:S(2)}, u32[]{:S(2)}) async-start(bf16[8,32,512]{2,1,0:T(8,128)(2,1)} %bitcast.8), calls=%async_computation.1 | async-start | bytes 524288 | tf_op jit(solution)/shard_map/all_to_all | solution.py:565
  52.0 0.9 %copy-done.13 = f32[16,4096]{1,0:T(8,128)S(1)} copy-done((f32[16,4096]{1,0:T(8,128)S(1)}, f32[16,4096]{1,0:T(8,128)}, u32[]{:S(2)}) %copy-start.13) | copy-done | bytes 262168
  52.9 4.9 %shard_map.115 = (f32[8,4096]{1,0:T(8,128)S(1)}, f32[8,4096]{1,0:T(8,128)S(1)}) custom-call(bf16[8,8192]{1,0:T(8,128)(2,1)S(1)} %get-tuple-element.14.vt.refs_0_, bf16[8,8192]{1,0:T(8,128)(2,1)S(1)} %get-tuple-element.20.refs_1_, bf16[16,1024]{1,0:T(8,128)(2,1)S(1)} %collective-permute-done.seen_a.refs_2_, ...), custom_call_target="tpu_custom_call" | custom-call | flops 3623878656 | bytes 1048576 | tf_op jit(solution)/shard_map/pallas_call | solution.py:59
  57.9 0.1 collective-permute-start.3
  58.0 1.3 %collective-permute-done.3.other_in = f32[8,4096]{1,0:T(8,128)S(1)} collective-permute-done((f32[8,4096]{1,0:T(8,128)S(1)}, f32[8,4096]{1,0:T(8,128)S(1)}, u32[]{:S(2)}, u32[]{:S(2)}) %collective-permute-start.3) | collective-permute-done | bytes 131104 | tf_op jit(solution)/shard_map/ppermute | solution.py:575
  59.3 4.3 %all-to-all-done.1 = bf16[8,32,512]{2,1,0:T(8,128)(2,1)S(1)} async-done(((bf16[8,32,512]{2,1,0:T(8,128)(2,1)}), bf16[8,32,512]{2,1,0:T(8,128)(2,1)S(1)}, u32[]{:S(2)}, u32[]{:S(2)}) %all-to-all-start.1) | async-done | bytes 262176 | tf_op jit(solution)/shard_map/all_to_all | solution.py:565
  63.6 3.8 %shard_map.116 = bf16[8,8192]{1,0:T(8,128)(2,1)} custom-call(bf16[256,512]{1,0:T(8,128)(2,1)S(1)} %bitcast.14, f32[8,4096]{1,0:T(8,128)S(1)} %get-tuple-element.21.mine_in, f32[8,4096]{1,0:T(8,128)S(1)} %collective-permute-done.3.other_in, bf16[3072,64]{1,0:T(8,128)(2,1)S(1)} %shard_map.110.mats.mats_in, bf16[30,64,64]{2,1,0:T(8,128)(2,1)S(1)} %copy-done.4, ...), custom_call_target="tpu_custom_call" | custom-call | flops 1073741824 | bytes 8388608 | tf_op jit(solution)/shard_map/pallas_call | solution.py:59
  (24 shorter events, 0.1 us)
Async XLA Ops:
  0.0 16.0 %copy-start.2 = (bf16[254,64,64]{0,2,1:T(8,128)(2,1)S(1)}, bf16[254,64,64]{0,2,1:T(8,128)(2,1)}, u32[]{:S(2)}) copy-start(bf16[254,64,64]{0,2,1:T(8,128)(2,1)} %param.21) | copy-start | bytes 6242308
  0.0 16.0 %copy-start.1 = (bf16[254,64,64]{0,2,1:T(8,128)(2,1)S(1)}, bf16[254,64,64]{0,2,1:T(8,128)(2,1)}, u32[]{:S(2)}) copy-start(bf16[254,64,64]{0,2,1:T(8,128)(2,1)} %param.20) | copy-start | bytes 6242308
  0.0 1.1 %copy-start.8 = (bf16[8,8192]{1,0:T(8,128)(2,1)S(1)}, bf16[8,8192]{1,0:T(8,128)(2,1)}, u32[]{:S(2)}) copy-start(bf16[8,8192]{1,0:T(8,128)(2,1)} %vec_in.1) | copy-start | bytes 393220
  1.1 1.1 %copy-start.9 = (bf16[3,8192]{1,0:T(4,128)(2,1)S(1)}, bf16[3,8192]{1,0:T(4,128)(2,1)}, u32[]{:S(2)}) copy-start(bf16[3,8192]{1,0:T(4,128)(2,1)} %pts_in.1) | copy-start | bytes 147460
  2.2 0.8 %copy-start.10 = (s32[1,8192]{1,0:T(1,128)S(1)}, s32[1,8192]{1,0:T(1,128)}, u32[]{:S(2)}) copy-start(s32[1,8192]{1,0:T(1,128)} %perm_in.3) | copy-start | bytes 98308
  6.2 15.6 %collective-permute-start.2 = (bf16[8,5120]{1,0:T(8,128)(2,1)S(1)}, bf16[8,5120]{1,0:T(8,128)(2,1)S(1)}, u32[]{:S(2)}, u32[]{:S(2)}) collective-permute-start(bf16[8,5120]{1,0:T(8,128)(2,1)S(1)} %get-tuple-element.19), channel_id=1, source_target_pairs={{0,1},{1,0},{2,3},{3,2},{4,5},{5,4},{6,7},{7,6},{8,9},{9,8},{10,11... | collective-permute-start | bytes 245768 | tf_op jit(solution)/shard_map/ppermute | solution.py:506
  6.3 15.5 %collective-permute-start = (bf16[16,1024]{1,0:T(8,128)(2,1)S(1)}, bf16[16,1024]{1,0:T(8,128)(2,1)S(1)}, u32[]{:S(2)}, u32[]{:S(2)}) collective-permute-start(bf16[16,1024]{1,0:T(8,128)(2,1)S(1)} %get-tuple-element.17), channel_id=1, source_target_pairs={{1,2},{2,1},{3,4},{4,3},{5,6},{6,5},{7,8},{8,7},{9,10},{10,9},{11,... | collective-permute-start | bytes 98312 | tf_op jit(solution)/shard_map/ppermute | solution.py:507
  14.0 7.7 %collective-permute-start.1 = (bf16[8,1024]{1,0:T(8,128)(2,1)S(1)}, bf16[8,1024]{1,0:T(8,128)(2,1)S(1)}, u32[]{:S(2)}, u32[]{:S(2)}) collective-permute-start(bf16[8,1024]{1,0:T(8,128)(2,1)S(1)} %get-tuple-element.18), channel_id=1, source_target_pairs={{0,2},{3,1},{2,4},{5,3},{4,6},{7,5},{6,8},{9,7},{8,10},{11,9},{10,... | collective-permute-start | bytes 49160 | tf_op jit(solution)/shard_map/ppermute | solution.py:508
  16.0 2.3 %copy-start.3 = (bf16[16,64,512]{2,1,0:T(8,128)(2,1)S(1)}, bf16[16,64,512]{2,1,0:T(8,128)(2,1)}, u32[]{:S(2)}) copy-start(bf16[16,64,512]{2,1,0:T(8,128)(2,1)} %bases.3) | copy-start | bytes 3145732
  16.0 2.3 %copy-start.4 = (bf16[30,64,64]{2,1,0:T(8,128)(2,1)S(1)}, bf16[30,64,64]{2,1,0:T(8,128)(2,1)}, u32[]{:S(2)}) copy-start(bf16[30,64,64]{2,1,0:T(8,128)(2,1)} %tr.3) | copy-start | bytes 737284
  18.3 3.5 %copy-start = (bf16[256,64,64]{0,2,1:T(8,128)(2,1)S(1)}, bf16[256,64,64]{0,2,1:T(8,128)(2,1)}, u32[]{:S(2)}) copy-start(bf16[256,64,64]{0,2,1:T(8,128)(2,1)} %param.16) | copy-start | bytes 6291460
  18.3 3.5 %copy-start.5 = (s32[256]{0:T(256)S(1)}, s32[256]{0:T(256)}, u32[]{:S(2)}) copy-start(s32[256]{0:T(256)} %param.17) | copy-start | bytes 3076
  18.3 3.5 %copy-start.6 = (s32[256,1]{0,1:T(1,128)S(1)}, s32[256,1]{0,1:T(1,128)}, u32[]{:S(2)}) copy-start(s32[256,1]{0,1:T(1,128)} %param.18) | copy-start | bytes 3076
  18.3 3.5 %copy-start.7 = (s32[256]{0:T(256)S(1)}, s32[256]{0:T(256)}, u32[]{:S(2)}) copy-start(s32[256]{0:T(256)} %param.19) | copy-start | bytes 3076
  26.1 18.9 %all-to-all-start = ((bf16[16,32,640]{2,1,0:T(8,128)(2,1)}), bf16[16,32,640]{2,1,0:T(8,128)(2,1)S(1)}, u32[]{:S(2)}, u32[]{:S(2)}) async-start(bf16[16,32,640]{2,1,0:T(8,128)(2,1)} %bitcast.6), calls=%async_computation | async-start | bytes 1310720 | tf_op jit(solution)/shard_map/all_to_all | solution.py:538
  41.8 0.7 %copy-start.12 = (f32[16,4096]{1,0:T(8,128)}, f32[16,4096]{1,0:T(8,128)S(1)}, u32[]{:S(2)}) copy-start(f32[16,4096]{1,0:T(8,128)S(1)} %shard_map.114.refs_5_) | copy-start | bytes 786436
  47.8 15.8 %all-to-all-start.1 = ((bf16[8,32,512]{2,1,0:T(8,128)(2,1)}), bf16[8,32,512]{2,1,0:T(8,128)(2,1)S(1)}, u32[]{:S(2)}, u32[]{:S(2)}) async-start(bf16[8,32,512]{2,1,0:T(8,128)(2,1)} %bitcast.8), calls=%async_computation.1 | async-start | bytes 524288 | tf_op jit(solution)/shard_map/all_to_all | solution.py:565
  52.0 0.9 %copy-start.13 = (f32[16,4096]{1,0:T(8,128)S(1)}, f32[16,4096]{1,0:T(8,128)}, u32[]{:S(2)}) copy-start(f32[16,4096]{1,0:T(8,128)} %copy-done.12) | copy-start | bytes 786436
  52.9 10.6 %copy-start.11 = (s32[1,8192]{1,0:T(1,128)S(1)}, s32[1,8192]{1,0:T(1,128)}, u32[]{:S(2)}) copy-start(s32[1,8192]{1,0:T(1,128)} %perm_in.3) | copy-start | bytes 98308
  57.9 1.4 %collective-permute-start.3 = (f32[8,4096]{1,0:T(8,128)S(1)}, f32[8,4096]{1,0:T(8,128)S(1)}, u32[]{:S(2)}, u32[]{:S(2)}) collective-permute-start(f32[8,4096]{1,0:T(8,128)S(1)} %get-tuple-element.22), channel_id=1, source_target_pairs={{0,1},{1,0},{2,3},{3,2},{4,5},{5,4},{6,7},{7,6},{8,9},{9,8},{10,11... | collective-permute-start | bytes 393224 | tf_op jit(solution)/shard_map/ppermute | solution.py:575

commit v4 on v3

--- a/solution.py
+++ b/solution.py
@@ -155,7 +155,11 @@
     return mats[64 * row : 64 * (row + count), :]
 
 
-def product_kernel(cf, path, cp, bsrc, bown, btgt, seen_a, seen_b, seen_c, send, pick, prod):
+def product_kernel(
+    cf, path, cp, bsrc, bown, btgt, halo_a, halo_b, seen_c, send, send_a, send_b, pick, prod
+):
+    send_a[...] = halo_a[...]
+    send_b[...] = halo_b[...]
     source = hot(iota((32, 256), 0) == bsrc[...])
     for v in range(8):
         mine = cf[pl.ds(v, 32, stride=8), :][:, :64].astype(bf16)
@@ -208,32 +212,33 @@
     return a, b, x - a - b
 
 
-def near_window(ins, bufs, sems, leaves, vw, fs, ft, pw):
+def leaf_cols(leaf):
+    return slice(LEAF * leaf, LEAF * leaf + LEAF)
+
+
+def load_window(vt, pt, rec_c, halo, leaves, vw, pw):
     core = lax.axis_index("vec")
-    for copy in fetch(sems, *zip(ins, bufs)):
-        copy.wait()
-    vt, pt, rec_a, rec_b, rec_c = bufs
-
-    @pl.when(core == 0)
-    def _():
-        vw[0:8, HALO:] = vt[:, :LOCAL]
-        vw[8:16, HALO:] = rec_c[...]
-        vw[0:8, :HALO] = rec_b[...]
-        vw[8:16, :HALO] = rec_a[0:8, :]
-        pw[:, HALO:] = pt[:, :LOCAL].astype(f32)
-        pw[:, :HALO] = rec_a[8:16, :].astype(f32)
-
-    @pl.when(core == 1)
-    def _():
-        vw[0:8, :LOCAL] = vt[:, COLS - LOCAL :]
-        vw[8:16, :LOCAL] = rec_c[...]
-        vw[0:8, LOCAL:] = rec_b[...]
-        vw[8:16, LOCAL:] = rec_a[0:8, :]
-        pw[:, :LOCAL] = pt[:, COLS - LOCAL :].astype(f32)
-        pw[:, LOCAL:] = rec_a[8:16, :].astype(f32)
-
+    for which in range(2):
+
+        @pl.when(core == which)
+        def _():
+            for w in leaves:
+                to = leaf_cols(w)
+                if w < 2:
+                    near_cols = leaf_cols(w if which == 0 else 1 - w)
+                    vw[0:8, to] = halo[1][:, near_cols]
+                    vw[8:16, to] = halo[0][0:8, near_cols]
+                    pw[:, to] = halo[0][8:16, near_cols].astype(f32)
+                else:
+                    local = leaf_cols(w - 2 if which == 0 else 17 - w)
+                    vw[0:8, to] = vt[:, local]
+                    vw[8:16, to] = rec_c[:, leaf_cols(w - 2 if which == 0 else 11 - w)]
+                    pw[:, to] = pt[:, local].astype(f32)
+
+
+def features(leaves, pw, fs, ft):
     for leaf in leaves:
-        cols = slice(LEAF * leaf, LEAF * leaf + LEAF)
+        cols = leaf_cols(leaf)
         p = pw[0:3, cols]
         norm = p[0:1] * p[0:1] + p[1:2] * p[1:2] + p[2:3] * p[2:3]
         parts = jnp.concatenate(split3(norm), axis=0)
@@ -248,47 +253,66 @@
 
 
 def near_target(t, vw, fs, ft, acc):
-    tc = slice(LEAF * t, LEAF * t + LEAF)
-    to = slice(LEAF * (t - 2), LEAF * (t - 1))
+    tc = leaf_cols(t)
     total = jnp.zeros((16, LEAF), f32)
     for s in range(t - 2, t + 3):
         if 2 <= s < t:
             continue
-        sc = slice(LEAF * s, LEAF * s + LEAF)
+        sc = leaf_cols(s)
         kernel = lax.rsqrt(dot(fs[sc, :], ft[:, tc])).astype(bf16)
         total = total + dot(vw[:, sc], kernel)
         if t < s < 10:
-            so = slice(LEAF * (s - 2), LEAF * (s - 1))
-            acc[:, so] += dot(vw[:, tc], kernel, NT)
-    acc[:, to] += total
-
-
-def near_first_kernel(*refs):
-    ins, begun, bufs = refs[:5], refs[5], refs[6:11]
-    vw, fs, ft, pw, acc, sems, out_sems = refs[11:]
-    near_window(ins, bufs, sems, range(0, 8), vw, fs, ft, pw)
+            acc[:, leaf_cols(s - 2)] += dot(vw[:, tc], kernel, NT)
+    acc[:, leaf_cols(t - 2)] += total
+
+
+SPLIT = 5
+
+
+def near_first_kernel(
+    vt_in, pt_in, c_in, begun, vt, pt, rec_c, vw, fs, ft, pw, acc, sems, out_sems
+):
+    for copy in fetch(sems, (vt_in, vt), (pt_in, pt), (c_in, rec_c)):
+        copy.wait()
+    load_window(vt, pt, rec_c, None, range(SPLIT, 12), vw, pw)
+    features(range(SPLIT, 12), pw, fs, ft)
     acc[...] = jnp.zeros_like(acc)
     copies = []
-    for t in range(2, 6):
+    for t in range(SPLIT, 10):
         near_target(t, vw, fs, ft, acc)
-        cols = slice(LEAF * (t - 2), LEAF * (t - 1) if t < 5 else HALF)
-        copies += [pltpu.make_async_copy(acc.at[:, cols], begun.at[:, cols], out_sems.at[t - 2])]
+        src, dst = acc.at[:, leaf_cols(t - 2)], begun.at[:, leaf_cols(t - SPLIT)]
+        copies += [pltpu.make_async_copy(src, dst, out_sems.at[t - SPLIT])]
         copies[-1].start()
     for copy in copies:
         copy.wait()
 
 
-def near_rest_kernel(*refs):
-    ins, begun, mine, other, bufs = refs[:5], refs[5], refs[6], refs[7], refs[8:13]
-    vw, fs, ft, pw, acc, sems, begun_sem = refs[13:]
-    first = pltpu.make_async_copy(begun, acc, begun_sem)
-    first.start()
-    near_window(ins, bufs, sems, range(6, 12), vw, fs, ft, pw)
-    first.wait()
-    for t in range(6, 10):
+def near_rest_kernel(
+    vt_in, pt_in, c_in, a_in, b_in, begun, mine, other,
+    vt, pt, rec_c, vw, fs, ft, pw, acc, sems, rec_a, rec_b,
+):
+    left = LEAF * (SPLIT - 2)
+    copies = fetch(
+        sems, (vt_in, vt), (pt_in, pt), (c_in, rec_c), (a_in, rec_a), (b_in, rec_b),
+        (begun, acc.at[:, left:]),
+    )
+    acc[:, :left] = jnp.zeros((16, left), f32)
+    for copy in copies[:5]:
+        copy.wait()
+    load_window(vt, pt, rec_c, (rec_a, rec_b), range(0, SPLIT + 2), vw, pw)
+    features(range(0, SPLIT + 2), pw, fs, ft)
+    copies[5].wait()
+    for t in range(2, SPLIT):
         near_target(t, vw, fs, ft, acc)
-    mine[...] = acc[0:8, :] * (8.0 / LEAF)
-    other[...] = acc[8:16, :] * (8.0 / LEAF)
+    core = lax.axis_index("vec")
+    for which in range(2):
+
+        @pl.when(core == which)
+        def _():
+            for i in range(8):
+                to = leaf_cols(i if which == 0 else 7 - i)
+                mine[:, to] = acc[0:8, leaf_cols(i)] * (8.0 / LEAF)
+                other[:, to] = acc[8:16, leaf_cols(i)] * (8.0 / LEAF)
 
 
 LEVEL_START = [256 - (256 >> u) for u in range(7)]
@@ -296,52 +320,55 @@
 OWN = 30
 SIBLING = 33
 OWN_UPPER = 36
-COUPLING = 40
-MATRICES = 48
 T_ROWS = 40
 C_ROWS = 8
 
 
-def matrices_kernel(ut, uc, mats, et, eu):
-    device = lax.axis_index("leaf")
-
-    def node(u, other=False):
-        n = lax.shift_right_logical(device, u)
-        return LEVEL_START[u] + (lax.bitwise_xor(n, 1) if other else n)
-
-    row, lane = iota((T_ROWS, 254), 0), iota((T_ROWS, 254), 1)
+def node(u, other=False):
+    n = lax.shift_right_logical(lax.axis_index("leaf"), u)
+    return LEVEL_START[u] + (lax.bitwise_xor(n, 1) if other else n)
+
+
+def pick_matrices(table, want, rows, count, mats, buf):
+    pick = hot(iota((rows, 254), 1) == want)
+
+    def step(g, carry):
+        out = dot(pick, table[pl.ds(4 * g, 4)].reshape(256, 254), NT)
+        for j in range(4):
+            at = pl.multiple_of((4 * g + j) * rows, 8)
+            buf[pl.ds(at, rows), :64] = out[:, 64 * j : 64 * j + 64]
+        return carry
+
+    lax.fori_loop(0, 16, step, 0, unroll=4)
+    for m in range(count):
+        mats[64 * m : 64 * m + 64, :] = buf[pl.ds(m, 64, stride=rows), :][:, :64].astype(bf16)
+
+
+def transfers_kernel(ut, mats, buf):
+    row = iota((T_ROWS, 254), 0)
     want = jnp.where(row < 30, row + UPPER, -1)
     for u in range(3):
         want = jnp.where(row == OWN + u, node(u), want)
         want = jnp.where(row == SIBLING + u, node(u, True), want)
         want = jnp.where(row == OWN_UPPER + u, node(u + 3), want)
-    pick_t = hot(lane == want)
-    row, lane = iota((C_ROWS, 254), 0), iota((C_ROWS, 254), 1)
+    pick_matrices(ut, want, T_ROWS, 39, mats, buf)
+
+
+def couplings_kernel(uc, seen, mats, buf):
+    row = iota((C_ROWS, 254), 0)
     want = jnp.zeros((C_ROWS, 254), i32) - 1
     for u in range(7):
         want = jnp.where(row == u, node(u, u < 3), want)
-    pick_c = hot(lane == want)
-
-    def step(g, carry):
-        for ref, pick, dest, rows in ((ut, pick_t, et, T_ROWS), (uc, pick_c, eu, C_ROWS)):
-            block = ref[pl.ds(4 * g, 4)].reshape(256, 254)
-            out = dot(pick, block, NT)
-            for j in range(4):
-                at = pl.multiple_of((4 * g + j) * rows, 8)
-                dest[pl.ds(at, rows), :64] = out[:, 64 * j : 64 * j + 64]
-        return carry
-
-    lax.fori_loop(0, 16, step, 0, unroll=4)
-    for m in range(39):
-        mats[64 * m : 64 * m + 64, :] = et[pl.ds(m, 64, stride=T_ROWS), :][:, :64].astype(bf16)
-    for m in range(7):
-        at = 64 * (COUPLING + m)
-        mats[at : at + 64, :] = eu[pl.ds(m, 64, stride=C_ROWS), :][:, :64].astype(bf16)
-
-
-def middle_kernel(recv_in, path_in, mats_in, send, recv, path, mats, ext, xs, gain, sems):
+    pick_matrices(uc, want, C_ROWS, 7, mats, buf)
+
+
+def middle_kernel(
+    recv_in, path_in, mats_in, coup_in, send, recv, path, mats, coup, ext, xs, gain, sems
+):
     device = lax.axis_index("leaf")
-    for copy in fetch(sems, (recv_in, recv), (path_in, path), (mats_in, mats)):
+    for copy in fetch(
+        sems, (recv_in, recv), (path_in, path), (mats_in, mats), (coup_in, coup)
+    ):
         copy.wait()
     ext[...] = recv[:, 512:640].astype(f32)
 
@@ -375,7 +402,7 @@
         else:
             sib = lax.bitwise_xor(lax.shift_right_logical(device, u), 1)
             partner = xs[pl.ds(pl.multiple_of((firsts[u] + sib) * 8, 8), 8), :]
-        gain[8 * u : 8 * u + 8, :] = dot_pair(partner, own_matrix(mats, COUPLING + u))
+        gain[8 * u : 8 * u + 8, :] = dot_pair(partner, own_matrix(coup, u))
     down = gain[48:56, :]
     for u in (5, 4, 3):
         w = own_matrix(mats, OWN_UPPER + u - 3)
@@ -504,16 +531,14 @@
             pairs_a += [(2 * d + 1, 2 * d + 2), (2 * d + 2, 2 * d + 1)]
             pairs_b += [(2 * d, 2 * d + 2), (2 * d + 3, 2 * d + 1)]
     rec_c = lax.ppermute(send_c, axes, pairs_c)
-    rec_a = lax.ppermute(send_a, axes, pairs_a)
-    rec_b = lax.ppermute(send_b, axes, pairs_b)
     ut = jnp.transpose(up_transfer, (1, 2, 0))
     uc = jnp.transpose(up_coupling, (1, 2, 0))
     (mats,) = call(
-        matrices_kernel,
-        [((64 * MATRICES, 64), bf16)],
-        [pltpu.VMEM((64 * T_ROWS, 128), f32), pltpu.VMEM((64 * C_ROWS, 128), f32)],
-        (ut, uc), "vv>v",
-        2 * 8192 * 256 * 48, 8 << 20,
+        transfers_kernel,
+        [((64 * T_ROWS, 64), bf16)],
+        [pltpu.VMEM((64 * T_ROWS, 128), f32)],
+        (ut,), "v>v",
+        2 * 4096 * 256 * 40, 3 << 20,
     )
     cf, path = call(
         coeff_kernel,
@@ -522,15 +547,15 @@
         (vt, leaf_bases, transfers, mats), "vvvv>vv",
         2 * 512 * 512 * 256, 2 << 20,
     )
-    (send,) = call(
+    send, send_a, send_b = call(
         product_kernel,
-        [((512, 640), bf16)],
+        [((512, 640), bf16), ((16, HALO), bf16), ((8, HALO), bf16)],
         [pltpu.VMEM((1024, 128), f32), pltpu.VMEM((640, 256), bf16)],
         (
             cf, path, jnp.transpose(coupling_blocks, (1, 2, 0)),
             block_source.reshape(1, -1), block_owner.reshape(1, -1), block_target.reshape(1, -1),
-            rec_a, rec_b, rec_c,
-        ), "vvvvvvaaa>v",
+            send_a, send_b, rec_c,
+        ), "vvvvvvvva>vvv",
         2 * 512 * 256 * 640, 4 << 20,
     )
     near_groups = [[xy * 8 + z for z in range(8)] for xy in range(peers // 8)]
@@ -538,28 +563,37 @@
     recv = lax.all_to_all(
         send, "leaf", split_axis=0, concat_axis=0, tiled=True, axis_index_groups=far_groups
     )
+    rec_a = lax.ppermute(send_a, axes, pairs_a)
+    rec_b = lax.ppermute(send_b, axes, pairs_b)
     buffers = [
-        pltpu.VMEM((8, COLS), bf16), pltpu.VMEM((8, COLS), bf16), pltpu.VMEM((16, HALO), bf16),
-        pltpu.VMEM((8, HALO), bf16), pltpu.VMEM((8, LOCAL), bf16),
+        pltpu.VMEM((8, COLS), bf16), pltpu.VMEM((8, COLS), bf16), pltpu.VMEM((8, LOCAL), bf16),
         pltpu.VMEM((16, 6144), bf16), pltpu.VMEM((6144, 16), bf16), pltpu.VMEM((16, 6144), bf16),
-        pltpu.VMEM((8, 6144), f32), pltpu.VMEM((16, HALF), f32), pltpu.SemaphoreType.DMA((5,)),
+        pltpu.VMEM((8, 6144), f32), pltpu.VMEM((16, HALF), f32), pltpu.SemaphoreType.DMA((6,)),
     ]
+    (coup,) = call(
+        couplings_kernel,
+        [((64 * C_ROWS, 64), bf16)],
+        [pltpu.VMEM((64 * C_ROWS, 128), f32)],
+        (uc, send), "va>v",
+        2 * 4096 * 256 * 8, 3 << 20,
+    )
     (begun,) = call(
         near_first_kernel,
-        [((16, HALF), f32)],
-        buffers + [pltpu.SemaphoreType.DMA((4,))],
-        (vt, pt, rec_a, rec_b, rec_c), "aaaaa>h",
-        2 * 40 * 512 * 512 * 256, 1 << 20, vmem=24,
+        [((16, LEAF * (10 - SPLIT)), f32)],
+        buffers + [pltpu.SemaphoreType.DMA((5,))],
+        (vt, pt, rec_c), "aaa>h",
+        2 * 37 * 512 * 512 * 256, 1 << 20, vmem=24,
     )
     (send,) = call(
         middle_kernel,
         [((256, 512), bf16)],
         [
             pltpu.VMEM((512, 640), bf16), pltpu.VMEM((32, 64), f32),
-            pltpu.VMEM((64 * MATRICES, 64), bf16), pltpu.VMEM((512, 128), f32),
-            pltpu.VMEM((256, 64), f32), pltpu.VMEM((56, 64), f32), pltpu.SemaphoreType.DMA((3,)),
+            pltpu.VMEM((64 * T_ROWS, 64), bf16), pltpu.VMEM((64 * C_ROWS, 64), bf16),
+            pltpu.VMEM((512, 128), f32), pltpu.VMEM((256, 64), f32), pltpu.VMEM((56, 64), f32),
+            pltpu.SemaphoreType.DMA((4,)),
         ],
-        (recv, path, mats), "aaa>v",
+        (recv, path, mats, coup), "aaaa>v",
         2 * 256 * 512 * 512, 2 << 20,
     )
     recv = lax.all_to_all(
@@ -568,9 +602,9 @@
     near_mine, near_send = call(
         near_rest_kernel,
         [((8, HALF), f32), ((8, HALF), f32)],
-        buffers + [pltpu.SemaphoreType.DMA(())],
-        (vt, pt, rec_a, rec_b, rec_c, begun), "aaaaah>vv",
-        2 * 27 * 512 * 512 * 256, 1 << 20, vmem=24,
+        buffers + [pltpu.VMEM((16, HALO), bf16), pltpu.VMEM((8, HALO), bf16)],
+        (vt, pt, rec_c, rec_a, rec_b, begun), "aaaaah>vv",
+        2 * 30 * 512 * 512 * 256, 1 << 20, vmem=24,
     )
     near_other = lax.ppermute(near_send, axes, pairs_c)
     (out,) = call(

time: 68 us -> 64.8 us (0.953); the launches traced: 67.6 us -> 63.7 us
  waiting for transfers between devices: 10 us -> 6.06 us
  Pallas kernels: 29.1 us -> 30.3 us
  starting transfers between devices: 23.5 us -> 22.7 us
    ppermute x1, waiting for transfers between devices: 1.94 us -> 0.01 us  [shards(): rec_b = lax.ppermute(send_b, axes, pairs_b)]
    all_to_all x2, waiting for transfers between devices: 6.72 us -> 5.07 us  [shards(): lax.all_to_all(send, 'leaf', split_axis=0, concat_axis=0, tiled=True, axi...]
    pallas_call x8 -> x9, Pallas kernels: 29.1 us -> 30.3 us  [call(): pl.pallas_call(kernel, out_shape=[jax.ShapeDtypeStruct(s, d) for s, d in...]
  transfers between devices with their start and end apart: 6 -> 6, of which waited for: 4 -> 2; matrix products, arithmetic and copies ran while one was open for 0% -> 0% of each run, Pallas kernels for 22% -> 30%
where the time goes in v4:
time: 64.8 us; the launch traced here: 63.7 us
  Pallas kernels  30.3 us (47%)
  starting transfers between devices  22.7 us (35%)
  waiting for transfers between devices  6.06 us (9%)
  local copies, waits for them, and re-layouts  4.28 us (7%)
    pallas_call x9, Pallas kernels, call(): pl.pallas_call(kernel, out_shape=[jax.ShapeDtypeStruct(s, d) for s, d in...  30.3 us
    all_to_all x2, starting transfers between devices, shards(): lax.all_to_all(send, 'leaf', split_axis=0, concat_axis=0, tiled=True, axi...  13 us
    ppermute x1, starting transfers between devices, shards(): rec_a = lax.ppermute(send_a, axes, pairs_a)  7.09 us
    all_to_all x2, waiting for transfers between devices, shards(): lax.all_to_all(send, 'leaf', split_axis=0, concat_axis=0, tiled=True, axi...  5.07 us
    unnamed x28, local copies, waits for them, and re-layouts  4.28 us
    ppermute x1, starting transfers between devices, shards(): rec_b = lax.ppermute(send_b, axes, pairs_b)  1.92 us
  transfers between devices with their start and end apart: 6, of which 2 were waited for; matrix products, arithmetic and copies ran while one was open for 0% of the time, Pallas kernels for 30%

profile of v4, /device:TPU:8, one launch (start us, length us, event | category | flops | bytes accessed | tf_op | source)
XLA Modules:
  0.0 63.7 jit_solution(2800608902373182953)
XLA Ops:
  0.0 1.1 %copy-done.8 = bf16[8,8192]{1,0:T(8,128)(2,1)S(1)} copy-done((bf16[8,8192]{1,0:T(8,128)(2,1)S(1)}, bf16[8,8192]{1,0:T(8,128)(2,1)}, u32[]{:S(2)}) %copy-start.8) | copy-done | bytes 131096
  1.1 0.8 %copy-done.9 = bf16[3,8192]{1,0:T(4,128)(2,1)S(1)} copy-done((bf16[3,8192]{1,0:T(4,128)(2,1)S(1)}, bf16[3,8192]{1,0:T(4,128)(2,1)}, u32[]{:S(2)}) %copy-start.9) | copy-done | bytes 49176
  1.9 0.8 %copy-done.10 = s32[1,8192]{1,0:T(1,128)S(1)} copy-done((s32[1,8192]{1,0:T(1,128)S(1)}, s32[1,8192]{1,0:T(1,128)}, u32[]{:S(2)}) %copy-start.10) | copy-done | bytes 32792
  2.7 3.3 %shard_map.109 = (bf16[8,8192]{1,0:T(8,128)(2,1)S(1)}, bf16[8,8192]{1,0:T(8,128)(2,1)S(1)}, bf16[16,1024]{1,0:T(8,128)(2,1)S(1)}, bf16[8,1024]{1,0:T(8,128)(2,1)S(1)}, bf16[8,5120]{1,0:T(8,128)(2,1)S(1)}) custom-call(bf16[3,8192]{1,0:T(4,128)(2,1)S(1)} %copy-done.9, bf16[8,8192]{1,0:T(8,128)(2,1)S(1)} %copy-done.8, s32[1,8192]{1,0:T(1,128)S(1)} %copy-done.10), custom_call_target="tpu_custom_call" | custom-call | flops 1610612736 | bytes 1048576 | tf_op jit(solution)/shard_map/pallas_call | solution.py:59
  5.9 0.0 copy-start.4
  5.9 0.1 collective-permute-start
  6.1 1.7 %shard_map.110.mats.mats_in = bf16[2560,64]{1,0:T(8,128)(2,1)S(1)} custom-call(bf16[64,64,254]{2,1,0:T(8,128)(2,1)S(1)} %bitcast.12), custom_call_target="tpu_custom_call" | custom-call | flops 83886080 | bytes 3145728 | tf_op jit(solution)/shard_map/pallas_call | solution.py:59
  7.8 1.5 %shard_map.111 = (f32[256,128]{1,0:T(8,128)S(1)}, f32[32,64]{1,0:T(8,128)S(1)}) custom-call(bf16[8,8192]{1,0:T(8,128)(2,1)S(1)} %get-tuple-element.17.vt.vt_in, bf16[16,64,512]{2,1,0:T(8,128)(2,1)S(1)} %copy-done.3, bf16[30,64,64]{2,1,0:T(8,128)(2,1)S(1)} %copy-done.4, bf16[2560,64]{1,0:T(8,128)(2,1)S(1)} %shard_map.110.mats.mats_in), custom_call_target="tpu_custom_call" | custom-call | flops 134217728 | bytes 2097152 | tf_op jit(solution)/shard_map/pallas_call | solution.py:59
  9.3 0.0 copy-done.5
  9.4 4.3 %shard_map.112 = (bf16[512,640]{1,0:T(8,128)(2,1)}, bf16[16,1024]{1,0:T(8,128)(2,1)S(1)}, bf16[8,1024]{1,0:T(8,128)(2,1)S(1)}) custom-call(f32[256,128]{1,0:T(8,128)S(1)} %get-tuple-element.18.cf, f32[32,64]{1,0:T(8,128)S(1)} %get-tuple-element.19.path.path_in, bf16[64,64,256]{2,1,0:T(8,128)(2,1)S(1)} %bitcast.11, s32[1,256]{1,0:T(1,128)S(1)} %bitcast.15, ...), custom_call_target="tpu_custom_call" | custom-call | flops 167772160 | bytes 4194304 | tf_op jit(solution)/shard_map/pallas_call | solution.py:59
  13.6 7.4 %all-to-all-start = ((bf16[16,32,640]{2,1,0:T(8,128)(2,1)}), bf16[16,32,640]{2,1,0:T(8,128)(2,1)S(1)}, u32[]{:S(2)}, u32[]{:S(2)}) async-start(bf16[16,32,640]{2,1,0:T(8,128)(2,1)} %bitcast.5), calls=%async_computation | async-start | bytes 1310720 | tf_op jit(solution)/shard_map/all_to_all | solution.py:563
  21.0 7.1 %collective-permute-start.1 = (bf16[16,1024]{1,0:T(8,128)(2,1)S(1)}, bf16[16,1024]{1,0:T(8,128)(2,1)S(1)}, u32[]{:S(2)}, u32[]{:S(2)}) collective-permute-start(bf16[16,1024]{1,0:T(8,128)(2,1)S(1)} %get-tuple-element.25), channel_id=1, source_target_pairs={{1,2},{2,1},{3,4},{4,3},{5,6},{6,5},{7,8},{8,7},{9,10},{10,9},{11,... | collective-permute-start | bytes 98312 | tf_op jit(solution)/shard_map/ppermute | solution.py:566
  28.1 1.9 %collective-permute-start.2 = (bf16[8,1024]{1,0:T(8,128)(2,1)S(1)}, bf16[8,1024]{1,0:T(8,128)(2,1)S(1)}, u32[]{:S(2)}, u32[]{:S(2)}) collective-permute-start(bf16[8,1024]{1,0:T(8,128)(2,1)S(1)} %get-tuple-element.26), channel_id=1, source_target_pairs={{0,2},{3,1},{2,4},{5,3},{4,6},{7,5},{6,8},{9,7},{8,10},{11,9},{10,... | collective-permute-start | bytes 49160 | tf_op jit(solution)/shard_map/ppermute | solution.py:567
  30.0 6.0 %shard_map.115.begun = f32[16,2560]{1,0:T(8,128)S(1)} custom-call(bf16[8,8192]{1,0:T(8,128)(2,1)S(1)} %get-tuple-element.17.vt.vt_in, bf16[8,8192]{1,0:T(8,128)(2,1)S(1)} %get-tuple-element.24.pt_in, bf16[8,5120]{1,0:T(8,128)(2,1)S(1)} %collective-permute-done.seen_c.c_in), custom_call_target="tpu_custom_call" | custom-call | flops 4966055936 | bytes 1048576 | tf_op jit(solution)/shard_map/pallas_call | solution.py:59
  36.1 0.7 %copy-done.12 = f32[16,2560]{1,0:T(8,128)} copy-done((f32[16,2560]{1,0:T(8,128)}, f32[16,2560]{1,0:T(8,128)S(1)}, u32[]{:S(2)}) %copy-start.12) | copy-done | bytes 163864
  36.8 1.3 %shard_map.113.coup_in = bf16[512,64]{1,0:T(8,128)(2,1)S(1)} custom-call(bf16[64,64,254]{2,1,0:T(8,128)(2,1)S(1)} %bitcast.13, bf16[512,640]{1,0:T(8,128)(2,1)} %get-tuple-element.23.seen), custom_call_target="tpu_custom_call" | custom-call | flops 16777216 | bytes 3145728 | tf_op jit(solution)/shard_map/pallas_call | solution.py:59
  38.1 3.2 %shard_map.114 = bf16[256,512]{1,0:T(8,128)(2,1)} custom-call(bf16[512,640]{1,0:T(8,128)(2,1)S(1)} %bitcast.10, f32[32,64]{1,0:T(8,128)S(1)} %get-tuple-element.19.path.path_in, bf16[2560,64]{1,0:T(8,128)(2,1)S(1)} %shard_map.110.mats.mats_in, bf16[512,64]{1,0:T(8,128)(2,1)S(1)} %shard_map.113.coup_in), custom_call_target="tpu_custom_call" | custom-call | flops 134217728 | bytes 2097152 | tf_op jit(solution)/shard_map/pallas_call | solution.py:59
  41.3 5.6 %all-to-all-start.1 = ((bf16[8,32,512]{2,1,0:T(8,128)(2,1)}), bf16[8,32,512]{2,1,0:T(8,128)(2,1)S(1)}, u32[]{:S(2)}, u32[]{:S(2)}) async-start(bf16[8,32,512]{2,1,0:T(8,128)(2,1)} %bitcast.8), calls=%async_computation.1 | async-start | bytes 524288 | tf_op jit(solution)/shard_map/all_to_all | solution.py:599
  46.9 0.9 %copy-done.13 = f32[16,2560]{1,0:T(8,128)S(1)} copy-done((f32[16,2560]{1,0:T(8,128)S(1)}, f32[16,2560]{1,0:T(8,128)}, u32[]{:S(2)}) %copy-start.13) | copy-done | bytes 163864
  47.8 5.2 %shard_map.116 = (f32[8,4096]{1,0:T(8,128)S(1)}, f32[8,4096]{1,0:T(8,128)S(1)}) custom-call(bf16[8,8192]{1,0:T(8,128)(2,1)S(1)} %get-tuple-element.17.vt.vt_in, bf16[8,8192]{1,0:T(8,128)(2,1)S(1)} %get-tuple-element.24.pt_in, bf16[8,5120]{1,0:T(8,128)(2,1)S(1)} %collective-permute-done.seen_c.c_in, bf16[16,1024]{1,0:T(8,128)(2,1)S(1)} %collective-permute-done.1.a_in, ...), custom_call_target="tpu_custom_call" | custom-call | flops 4026531840 | bytes 1048576 | tf_op jit(solution)/shard_map/pallas_call | solution.py:59
  53.1 0.6 collective-permute-start.3
  53.6 1.0 %collective-permute-done.3.other_in = f32[8,4096]{1,0:T(8,128)S(1)} collective-permute-done((f32[8,4096]{1,0:T(8,128)S(1)}, f32[8,4096]{1,0:T(8,128)S(1)}, u32[]{:S(2)}, u32[]{:S(2)}) %collective-permute-start.3) | collective-permute-done | bytes 131104 | tf_op jit(solution)/shard_map/ppermute | solution.py:609
  54.6 5.1 %all-to-all-done.1 = bf16[8,32,512]{2,1,0:T(8,128)(2,1)S(1)} async-done(((bf16[8,32,512]{2,1,0:T(8,128)(2,1)}), bf16[8,32,512]{2,1,0:T(8,128)(2,1)S(1)}, u32[]{:S(2)}, u32[]{:S(2)}) %all-to-all-start.1) | async-done | bytes 262176 | tf_op jit(solution)/shard_map/all_to_all | solution.py:599
  59.7 3.8 %shard_map.117 = bf16[8,8192]{1,0:T(8,128)(2,1)} custom-call(bf16[256,512]{1,0:T(8,128)(2,1)S(1)} %bitcast.14, f32[8,4096]{1,0:T(8,128)S(1)} %get-tuple-element.27.mine_in, f32[8,4096]{1,0:T(8,128)S(1)} %collective-permute-done.3.other_in, bf16[2560,64]{1,0:T(8,128)(2,1)S(1)} %shard_map.110.mats.mats_in, bf16[30,64,64]{2,1,0:T(8,128)(2,1)S(1)} %copy-done.4, ...), custom_call_target="tpu_custom_call" | custom-call | flops 1073741824 | bytes 8388608 | tf_op jit(solution)/shard_map/pallas_call | solution.py:59
  (25 shorter events, 0.1 us)
Async XLA Ops:
  0.0 6.0 %copy-start.1 = (bf16[254,64,64]{0,2,1:T(8,128)(2,1)S(1)}, bf16[254,64,64]{0,2,1:T(8,128)(2,1)}, u32[]{:S(2)}) copy-start(bf16[254,64,64]{0,2,1:T(8,128)(2,1)} %param.20) | copy-start | bytes 6242308
  0.0 1.1 %copy-start.8 = (bf16[8,8192]{1,0:T(8,128)(2,1)S(1)}, bf16[8,8192]{1,0:T(8,128)(2,1)}, u32[]{:S(2)}) copy-start(bf16[8,8192]{1,0:T(8,128)(2,1)} %vec_in.1) | copy-start | bytes 393220
  1.1 0.8 %copy-start.9 = (bf16[3,8192]{1,0:T(4,128)(2,1)S(1)}, bf16[3,8192]{1,0:T(4,128)(2,1)}, u32[]{:S(2)}) copy-start(bf16[3,8192]{1,0:T(4,128)(2,1)} %pts_in.1) | copy-start | bytes 147460
  1.9 0.8 %copy-start.10 = (s32[1,8192]{1,0:T(1,128)S(1)}, s32[1,8192]{1,0:T(1,128)}, u32[]{:S(2)}) copy-start(s32[1,8192]{1,0:T(1,128)} %perm_in.3) | copy-start | bytes 98308
  5.9 1.8 %copy-start.3 = (bf16[16,64,512]{2,1,0:T(8,128)(2,1)S(1)}, bf16[16,64,512]{2,1,0:T(8,128)(2,1)}, u32[]{:S(2)}) copy-start(bf16[16,64,512]{2,1,0:T(8,128)(2,1)} %bases.3) | copy-start | bytes 3145732
  5.9 1.8 %copy-start.4 = (bf16[30,64,64]{2,1,0:T(8,128)(2,1)S(1)}, bf16[30,64,64]{2,1,0:T(8,128)(2,1)}, u32[]{:S(2)}) copy-start(bf16[30,64,64]{2,1,0:T(8,128)(2,1)} %tr.3) | copy-start | bytes 737284
  5.9 3.4 %collective-permute-start = (bf16[8,5120]{1,0:T(8,128)(2,1)S(1)}, bf16[8,5120]{1,0:T(8,128)(2,1)S(1)}, u32[]{:S(2)}, u32[]{:S(2)}) collective-permute-start(bf16[8,5120]{1,0:T(8,128)(2,1)S(1)} %get-tuple-element.22), channel_id=1, source_target_pairs={{0,1},{1,0},{2,3},{3,2},{4,5},{5,4},{6,7},{7,6},{8,9},{9,8},{10,11... | collective-permute-start | bytes 245768 | tf_op jit(solution)/shard_map/ppermute | solution.py:533
  6.1 3.3 %copy-start = (bf16[256,64,64]{0,2,1:T(8,128)(2,1)S(1)}, bf16[256,64,64]{0,2,1:T(8,128)(2,1)}, u32[]{:S(2)}) copy-start(bf16[256,64,64]{0,2,1:T(8,128)(2,1)} %param.16) | copy-start | bytes 6291460
  6.1 3.3 %copy-start.5 = (s32[256]{0:T(256)S(1)}, s32[256]{0:T(256)}, u32[]{:S(2)}) copy-start(s32[256]{0:T(256)} %param.17) | copy-start | bytes 3076
  6.1 3.3 %copy-start.6 = (s32[256,1]{0,1:T(1,128)S(1)}, s32[256,1]{0,1:T(1,128)}, u32[]{:S(2)}) copy-start(s32[256,1]{0,1:T(1,128)} %param.18) | copy-start | bytes 3076
  6.1 3.3 %copy-start.7 = (s32[256]{0:T(256)S(1)}, s32[256]{0:T(256)}, u32[]{:S(2)}) copy-start(s32[256]{0:T(256)} %param.19) | copy-start | bytes 3076
  13.6 24.5 %all-to-all-start = ((bf16[16,32,640]{2,1,0:T(8,128)(2,1)}), bf16[16,32,640]{2,1,0:T(8,128)(2,1)S(1)}, u32[]{:S(2)}, u32[]{:S(2)}) async-start(bf16[16,32,640]{2,1,0:T(8,128)(2,1)} %bitcast.5), calls=%async_computation | async-start | bytes 1310720 | tf_op jit(solution)/shard_map/all_to_all | solution.py:563
  21.0 25.9 %collective-permute-start.1 = (bf16[16,1024]{1,0:T(8,128)(2,1)S(1)}, bf16[16,1024]{1,0:T(8,128)(2,1)S(1)}, u32[]{:S(2)}, u32[]{:S(2)}) collective-permute-start(bf16[16,1024]{1,0:T(8,128)(2,1)S(1)} %get-tuple-element.25), channel_id=1, source_target_pairs={{1,2},{2,1},{3,4},{4,3},{5,6},{6,5},{7,8},{8,7},{9,10},{10,9},{11,... | collective-permute-start | bytes 98312 | tf_op jit(solution)/shard_map/ppermute | solution.py:566
  28.1 18.8 %collective-permute-start.2 = (bf16[8,1024]{1,0:T(8,128)(2,1)S(1)}, bf16[8,1024]{1,0:T(8,128)(2,1)S(1)}, u32[]{:S(2)}, u32[]{:S(2)}) collective-permute-start(bf16[8,1024]{1,0:T(8,128)(2,1)S(1)} %get-tuple-element.26), channel_id=1, source_target_pairs={{0,2},{3,1},{2,4},{5,3},{4,6},{7,5},{6,8},{9,7},{8,10},{11,9},{10,... | collective-permute-start | bytes 49160 | tf_op jit(solution)/shard_map/ppermute | solution.py:567
  30.0 6.7 %copy-start.2 = (bf16[254,64,64]{0,2,1:T(8,128)(2,1)S(1)}, bf16[254,64,64]{0,2,1:T(8,128)(2,1)}, u32[]{:S(2)}) copy-start(bf16[254,64,64]{0,2,1:T(8,128)(2,1)} %param.21) | copy-start | bytes 6242308
  36.1 0.7 %copy-start.12 = (f32[16,2560]{1,0:T(8,128)}, f32[16,2560]{1,0:T(8,128)S(1)}, u32[]{:S(2)}) copy-start(f32[16,2560]{1,0:T(8,128)S(1)} %shard_map.115.begun) | copy-start | bytes 491524
  41.3 18.4 %all-to-all-start.1 = ((bf16[8,32,512]{2,1,0:T(8,128)(2,1)}), bf16[8,32,512]{2,1,0:T(8,128)(2,1)S(1)}, u32[]{:S(2)}, u32[]{:S(2)}) async-start(bf16[8,32,512]{2,1,0:T(8,128)(2,1)} %bitcast.8), calls=%async_computation.1 | async-start | bytes 524288 | tf_op jit(solution)/shard_map/all_to_all | solution.py:599
  46.9 12.8 %copy-start.11 = (s32[1,8192]{1,0:T(1,128)S(1)}, s32[1,8192]{1,0:T(1,128)}, u32[]{:S(2)}) copy-start(s32[1,8192]{1,0:T(1,128)} %perm_in.3) | copy-start | bytes 98308
  46.9 0.9 %copy-start.13 = (f32[16,2560]{1,0:T(8,128)S(1)}, f32[16,2560]{1,0:T(8,128)}, u32[]{:S(2)}) copy-start(f32[16,2560]{1,0:T(8,128)} %copy-done.12) | copy-start | bytes 491524
  53.1 1.6 %collective-permute-start.3 = (f32[8,4096]{1,0:T(8,128)S(1)}, f32[8,4096]{1,0:T(8,128)S(1)}, u32[]{:S(2)}, u32[]{:S(2)}) collective-permute-start(f32[8,4096]{1,0:T(8,128)S(1)} %get-tuple-element.28), channel_id=1, source_target_pairs={{0,1},{1,0},{2,3},{3,2},{4,5},{5,4},{6,7},{7,6},{8,9},{9,8},{10,11... | collective-permute-start | bytes 393224 | tf_op jit(solution)/shard_map/ppermute | solution.py:609

commit v5 on v4

--- a/solution.py
+++ b/solution.py
@@ -56,9 +56,16 @@
 
 def call(kernel, outs, scratch, args, kinds, flops, nbytes, vmem=16):
     ins, results = kinds.split(">")
+    args = [
+        pltpu.with_memory_space_constraint(x, pltpu.HBM) if k == "h" else x
+        for x, k in zip(args, ins)
+    ]
     return pl.pallas_call(
         kernel,
-        out_shape=[jax.ShapeDtypeStruct(s, d) for s, d in outs],
+        out_shape=[
+            pltpu.HBM(s, d) if k == "h" else jax.ShapeDtypeStruct(s, d)
+            for (s, d), k in zip(outs, results)
+        ],
         in_specs=[SPEC[k] for k in ins],
         out_specs=[SPEC[k] for k in results],
         scratch_shapes=scratch,
@@ -77,7 +84,7 @@
 
 
 def gather_kernel(
-    pts_in, vec_in, perm_in, vt, pt, send_a, send_b, send_c, pts, vec, perm, dv, dp, sems
+    pts_in, vec_in, perm_in, vt, pt, send_c, pts, vec, perm, dv, dp, sems
 ):
     core = lax.axis_index("vec")
     for copy in fetch(sems, (perm_in, perm), (vec_in, vec), (pts_in, pts)):
@@ -111,24 +118,27 @@
             out = jnp.where(pair == 2 * m, got[8 * m : 8 * m + 8], out)
         out = out[:4] + out[4:]
         pt[:, cols] = jnp.concatenate([out, jnp.zeros((4, width), f32)], axis=0).astype(bf16)
-    first, last = slice(0, HALO), slice(COLS - HALO, COLS)
 
     @pl.when(core == 0)
     def _():
-        send_a[0:8, :] = vt[:, first]
-        send_a[8:16, :] = pt[:, first]
-        send_b[...] = vt[:, last]
         send_c[...] = vt[:, COLS - LOCAL :]
 
     @pl.when(core == 1)
     def _():
-        send_a[0:8, :] = vt[:, last]
-        send_a[8:16, :] = pt[:, last]
-        send_b[...] = vt[:, first]
         send_c[...] = vt[:, :LOCAL]
 
 
-def coeff_kernel(vt, bases, tr, mats, cf, path):
+def coeff_kernel(vt, pt, rec_c, bases, tr, mats, cf, path, halo):
+    core = lax.axis_index("vec")
+    ends = ((slice(0, HALO), slice(0, HALO)), (slice(COLS - HALO, COLS), slice(LOCAL - HALO, LOCAL)))
+    for which, (cols, other) in enumerate(ends):
+
+        @pl.when(core == which)
+        def _():
+            halo[0:8, :] = vt[:, cols]
+            halo[8:16, :] = rec_c[:, other]
+            halo[16:24, :] = pt[:, cols]
+
     cf[248:256, :] = jnp.zeros((8, 128), f32)
     for leaf in range(16):
         cf[8 * leaf : 8 * leaf + 8, :64] = dot(
@@ -156,10 +166,8 @@
 
 
 def product_kernel(
-    cf, path, cp, bsrc, bown, btgt, halo_a, halo_b, seen_c, send, send_a, send_b, pick, prod
+    cf, path, cp, bsrc, bown, btgt, send, pick, prod
 ):
-    send_a[...] = halo_a[...]
-    send_b[...] = halo_b[...]
     source = hot(iota((32, 256), 0) == bsrc[...])
     for v in range(8):
         mine = cf[pl.ds(v, 32, stride=8), :][:, :64].astype(bf16)
@@ -226,9 +234,9 @@
                 to = leaf_cols(w)
                 if w < 2:
                     near_cols = leaf_cols(w if which == 0 else 1 - w)
-                    vw[0:8, to] = halo[1][:, near_cols]
-                    vw[8:16, to] = halo[0][0:8, near_cols]
-                    pw[:, to] = halo[0][8:16, near_cols].astype(f32)
+                    vw[0:8, to] = halo[8:16, near_cols]
+                    vw[8:16, to] = halo[0:8, near_cols]
+                    pw[:, to] = halo[16:24, near_cols].astype(f32)
                 else:
                     local = leaf_cols(w - 2 if which == 0 else 17 - w)
                     vw[0:8, to] = vt[:, local]
@@ -288,20 +296,20 @@
 
 
 def near_rest_kernel(
-    vt_in, pt_in, c_in, a_in, b_in, begun, mine, other,
-    vt, pt, rec_c, vw, fs, ft, pw, acc, sems, rec_a, rec_b,
+    vt_in, pt_in, c_in, halo_in, begun, mine, other,
+    vt, pt, rec_c, vw, fs, ft, pw, acc, sems, halo,
 ):
     left = LEAF * (SPLIT - 2)
     copies = fetch(
-        sems, (vt_in, vt), (pt_in, pt), (c_in, rec_c), (a_in, rec_a), (b_in, rec_b),
+        sems, (vt_in, vt), (pt_in, pt), (c_in, rec_c), (halo_in, halo),
         (begun, acc.at[:, left:]),
     )
     acc[:, :left] = jnp.zeros((16, left), f32)
-    for copy in copies[:5]:
+    for copy in copies[:4]:
         copy.wait()
-    load_window(vt, pt, rec_c, (rec_a, rec_b), range(0, SPLIT + 2), vw, pw)
+    load_window(vt, pt, rec_c, halo, range(0, SPLIT + 2), vw, pw)
     features(range(0, SPLIT + 2), pw, fs, ft)
-    copies[5].wait()
+    copies[4].wait()
     for t in range(2, SPLIT):
         near_target(t, vw, fs, ft, acc)
     core = lax.axis_index("vec")
@@ -514,22 +522,21 @@
 ):
     peers = lax.axis_size("leaf")
     axes = ("leaf", "vec")
-    vt, pt, send_a, send_b, send_c = call(
+    vt, pt, send_c = call(
         gather_kernel,
-        [((8, COLS), bf16), ((8, COLS), bf16), ((16, HALO), bf16), ((8, HALO), bf16), ((8, LOCAL), bf16)],
+        [((8, COLS), bf16), ((8, COLS), bf16), ((8, LOCAL), bf16)],
         [
             pltpu.VMEM((3, COLS), bf16), pltpu.VMEM((8, COLS), bf16), pltpu.VMEM((1, COLS), i32),
             pltpu.VMEM((256, 256), bf16), pltpu.VMEM((128, 256), f32), pltpu.SemaphoreType.DMA((3,)),
         ],
-        (points, vectors, leaf_order), "hhh>vvvvv",
+        (points, vectors, leaf_order), "hhh>vvv",
         2 * 384 * 256 * COLS, 1 << 20,
     )
-    pairs_a, pairs_b, pairs_c = [], [], []
+    pairs_a, pairs_c = [], []
     for d in range(peers):
         pairs_c += [(2 * d, 2 * d + 1), (2 * d + 1, 2 * d)]
         if d + 1 < peers:
             pairs_a += [(2 * d + 1, 2 * d + 2), (2 * d + 2, 2 * d + 1)]
-            pairs_b += [(2 * d, 2 * d + 2), (2 * d + 3, 2 * d + 1)]
     rec_c = lax.ppermute(send_c, axes, pairs_c)
     ut = jnp.transpose(up_transfer, (1, 2, 0))
     uc = jnp.transpose(up_coupling, (1, 2, 0))
@@ -540,31 +547,30 @@
         (ut,), "v>v",
         2 * 4096 * 256 * 40, 3 << 20,
     )
-    cf, path = call(
+    cf, path, halo = call(
         coeff_kernel,
-        [((256, 128), f32), ((32, 64), f32)],
+        [((256, 128), f32), ((32, 64), f32), ((24, HALO), bf16)],
         [],
-        (vt, leaf_bases, transfers, mats), "vvvv>vv",
+        (vt, pt, rec_c, leaf_bases, transfers, mats), "vvvvvv>vvv",
         2 * 512 * 512 * 256, 2 << 20,
     )
-    send, send_a, send_b = call(
+    halo = lax.ppermute(halo, axes, pairs_a)
+    (send,) = call(
         product_kernel,
-        [((512, 640), bf16), ((16, HALO), bf16), ((8, HALO), bf16)],
+        [((512, 640), bf16)],
         [pltpu.VMEM((1024, 128), f32), pltpu.VMEM((640, 256), bf16)],
         (
             cf, path, jnp.transpose(coupling_blocks, (1, 2, 0)),
             block_source.reshape(1, -1), block_owner.reshape(1, -1), block_target.reshape(1, -1),
-            send_a, send_b, rec_c,
-        ), "vvvvvvvva>vvv",
+        ), "vvvvvv>v",
         2 * 512 * 256 * 640, 4 << 20,
     )
+    send, halo = lax.optimization_barrier((send, halo))
     near_groups = [[xy * 8 + z for z in range(8)] for xy in range(peers // 8)]
     far_groups = [[xy * 8 + z for xy in range(peers // 8)] for z in range(8)]
     recv = lax.all_to_all(
         send, "leaf", split_axis=0, concat_axis=0, tiled=True, axis_index_groups=far_groups
     )
-    rec_a = lax.ppermute(send_a, axes, pairs_a)
-    rec_b = lax.ppermute(send_b, axes, pairs_b)
     buffers = [
         pltpu.VMEM((8, COLS), bf16), pltpu.VMEM((8, COLS), bf16), pltpu.VMEM((8, LOCAL), bf16),
         pltpu.VMEM((16, 6144), bf16), pltpu.VMEM((6144, 16), bf16), pltpu.VMEM((16, 6144), bf16),
@@ -602,8 +608,8 @@
     near_mine, near_send = call(
         near_rest_kernel,
         [((8, HALF), f32), ((8, HALF), f32)],
-        buffers + [pltpu.VMEM((16, HALO), bf16), pltpu.VMEM((8, HALO), bf16)],
-        (vt, pt, rec_c, rec_a, rec_b, begun), "aaaaah>vv",
+        buffers + [pltpu.VMEM((24, HALO), bf16)],
+        (vt, pt, rec_c, halo, begun), "aaaah>vv",
         2 * 30 * 512 * 512 * 256, 1 << 20, vmem=24,
     )
     near_other = lax.ppermute(near_send, axes, pairs_c)

time: 64.8 us -> 62.3 us (0.961); the launches traced: 63.7 us -> 61.9 us
  local copies, waits for them, and re-layouts: 4.28 us -> 0.05 us
  Pallas kernels: 30.3 us -> 32.2 us
  waiting for transfers between devices: 6.06 us -> 7.8 us
  starting transfers between devices: 22.7 us -> 21.5 us
    unnamed x28 -> x16, local copies, waits for them, and re-layouts: 4.28 us -> 0.05 us
    pallas_call x9, Pallas kernels: 30.3 us -> 32.2 us  [call(): pl.pallas_call(kernel, out_shape=[pltpu.HBM(s, d) if k == 'h' else jax.Sh...]
    all_to_all x2, waiting for transfers between devices: 5.07 us -> 6.46 us  [shards(): lax.all_to_all(send, 'leaf', split_axis=0, concat_axis=0, tiled=True, axi...]
    ppermute x2 -> x1, starting transfers between devices: 9.01 us -> 7.73 us  [shards(): halo = lax.ppermute(halo, axes, pairs_a)]
  transfers between devices with their start and end apart: 6 -> 5, of which waited for: 2 -> 3; matrix products, arithmetic and copies ran while one was open for 0% -> 0% of each run, Pallas kernels for 30% -> 31%
where the time goes in v5:
time: 62.3 us; the launch traced here: 61.9 us
  Pallas kernels  32.2 us (52%)
  starting transfers between devices  21.5 us (35%)
  waiting for transfers between devices  7.8 us (13%)
    pallas_call x9, Pallas kernels, call(): pl.pallas_call(kernel, out_shape=[pltpu.HBM(s, d) if k == 'h' else jax.Sh...  32.2 us
    all_to_all x2, starting transfers between devices, shards(): lax.all_to_all(send, 'leaf', split_axis=0, concat_axis=0, tiled=True, axi...  13.6 us
    ppermute x1, starting transfers between devices, shards(): halo = lax.ppermute(halo, axes, pairs_a)  7.73 us
    all_to_all x2, waiting for transfers between devices, shards(): lax.all_to_all(send, 'leaf', split_axis=0, concat_axis=0, tiled=True, axi...  6.46 us
    ppermute x1, waiting for transfers between devices, shards(): near_other = lax.ppermute(near_send, axes, pairs_c)  1.33 us
  transfers between devices with their start and end apart: 5, of which 3 were waited for; matrix products, arithmetic and copies ran while one was open for 0% of the time, Pallas kernels for 31%

profile of v5, /device:TPU:8, one launch (start us, length us, event | category | flops | bytes accessed | tf_op | source)
XLA Modules:
  0.0 61.9 jit_solution(14915888404212873806)
XLA Ops:
  0.0 4.1 %shard_map.109 = (bf16[8,8192]{1,0:T(8,128)(2,1)S(1)}, bf16[8,8192]{1,0:T(8,128)(2,1)S(1)}, bf16[8,5120]{1,0:T(8,128)(2,1)S(1)}) custom-call(bf16[3,8192]{1,0:T(4,128)(2,1)} %pts_in.1, bf16[8,8192]{1,0:T(8,128)(2,1)} %vec_in.1, s32[1,8192]{1,0:T(1,128)} %perm_in.3), custom_call_target="tpu_custom_call" | custom-call | flops 1610612736 | bytes 1048576 | tf_op jit(solution)/shard_map/pallas_call | solution.py:63
  4.1 0.0 copy-start.3
  4.1 0.0 copy-start.4
  4.1 0.1 collective-permute-start
  4.2 0.0 copy-start.1
  4.2 0.0 copy-start.5
  4.2 0.0 copy-start.6
  4.2 0.0 copy-start.7
  4.3 1.7 %shard_map.110.mats.mats_in = bf16[2560,64]{1,0:T(8,128)(2,1)S(1)} custom-call(bf16[64,64,254]{2,1,0:T(8,128)(2,1)S(1)} %bitcast.11), custom_call_target="tpu_custom_call" | custom-call | flops 83886080 | bytes 3145728 | tf_op jit(solution)/shard_map/pallas_call | solution.py:63
  5.9 0.0 collective-permute-done.rec_c.c_in
  5.9 1.5 %shard_map.111 = (f32[256,128]{1,0:T(8,128)S(1)}, f32[32,64]{1,0:T(8,128)S(1)}, bf16[24,1024]{1,0:T(8,128)(2,1)S(1)}) custom-call(bf16[8,8192]{1,0:T(8,128)(2,1)S(1)} %get-tuple-element.15.vt.vt_in, bf16[8,8192]{1,0:T(8,128)(2,1)S(1)} %get-tuple-element.16.pt.pt_in, bf16[8,5120]{1,0:T(8,128)(2,1)S(1)} %collective-permute-done.rec_c.c_in, ...), custom_call_target="tpu_custom_call" | custom-call | flops 134217728 | bytes 2097152 | tf_op jit(solution)/shard_map/pallas_call | solution.py:63
  7.5 7.7 %collective-permute-start.1 = (bf16[24,1024]{1,0:T(8,128)(2,1)S(1)}, bf16[24,1024]{1,0:T(8,128)(2,1)S(1)}, u32[]{:S(2)}, u32[]{:S(2)}) collective-permute-start(bf16[24,1024]{1,0:T(8,128)(2,1)S(1)} %get-tuple-element.20), channel_id=1, source_target_pairs={{1,2},{2,1},{3,4},{4,3},{5,6},{6,5},{7,8},{8,7},{9,10},{10,9},{11,... | collective-permute-start | bytes 147464 | tf_op jit(solution)/shard_map/ppermute | solution.py:557
  15.3 4.2 %shard_map.112.seen = bf16[512,640]{1,0:T(8,128)(2,1)} custom-call(f32[256,128]{1,0:T(8,128)S(1)} %get-tuple-element.18.cf, f32[32,64]{1,0:T(8,128)S(1)} %get-tuple-element.19.path.path_in, bf16[64,64,256]{2,1,0:T(8,128)(2,1)S(1)} %bitcast.12, s32[1,256]{1,0:T(1,128)S(1)} %bitcast.15, s32[1,256]{1,0:T(1,128)S(1)} %bitcast.16, s32[1,256]{1,0:T(1,128)S(1)} %bitcast.17), custom_call_target="tpu_custom_call" | custom-call | flops 167772160 | bytes 4194304 | tf_op jit(solution)/shard_map/pallas_call | solution.py:63
  19.5 7.5 %all-to-all-start = ((bf16[16,32,640]{2,1,0:T(8,128)(2,1)}), bf16[16,32,640]{2,1,0:T(8,128)(2,1)S(1)}, u32[]{:S(2)}, u32[]{:S(2)}) async-start(bf16[16,32,640]{2,1,0:T(8,128)(2,1)} %bitcast.5), calls=%async_computation | async-start | bytes 1310720 | tf_op jit(solution)/shard_map/all_to_all | solution.py:571
  27.0 6.2 %shard_map.115.begun = f32[16,2560]{1,0:T(8,128)} custom-call(bf16[8,8192]{1,0:T(8,128)(2,1)S(1)} %get-tuple-element.15.vt.vt_in, bf16[8,8192]{1,0:T(8,128)(2,1)S(1)} %get-tuple-element.16.pt.pt_in, bf16[8,5120]{1,0:T(8,128)(2,1)S(1)} %collective-permute-done.rec_c.c_in), custom_call_target="tpu_custom_call" | custom-call | flops 4966055936 | bytes 1048576 | tf_op jit(solution)/shard_map/pallas_call | solution.py:63
  33.2 1.3 %shard_map.113.coup_in = bf16[512,64]{1,0:T(8,128)(2,1)S(1)} custom-call(bf16[64,64,254]{2,1,0:T(8,128)(2,1)S(1)} %bitcast.13, bf16[512,640]{1,0:T(8,128)(2,1)} %shard_map.112.seen), custom_call_target="tpu_custom_call" | custom-call | flops 16777216 | bytes 3145728 | tf_op jit(solution)/shard_map/pallas_call | solution.py:63
  34.6 1.8 %all-to-all-done = bf16[16,32,640]{2,1,0:T(8,128)(2,1)S(1)} async-done(((bf16[16,32,640]{2,1,0:T(8,128)(2,1)}), bf16[16,32,640]{2,1,0:T(8,128)(2,1)S(1)}, u32[]{:S(2)}, u32[]{:S(2)}) %all-to-all-start) | async-done | bytes 655392 | tf_op jit(solution)/shard_map/all_to_all | solution.py:571
  36.4 3.1 %shard_map.114 = bf16[256,512]{1,0:T(8,128)(2,1)} custom-call(bf16[512,640]{1,0:T(8,128)(2,1)S(1)} %bitcast.10, f32[32,64]{1,0:T(8,128)S(1)} %get-tuple-element.19.path.path_in, bf16[2560,64]{1,0:T(8,128)(2,1)S(1)} %shard_map.110.mats.mats_in, bf16[512,64]{1,0:T(8,128)(2,1)S(1)} %shard_map.113.coup_in), custom_call_target="tpu_custom_call" | custom-call | flops 134217728 | bytes 2097152 | tf_op jit(solution)/shard_map/pallas_call | solution.py:63
  39.6 6.1 %all-to-all-start.1 = ((bf16[8,32,512]{2,1,0:T(8,128)(2,1)}), bf16[8,32,512]{2,1,0:T(8,128)(2,1)S(1)}, u32[]{:S(2)}, u32[]{:S(2)}) async-start(bf16[8,32,512]{2,1,0:T(8,128)(2,1)} %bitcast.8), calls=%async_computation.1 | async-start | bytes 524288 | tf_op jit(solution)/shard_map/all_to_all | solution.py:605
  45.7 5.5 %shard_map.116 = (f32[8,4096]{1,0:T(8,128)S(1)}, f32[8,4096]{1,0:T(8,128)S(1)}) custom-call(bf16[8,8192]{1,0:T(8,128)(2,1)S(1)} %get-tuple-element.15.vt.vt_in, bf16[8,8192]{1,0:T(8,128)(2,1)S(1)} %get-tuple-element.16.pt.pt_in, bf16[8,5120]{1,0:T(8,128)(2,1)S(1)} %collective-permute-done.rec_c.c_in, bf16[24,1024]{1,0:T(8,128)(2,1)S(1)} %collective-permute-done.1.halo_in, ...), custom_call_target="tpu_custom_call" | custom-call | flops 4026531840 | bytes 1048576 | tf_op jit(solution)/shard_map/pallas_call | solution.py:63
  51.2 0.1 collective-permute-start.2
  51.3 1.3 %collective-permute-done.2.other_in = f32[8,4096]{1,0:T(8,128)S(1)} collective-permute-done((f32[8,4096]{1,0:T(8,128)S(1)}, f32[8,4096]{1,0:T(8,128)S(1)}, u32[]{:S(2)}, u32[]{:S(2)}) %collective-permute-start.2) | collective-permute-done | bytes 131104 | tf_op jit(solution)/shard_map/ppermute | solution.py:615
  52.6 4.6 %all-to-all-done.1 = bf16[8,32,512]{2,1,0:T(8,128)(2,1)S(1)} async-done(((bf16[8,32,512]{2,1,0:T(8,128)(2,1)}), bf16[8,32,512]{2,1,0:T(8,128)(2,1)S(1)}, u32[]{:S(2)}, u32[]{:S(2)}) %all-to-all-start.1) | async-done | bytes 262176 | tf_op jit(solution)/shard_map/all_to_all | solution.py:605
  57.3 4.5 %shard_map.117 = bf16[8,8192]{1,0:T(8,128)(2,1)} custom-call(bf16[256,512]{1,0:T(8,128)(2,1)S(1)} %bitcast.14, f32[8,4096]{1,0:T(8,128)S(1)} %get-tuple-element.23.mine_in, f32[8,4096]{1,0:T(8,128)S(1)} %collective-permute-done.2.other_in, bf16[2560,64]{1,0:T(8,128)(2,1)S(1)} %shard_map.110.mats.mats_in, bf16[30,64,64]{2,1,0:T(8,128)(2,1)S(1)} %copy-done.4, ...), custom_call_target="tpu_custom_call" | custom-call | flops 1073741824 | bytes 8388608 | tf_op jit(solution)/shard_map/pallas_call | solution.py:63
  (11 shorter events, 0.0 us)
Async XLA Ops:
  0.0 4.2 %copy-start = (bf16[254,64,64]{0,2,1:T(8,128)(2,1)S(1)}, bf16[254,64,64]{0,2,1:T(8,128)(2,1)}, u32[]{:S(2)}) copy-start(bf16[254,64,64]{0,2,1:T(8,128)(2,1)} %param.20) | copy-start | bytes 6242308
  4.1 1.9 %copy-start.3 = (bf16[16,64,512]{2,1,0:T(8,128)(2,1)S(1)}, bf16[16,64,512]{2,1,0:T(8,128)(2,1)}, u32[]{:S(2)}) copy-start(bf16[16,64,512]{2,1,0:T(8,128)(2,1)} %bases.3) | copy-start | bytes 3145732
  4.1 1.9 %copy-start.4 = (bf16[30,64,64]{2,1,0:T(8,128)(2,1)S(1)}, bf16[30,64,64]{2,1,0:T(8,128)(2,1)}, u32[]{:S(2)}) copy-start(bf16[30,64,64]{2,1,0:T(8,128)(2,1)} %tr.3) | copy-start | bytes 737284
  4.1 1.8 %collective-permute-start = (bf16[8,5120]{1,0:T(8,128)(2,1)S(1)}, bf16[8,5120]{1,0:T(8,128)(2,1)S(1)}, u32[]{:S(2)}, u32[]{:S(2)}) collective-permute-start(bf16[8,5120]{1,0:T(8,128)(2,1)S(1)} %get-tuple-element.17), channel_id=1, source_target_pairs={{0,1},{1,0},{2,3},{3,2},{4,5},{5,4},{6,7},{7,6},{8,9},{9,8},{10,11... | collective-permute-start | bytes 245768 | tf_op jit(solution)/shard_map/ppermute | solution.py:540
  4.2 11.0 %copy-start.1 = (bf16[256,64,64]{0,2,1:T(8,128)(2,1)S(1)}, bf16[256,64,64]{0,2,1:T(8,128)(2,1)}, u32[]{:S(2)}) copy-start(bf16[256,64,64]{0,2,1:T(8,128)(2,1)} %param.16) | copy-start | bytes 6291460
  4.2 11.0 %copy-start.5 = (s32[256]{0:T(256)S(1)}, s32[256]{0:T(256)}, u32[]{:S(2)}) copy-start(s32[256]{0:T(256)} %param.17) | copy-start | bytes 3076
  4.2 11.0 %copy-start.6 = (s32[256,1]{0,1:T(1,128)S(1)}, s32[256,1]{0,1:T(1,128)}, u32[]{:S(2)}) copy-start(s32[256,1]{0,1:T(1,128)} %param.18) | copy-start | bytes 3076
  4.2 11.0 %copy-start.7 = (s32[256]{0:T(256)S(1)}, s32[256]{0:T(256)}, u32[]{:S(2)}) copy-start(s32[256]{0:T(256)} %param.19) | copy-start | bytes 3076
  7.5 12.0 %collective-permute-start.1 = (bf16[24,1024]{1,0:T(8,128)(2,1)S(1)}, bf16[24,1024]{1,0:T(8,128)(2,1)S(1)}, u32[]{:S(2)}, u32[]{:S(2)}) collective-permute-start(bf16[24,1024]{1,0:T(8,128)(2,1)S(1)} %get-tuple-element.20), channel_id=1, source_target_pairs={{1,2},{2,1},{3,4},{4,3},{5,6},{6,5},{7,8},{8,7},{9,10},{10,9},{11,... | collective-permute-start | bytes 147464 | tf_op jit(solution)/shard_map/ppermute | solution.py:557
  19.5 16.9 %all-to-all-start = ((bf16[16,32,640]{2,1,0:T(8,128)(2,1)}), bf16[16,32,640]{2,1,0:T(8,128)(2,1)S(1)}, u32[]{:S(2)}, u32[]{:S(2)}) async-start(bf16[16,32,640]{2,1,0:T(8,128)(2,1)} %bitcast.5), calls=%async_computation | async-start | bytes 1310720 | tf_op jit(solution)/shard_map/all_to_all | solution.py:571
  27.0 6.2 %copy-start.2 = (bf16[254,64,64]{0,2,1:T(8,128)(2,1)S(1)}, bf16[254,64,64]{0,2,1:T(8,128)(2,1)}, u32[]{:S(2)}) copy-start(bf16[254,64,64]{0,2,1:T(8,128)(2,1)} %param.21) | copy-start | bytes 6242308
  39.6 17.7 %all-to-all-start.1 = ((bf16[8,32,512]{2,1,0:T(8,128)(2,1)}), bf16[8,32,512]{2,1,0:T(8,128)(2,1)S(1)}, u32[]{:S(2)}, u32[]{:S(2)}) async-start(bf16[8,32,512]{2,1,0:T(8,128)(2,1)} %bitcast.8), calls=%async_computation.1 | async-start | bytes 524288 | tf_op jit(solution)/shard_map/all_to_all | solution.py:605
  51.2 1.4 %collective-permute-start.2 = (f32[8,4096]{1,0:T(8,128)S(1)}, f32[8,4096]{1,0:T(8,128)S(1)}, u32[]{:S(2)}, u32[]{:S(2)}) collective-permute-start(f32[8,4096]{1,0:T(8,128)S(1)} %get-tuple-element.24), channel_id=1, source_target_pairs={{0,1},{1,0},{2,3},{3,2},{4,5},{5,4},{6,7},{7,6},{8,9},{9,8},{10,11... | collective-permute-start | bytes 393224 | tf_op jit(solution)/shard_map/ppermute | solution.py:615

commit v6 on v5

--- a/solution.py
+++ b/solution.py
@@ -307,12 +307,18 @@
     acc[:, :left] = jnp.zeros((16, left), f32)
     for copy in copies[:4]:
         copy.wait()
+    core = lax.axis_index("vec")
+    end = lax.axis_index("leaf") == (lax.axis_size("leaf") - 1) * core
+
+    @pl.when(end)
+    def _():
+        halo[...] = jnp.zeros_like(halo)
+
     load_window(vt, pt, rec_c, halo, range(0, SPLIT + 2), vw, pw)
     features(range(0, SPLIT + 2), pw, fs, ft)
     copies[4].wait()
     for t in range(2, SPLIT):
         near_target(t, vw, fs, ft, acc)
-    core = lax.axis_index("vec")
     for which in range(2):
 
         @pl.when(core == which)
@@ -532,7 +538,8 @@
         (points, vectors, leaf_order), "hhh>vvv",
         2 * 384 * 256 * COLS, 1 << 20,
     )
-    pairs_a, pairs_c = [], []
+    pairs_c = []
+    pairs_a = [(0, 2 * peers - 1), (2 * peers - 1, 0)]
     for d in range(peers):
         pairs_c += [(2 * d, 2 * d + 1), (2 * d + 1, 2 * d)]
         if d + 1 < peers:

time: 62.3 us -> 60.4 us (0.970)
  starting transfers between devices: 21.5 us -> 19.5 us
    ppermute x1, starting transfers between devices: 7.73 us -> 5.84 us  [shards(): halo = lax.ppermute(halo, axes, pairs_a)]
  transfers between devices with their start and end apart: 5 -> 5, of which waited for: 3 -> 3; matrix products, arithmetic and copies ran while one was open for 0% -> 0% of each run, Pallas kernels for 31% -> 32%
where the time goes in v6:
time: 60.4 us; the launch traced here: 60 us
  Pallas kernels  32.2 us (53%)
  starting transfers between devices  19.5 us (32%)
  waiting for transfers between devices  7.91 us (13%)
    pallas_call x9, Pallas kernels, call(): pl.pallas_call(kernel, out_shape=[pltpu.HBM(s, d) if k == 'h' else jax.Sh...  32.2 us
    all_to_all x2, starting transfers between devices, shards(): lax.all_to_all(send, 'leaf', split_axis=0, concat_axis=0, tiled=True, axi...  13.5 us
    all_to_all x2, waiting for transfers between devices, shards(): lax.all_to_all(send, 'leaf', split_axis=0, concat_axis=0, tiled=True, axi...  6.57 us
    ppermute x1, starting transfers between devices, shards(): halo = lax.ppermute(halo, axes, pairs_a)  5.84 us
    ppermute x1, waiting for transfers between devices, shards(): near_other = lax.ppermute(near_send, axes, pairs_c)  1.33 us
  transfers between devices with their start and end apart: 5, of which 3 were waited for; matrix products, arithmetic and copies ran while one was open for 0% of the time, Pallas kernels for 32%

profile of v6, /device:TPU:8, one launch (start us, length us, event | category | flops | bytes accessed | tf_op | source)
XLA Modules:
  0.0 60.0 jit_solution(1124368625918892766)
XLA Ops:
  0.0 4.1 %shard_map.109 = (bf16[8,8192]{1,0:T(8,128)(2,1)S(1)}, bf16[8,8192]{1,0:T(8,128)(2,1)S(1)}, bf16[8,5120]{1,0:T(8,128)(2,1)S(1)}) custom-call(bf16[3,8192]{1,0:T(4,128)(2,1)} %pts_in.1, bf16[8,8192]{1,0:T(8,128)(2,1)} %vec_in.1, s32[1,8192]{1,0:T(1,128)} %perm_in.3), custom_call_target="tpu_custom_call" | custom-call | flops 1610612736 | bytes 1048576 | tf_op jit(solution)/shard_map/pallas_call | solution.py:63
  4.1 0.0 copy-start.3
  4.1 0.0 copy-start.4
  4.1 0.1 collective-permute-start
  4.2 0.0 copy-start.1
  4.2 0.0 copy-start.5
  4.2 0.0 copy-start.6
  4.2 0.0 copy-start.7
  4.3 1.7 %shard_map.110.mats.mats_in = bf16[2560,64]{1,0:T(8,128)(2,1)S(1)} custom-call(bf16[64,64,254]{2,1,0:T(8,128)(2,1)S(1)} %bitcast.11), custom_call_target="tpu_custom_call" | custom-call | flops 83886080 | bytes 3145728 | tf_op jit(solution)/shard_map/pallas_call | solution.py:63
  5.9 0.0 collective-permute-done.rec_c.c_in
  5.9 1.5 %shard_map.111 = (f32[256,128]{1,0:T(8,128)S(1)}, f32[32,64]{1,0:T(8,128)S(1)}, bf16[24,1024]{1,0:T(8,128)(2,1)S(1)}) custom-call(bf16[8,8192]{1,0:T(8,128)(2,1)S(1)} %get-tuple-element.15.vt.vt_in, bf16[8,8192]{1,0:T(8,128)(2,1)S(1)} %get-tuple-element.16.pt.pt_in, bf16[8,5120]{1,0:T(8,128)(2,1)S(1)} %collective-permute-done.rec_c.c_in, ...), custom_call_target="tpu_custom_call" | custom-call | flops 134217728 | bytes 2097152 | tf_op jit(solution)/shard_map/pallas_call | solution.py:63
  7.5 5.8 %collective-permute-start.1 = (bf16[24,1024]{1,0:T(8,128)(2,1)S(1)}, bf16[24,1024]{1,0:T(8,128)(2,1)S(1)}, u32[]{:S(2)}, u32[]{:S(2)}) collective-permute-start(bf16[24,1024]{1,0:T(8,128)(2,1)S(1)} %get-tuple-element.20), channel_id=1, source_target_pairs={{0,255},{255,0},{1,2},{2,1},{3,4},{4,3},{5,6},{6,5},{7,8},{8,7},{9... | collective-permute-start | bytes 147464 | tf_op jit(solution)/shard_map/ppermute | solution.py:564
  13.3 4.2 %shard_map.112.seen = bf16[512,640]{1,0:T(8,128)(2,1)} custom-call(f32[256,128]{1,0:T(8,128)S(1)} %get-tuple-element.18.cf, f32[32,64]{1,0:T(8,128)S(1)} %get-tuple-element.19.path.path_in, bf16[64,64,256]{2,1,0:T(8,128)(2,1)S(1)} %bitcast.12, s32[1,256]{1,0:T(1,128)S(1)} %bitcast.15, s32[1,256]{1,0:T(1,128)S(1)} %bitcast.16, s32[1,256]{1,0:T(1,128)S(1)} %bitcast.17), custom_call_target="tpu_custom_call" | custom-call | flops 167772160 | bytes 4194304 | tf_op jit(solution)/shard_map/pallas_call | solution.py:63
  17.6 8.6 %all-to-all-start = ((bf16[16,32,640]{2,1,0:T(8,128)(2,1)}), bf16[16,32,640]{2,1,0:T(8,128)(2,1)S(1)}, u32[]{:S(2)}, u32[]{:S(2)}) async-start(bf16[16,32,640]{2,1,0:T(8,128)(2,1)} %bitcast.5), calls=%async_computation | async-start | bytes 1310720 | tf_op jit(solution)/shard_map/all_to_all | solution.py:578
  26.2 6.2 %shard_map.115.begun = f32[16,2560]{1,0:T(8,128)} custom-call(bf16[8,8192]{1,0:T(8,128)(2,1)S(1)} %get-tuple-element.15.vt.vt_in, bf16[8,8192]{1,0:T(8,128)(2,1)S(1)} %get-tuple-element.16.pt.pt_in, bf16[8,5120]{1,0:T(8,128)(2,1)S(1)} %collective-permute-done.rec_c.c_in), custom_call_target="tpu_custom_call" | custom-call | flops 4966055936 | bytes 1048576 | tf_op jit(solution)/shard_map/pallas_call | solution.py:63
  32.4 1.3 %shard_map.113.coup_in = bf16[512,64]{1,0:T(8,128)(2,1)S(1)} custom-call(bf16[64,64,254]{2,1,0:T(8,128)(2,1)S(1)} %bitcast.13, bf16[512,640]{1,0:T(8,128)(2,1)} %shard_map.112.seen), custom_call_target="tpu_custom_call" | custom-call | flops 16777216 | bytes 3145728 | tf_op jit(solution)/shard_map/pallas_call | solution.py:63
  33.7 1.9 %all-to-all-done = bf16[16,32,640]{2,1,0:T(8,128)(2,1)S(1)} async-done(((bf16[16,32,640]{2,1,0:T(8,128)(2,1)}), bf16[16,32,640]{2,1,0:T(8,128)(2,1)S(1)}, u32[]{:S(2)}, u32[]{:S(2)}) %all-to-all-start) | async-done | bytes 655392 | tf_op jit(solution)/shard_map/all_to_all | solution.py:578
  35.7 3.1 %shard_map.114 = bf16[256,512]{1,0:T(8,128)(2,1)} custom-call(bf16[512,640]{1,0:T(8,128)(2,1)S(1)} %bitcast.10, f32[32,64]{1,0:T(8,128)S(1)} %get-tuple-element.19.path.path_in, bf16[2560,64]{1,0:T(8,128)(2,1)S(1)} %shard_map.110.mats.mats_in, bf16[512,64]{1,0:T(8,128)(2,1)S(1)} %shard_map.113.coup_in), custom_call_target="tpu_custom_call" | custom-call | flops 134217728 | bytes 2097152 | tf_op jit(solution)/shard_map/pallas_call | solution.py:63
  38.8 4.9 %all-to-all-start.1 = ((bf16[8,32,512]{2,1,0:T(8,128)(2,1)}), bf16[8,32,512]{2,1,0:T(8,128)(2,1)S(1)}, u32[]{:S(2)}, u32[]{:S(2)}) async-start(bf16[8,32,512]{2,1,0:T(8,128)(2,1)} %bitcast.8), calls=%async_computation.1 | async-start | bytes 524288 | tf_op jit(solution)/shard_map/all_to_all | solution.py:612
  43.8 5.5 %shard_map.116 = (f32[8,4096]{1,0:T(8,128)S(1)}, f32[8,4096]{1,0:T(8,128)S(1)}) custom-call(bf16[8,8192]{1,0:T(8,128)(2,1)S(1)} %get-tuple-element.15.vt.vt_in, bf16[8,8192]{1,0:T(8,128)(2,1)S(1)} %get-tuple-element.16.pt.pt_in, bf16[8,5120]{1,0:T(8,128)(2,1)S(1)} %collective-permute-done.rec_c.c_in, bf16[24,1024]{1,0:T(8,128)(2,1)S(1)} %collective-permute-done.1.halo_in, ...), custom_call_target="tpu_custom_call" | custom-call | flops 4026531840 | bytes 1048576 | tf_op jit(solution)/shard_map/pallas_call | solution.py:63
  49.3 0.1 collective-permute-start.2
  49.4 1.3 %collective-permute-done.2.other_in = f32[8,4096]{1,0:T(8,128)S(1)} collective-permute-done((f32[8,4096]{1,0:T(8,128)S(1)}, f32[8,4096]{1,0:T(8,128)S(1)}, u32[]{:S(2)}, u32[]{:S(2)}) %collective-permute-start.2) | collective-permute-done | bytes 131104 | tf_op jit(solution)/shard_map/ppermute | solution.py:622
  50.7 4.6 %all-to-all-done.1 = bf16[8,32,512]{2,1,0:T(8,128)(2,1)S(1)} async-done(((bf16[8,32,512]{2,1,0:T(8,128)(2,1)}), bf16[8,32,512]{2,1,0:T(8,128)(2,1)S(1)}, u32[]{:S(2)}, u32[]{:S(2)}) %all-to-all-start.1) | async-done | bytes 262176 | tf_op jit(solution)/shard_map/all_to_all | solution.py:612
  55.3 4.5 %shard_map.117 = bf16[8,8192]{1,0:T(8,128)(2,1)} custom-call(bf16[256,512]{1,0:T(8,128)(2,1)S(1)} %bitcast.14, f32[8,4096]{1,0:T(8,128)S(1)} %get-tuple-element.23.mine_in, f32[8,4096]{1,0:T(8,128)S(1)} %collective-permute-done.2.other_in, bf16[2560,64]{1,0:T(8,128)(2,1)S(1)} %shard_map.110.mats.mats_in, bf16[30,64,64]{2,1,0:T(8,128)(2,1)S(1)} %copy-done.4, ...), custom_call_target="tpu_custom_call" | custom-call | flops 1073741824 | bytes 8388608 | tf_op jit(solution)/shard_map/pallas_call | solution.py:63
  (11 shorter events, 0.0 us)
Async XLA Ops:
  0.0 4.2 %copy-start = (bf16[254,64,64]{0,2,1:T(8,128)(2,1)S(1)}, bf16[254,64,64]{0,2,1:T(8,128)(2,1)}, u32[]{:S(2)}) copy-start(bf16[254,64,64]{0,2,1:T(8,128)(2,1)} %param.20) | copy-start | bytes 6242308
  4.1 1.9 %copy-start.3 = (bf16[16,64,512]{2,1,0:T(8,128)(2,1)S(1)}, bf16[16,64,512]{2,1,0:T(8,128)(2,1)}, u32[]{:S(2)}) copy-start(bf16[16,64,512]{2,1,0:T(8,128)(2,1)} %bases.3) | copy-start | bytes 3145732
  4.1 1.9 %copy-start.4 = (bf16[30,64,64]{2,1,0:T(8,128)(2,1)S(1)}, bf16[30,64,64]{2,1,0:T(8,128)(2,1)}, u32[]{:S(2)}) copy-start(bf16[30,64,64]{2,1,0:T(8,128)(2,1)} %tr.3) | copy-start | bytes 737284
  4.1 1.8 %collective-permute-start = (bf16[8,5120]{1,0:T(8,128)(2,1)S(1)}, bf16[8,5120]{1,0:T(8,128)(2,1)S(1)}, u32[]{:S(2)}, u32[]{:S(2)}) collective-permute-start(bf16[8,5120]{1,0:T(8,128)(2,1)S(1)} %get-tuple-element.17), channel_id=1, source_target_pairs={{0,1},{1,0},{2,3},{3,2},{4,5},{5,4},{6,7},{7,6},{8,9},{9,8},{10,11... | collective-permute-start | bytes 245768 | tf_op jit(solution)/shard_map/ppermute | solution.py:547
  4.2 9.1 %copy-start.1 = (bf16[256,64,64]{0,2,1:T(8,128)(2,1)S(1)}, bf16[256,64,64]{0,2,1:T(8,128)(2,1)}, u32[]{:S(2)}) copy-start(bf16[256,64,64]{0,2,1:T(8,128)(2,1)} %param.16) | copy-start | bytes 6291460
  4.2 9.1 %copy-start.5 = (s32[256]{0:T(256)S(1)}, s32[256]{0:T(256)}, u32[]{:S(2)}) copy-start(s32[256]{0:T(256)} %param.17) | copy-start | bytes 3076
  4.2 9.1 %copy-start.6 = (s32[256,1]{0,1:T(1,128)S(1)}, s32[256,1]{0,1:T(1,128)}, u32[]{:S(2)}) copy-start(s32[256,1]{0,1:T(1,128)} %param.18) | copy-start | bytes 3076
  4.2 9.1 %copy-start.7 = (s32[256]{0:T(256)S(1)}, s32[256]{0:T(256)}, u32[]{:S(2)}) copy-start(s32[256]{0:T(256)} %param.19) | copy-start | bytes 3076
  7.5 10.1 %collective-permute-start.1 = (bf16[24,1024]{1,0:T(8,128)(2,1)S(1)}, bf16[24,1024]{1,0:T(8,128)(2,1)S(1)}, u32[]{:S(2)}, u32[]{:S(2)}) collective-permute-start(bf16[24,1024]{1,0:T(8,128)(2,1)S(1)} %get-tuple-element.20), channel_id=1, source_target_pairs={{0,255},{255,0},{1,2},{2,1},{3,4},{4,3},{5,6},{6,5},{7,8},{8,7},{9... | collective-permute-start | bytes 147464 | tf_op jit(solution)/shard_map/ppermute | solution.py:564
  17.6 18.1 %all-to-all-start = ((bf16[16,32,640]{2,1,0:T(8,128)(2,1)}), bf16[16,32,640]{2,1,0:T(8,128)(2,1)S(1)}, u32[]{:S(2)}, u32[]{:S(2)}) async-start(bf16[16,32,640]{2,1,0:T(8,128)(2,1)} %bitcast.5), calls=%async_computation | async-start | bytes 1310720 | tf_op jit(solution)/shard_map/all_to_all | solution.py:578
  26.2 6.2 %copy-start.2 = (bf16[254,64,64]{0,2,1:T(8,128)(2,1)S(1)}, bf16[254,64,64]{0,2,1:T(8,128)(2,1)}, u32[]{:S(2)}) copy-start(bf16[254,64,64]{0,2,1:T(8,128)(2,1)} %param.21) | copy-start | bytes 6242308
  38.8 16.5 %all-to-all-start.1 = ((bf16[8,32,512]{2,1,0:T(8,128)(2,1)}), bf16[8,32,512]{2,1,0:T(8,128)(2,1)S(1)}, u32[]{:S(2)}, u32[]{:S(2)}) async-start(bf16[8,32,512]{2,1,0:T(8,128)(2,1)} %bitcast.8), calls=%async_computation.1 | async-start | bytes 524288 | tf_op jit(solution)/shard_map/all_to_all | solution.py:612
  49.3 1.4 %collective-permute-start.2 = (f32[8,4096]{1,0:T(8,128)S(1)}, f32[8,4096]{1,0:T(8,128)S(1)}, u32[]{:S(2)}, u32[]{:S(2)}) collective-permute-start(f32[8,4096]{1,0:T(8,128)S(1)} %get-tuple-element.24), channel_id=1, source_target_pairs={{0,1},{1,0},{2,3},{3,2},{4,5},{5,4},{6,7},{7,6},{8,9},{9,8},{10,11... | collective-permute-start | bytes 393224 | tf_op jit(solution)/shard_map/ppermute | solution.py:622

commit v7 on v6

--- a/solution.py
+++ b/solution.py
@@ -179,12 +179,12 @@
         for pb in range(4):
             rows = slice(16 * pb, 16 * pb + 16)
 
-            def step(k, acc):
+            acc = [jnp.zeros((16, 128), f32)] * 8
+            for k in range(64):
                 block = cp[k, rows, lanes].astype(f32)
-                picked = pick[pl.ds(pl.multiple_of(512 * half + 8 * k, 8), 8), :]
-                return tuple(acc[v] + picked[v : v + 1] * block for v in range(8))
-
-            acc = lax.fori_loop(0, 64, step, (jnp.zeros((16, 128), f32),) * 8, unroll=8)
+                for v in range(8):
+                    row = pick[pl.ds(512 * half + 8 * k + v, 8, stride=0), :]
+                    acc[v] = acc[v] + jnp.concatenate([row, row], axis=0) * block
             for v in range(8):
                 top = 64 * v + 16 * pb
                 prod[top : top + 16, lanes] = acc[v].astype(bf16)
@@ -572,7 +572,6 @@
         ), "vvvvvv>v",
         2 * 512 * 256 * 640, 4 << 20,
     )
-    send, halo = lax.optimization_barrier((send, halo))
     near_groups = [[xy * 8 + z for z in range(8)] for xy in range(peers // 8)]
     far_groups = [[xy * 8 + z for xy in range(peers // 8)] for z in range(8)]
     recv = lax.all_to_all(

time: 60.4 us -> 58.2 us (0.964)
  waiting for transfers between devices: 7.91 us -> 4.86 us
  starting transfers between devices: 19.5 us -> 20.6 us
    all_to_all x2, waiting for transfers between devices: 6.57 us -> 3.52 us  [shards(): lax.all_to_all(send, 'leaf', split_axis=0, concat_axis=0, tiled=True, axi...]
    all_to_all x2, starting transfers between devices: 13.5 us -> 15.2 us  [shards(): lax.all_to_all(send, 'leaf', split_axis=0, concat_axis=0, tiled=True, axi...]
  transfers between devices with their start and end apart: 5 -> 5, of which waited for: 3 -> 2; matrix products, arithmetic and copies ran while one was open for 0% -> 0% of each run, Pallas kernels for 32% -> 31%
where the time goes in v7:
time: 58.2 us; the launch traced here: 57.8 us
  Pallas kernels  32 us (55%)
  starting transfers between devices  20.6 us (35%)
  waiting for transfers between devices  4.86 us (8%)
    pallas_call x9, Pallas kernels, call(): pl.pallas_call(kernel, out_shape=[pltpu.HBM(s, d) if k == 'h' else jax.Sh...  32 us
    all_to_all x2, starting transfers between devices, shards(): lax.all_to_all(send, 'leaf', split_axis=0, concat_axis=0, tiled=True, axi...  15.2 us
    ppermute x1, starting transfers between devices, shards(): halo = lax.ppermute(halo, axes, pairs_a)  5.27 us
    all_to_all x2, waiting for transfers between devices, shards(): lax.all_to_all(send, 'leaf', split_axis=0, concat_axis=0, tiled=True, axi...  3.52 us
    ppermute x1, waiting for transfers between devices, shards(): near_other = lax.ppermute(near_send, axes, pairs_c)  1.33 us
  transfers between devices with their start and end apart: 5, of which 2 were waited for; matrix products, arithmetic and copies ran while one was open for 0% of the time, Pallas kernels for 31%

profile of v7, /device:TPU:8, one launch (start us, length us, event | category | flops | bytes accessed | tf_op | source)
XLA Modules:
  0.0 57.8 jit_solution(12581633651894241769)
XLA Ops:
  0.0 4.1 %shard_map.109 = (bf16[8,8192]{1,0:T(8,128)(2,1)S(1)}, bf16[8,8192]{1,0:T(8,128)(2,1)S(1)}, bf16[8,5120]{1,0:T(8,128)(2,1)S(1)}) custom-call(bf16[3,8192]{1,0:T(4,128)(2,1)} %pts_in.1, bf16[8,8192]{1,0:T(8,128)(2,1)} %vec_in.1, s32[1,8192]{1,0:T(1,128)} %perm_in.3), custom_call_target="tpu_custom_call" | custom-call | flops 1610612736 | bytes 1048576 | tf_op jit(solution)/shard_map/pallas_call | solution.py:63
  4.1 0.0 copy-start.3
  4.1 0.0 copy-start.4
  4.1 0.1 collective-permute-start
  4.2 0.0 copy-start.1
  4.2 0.0 copy-start.5
  4.2 0.0 copy-start.6
  4.2 0.0 copy-start.7
  4.3 1.7 %shard_map.110.mats.mats_in = bf16[2560,64]{1,0:T(8,128)(2,1)S(1)} custom-call(bf16[64,64,254]{2,1,0:T(8,128)(2,1)S(1)} %bitcast.11), custom_call_target="tpu_custom_call" | custom-call | flops 83886080 | bytes 3145728 | tf_op jit(solution)/shard_map/pallas_call | solution.py:63
  5.9 1.5 %shard_map.111 = (f32[256,128]{1,0:T(8,128)S(1)}, f32[32,64]{1,0:T(8,128)S(1)}, bf16[24,1024]{1,0:T(8,128)(2,1)S(1)}) custom-call(bf16[8,8192]{1,0:T(8,128)(2,1)S(1)} %get-tuple-element.13.vt.vt_in, bf16[8,8192]{1,0:T(8,128)(2,1)S(1)} %get-tuple-element.14.pt.pt_in, bf16[8,5120]{1,0:T(8,128)(2,1)S(1)} %collective-permute-done.rec_c.c_in, ...), custom_call_target="tpu_custom_call" | custom-call | flops 134217728 | bytes 2097152 | tf_op jit(solution)/shard_map/pallas_call | solution.py:63
  7.5 0.0 copy-done.6
  7.5 3.8 %shard_map.112.seen = bf16[512,640]{1,0:T(8,128)(2,1)} custom-call(f32[256,128]{1,0:T(8,128)S(1)} %get-tuple-element.16.cf, f32[32,64]{1,0:T(8,128)S(1)} %get-tuple-element.17.path.path_in, bf16[64,64,256]{2,1,0:T(8,128)(2,1)S(1)} %bitcast.12, s32[1,256]{1,0:T(1,128)S(1)} %bitcast.15, s32[1,256]{1,0:T(1,128)S(1)} %bitcast.16, s32[1,256]{1,0:T(1,128)S(1)} %bitcast.17), custom_call_target="tpu_custom_call" | custom-call | flops 167772160 | bytes 4194304 | tf_op jit(solution)/shard_map/pallas_call | solution.py:63
  11.3 7.4 %all-to-all-start = ((bf16[16,32,640]{2,1,0:T(8,128)(2,1)}), bf16[16,32,640]{2,1,0:T(8,128)(2,1)S(1)}, u32[]{:S(2)}, u32[]{:S(2)}) async-start(bf16[16,32,640]{2,1,0:T(8,128)(2,1)} %bitcast.5), calls=%async_computation | async-start | bytes 1310720 | tf_op jit(solution)/shard_map/all_to_all | solution.py:577
  18.7 5.3 %collective-permute-start.1 = (bf16[24,1024]{1,0:T(8,128)(2,1)S(1)}, bf16[24,1024]{1,0:T(8,128)(2,1)S(1)}, u32[]{:S(2)}, u32[]{:S(2)}) collective-permute-start(bf16[24,1024]{1,0:T(8,128)(2,1)S(1)} %get-tuple-element.18), channel_id=1, source_target_pairs={{0,255},{255,0},{1,2},{2,1},{3,4},{4,3},{5,6},{6,5},{7,8},{8,7},{9... | collective-permute-start | bytes 147464 | tf_op jit(solution)/shard_map/ppermute | solution.py:564
  24.0 6.4 %shard_map.115.begun = f32[16,2560]{1,0:T(8,128)} custom-call(bf16[8,8192]{1,0:T(8,128)(2,1)S(1)} %get-tuple-element.13.vt.vt_in, bf16[8,8192]{1,0:T(8,128)(2,1)S(1)} %get-tuple-element.14.pt.pt_in, bf16[8,5120]{1,0:T(8,128)(2,1)S(1)} %collective-permute-done.rec_c.c_in), custom_call_target="tpu_custom_call" | custom-call | flops 4966055936 | bytes 1048576 | tf_op jit(solution)/shard_map/pallas_call | solution.py:63
  30.4 1.3 %shard_map.113.coup_in = bf16[512,64]{1,0:T(8,128)(2,1)S(1)} custom-call(bf16[64,64,254]{2,1,0:T(8,128)(2,1)S(1)} %bitcast.13, bf16[512,640]{1,0:T(8,128)(2,1)} %shard_map.112.seen), custom_call_target="tpu_custom_call" | custom-call | flops 16777216 | bytes 3145728 | tf_op jit(solution)/shard_map/pallas_call | solution.py:63
  31.7 0.0 all-to-all-done
  31.7 3.2 %shard_map.114 = bf16[256,512]{1,0:T(8,128)(2,1)} custom-call(bf16[512,640]{1,0:T(8,128)(2,1)S(1)} %bitcast.10, f32[32,64]{1,0:T(8,128)S(1)} %get-tuple-element.17.path.path_in, bf16[2560,64]{1,0:T(8,128)(2,1)S(1)} %shard_map.110.mats.mats_in, bf16[512,64]{1,0:T(8,128)(2,1)S(1)} %shard_map.113.coup_in), custom_call_target="tpu_custom_call" | custom-call | flops 134217728 | bytes 2097152 | tf_op jit(solution)/shard_map/pallas_call | solution.py:63
  34.9 7.8 %all-to-all-start.1 = ((bf16[8,32,512]{2,1,0:T(8,128)(2,1)}), bf16[8,32,512]{2,1,0:T(8,128)(2,1)S(1)}, u32[]{:S(2)}, u32[]{:S(2)}) async-start(bf16[8,32,512]{2,1,0:T(8,128)(2,1)} %bitcast.8), calls=%async_computation.1 | async-start | bytes 524288 | tf_op jit(solution)/shard_map/all_to_all | solution.py:611
  42.7 5.5 %shard_map.116 = (f32[8,4096]{1,0:T(8,128)S(1)}, f32[8,4096]{1,0:T(8,128)S(1)}) custom-call(bf16[8,8192]{1,0:T(8,128)(2,1)S(1)} %get-tuple-element.13.vt.vt_in, bf16[8,8192]{1,0:T(8,128)(2,1)S(1)} %get-tuple-element.14.pt.pt_in, bf16[8,5120]{1,0:T(8,128)(2,1)S(1)} %collective-permute-done.rec_c.c_in, bf16[24,1024]{1,0:T(8,128)(2,1)S(1)} %collective-permute-done.1.halo_in, ...), custom_call_target="tpu_custom_call" | custom-call | flops 4026531840 | bytes 1048576 | tf_op jit(solution)/shard_map/pallas_call | solution.py:63
  48.2 0.1 collective-permute-start.2
  48.3 1.3 %collective-permute-done.2.other_in = f32[8,4096]{1,0:T(8,128)S(1)} collective-permute-done((f32[8,4096]{1,0:T(8,128)S(1)}, f32[8,4096]{1,0:T(8,128)S(1)}, u32[]{:S(2)}, u32[]{:S(2)}) %collective-permute-start.2) | collective-permute-done | bytes 131104 | tf_op jit(solution)/shard_map/ppermute | solution.py:621
  49.6 3.5 %all-to-all-done.1 = bf16[8,32,512]{2,1,0:T(8,128)(2,1)S(1)} async-done(((bf16[8,32,512]{2,1,0:T(8,128)(2,1)}), bf16[8,32,512]{2,1,0:T(8,128)(2,1)S(1)}, u32[]{:S(2)}, u32[]{:S(2)}) %all-to-all-start.1) | async-done | bytes 262176 | tf_op jit(solution)/shard_map/all_to_all | solution.py:611
  53.1 4.5 %shard_map.117 = bf16[8,8192]{1,0:T(8,128)(2,1)} custom-call(bf16[256,512]{1,0:T(8,128)(2,1)S(1)} %bitcast.14, f32[8,4096]{1,0:T(8,128)S(1)} %get-tuple-element.19.mine_in, f32[8,4096]{1,0:T(8,128)S(1)} %collective-permute-done.2.other_in, bf16[2560,64]{1,0:T(8,128)(2,1)S(1)} %shard_map.110.mats.mats_in, bf16[30,64,64]{2,1,0:T(8,128)(2,1)S(1)} %copy-done.4, ...), custom_call_target="tpu_custom_call" | custom-call | flops 1073741824 | bytes 8388608 | tf_op jit(solution)/shard_map/pallas_call | solution.py:63
  (11 shorter events, 0.0 us)
Async XLA Ops:
  0.0 4.2 %copy-start = (bf16[254,64,64]{0,2,1:T(8,128)(2,1)S(1)}, bf16[254,64,64]{0,2,1:T(8,128)(2,1)}, u32[]{:S(2)}) copy-start(bf16[254,64,64]{0,2,1:T(8,128)(2,1)} %param.20) | copy-start | bytes 6242308
  4.1 1.9 %copy-start.3 = (bf16[16,64,512]{2,1,0:T(8,128)(2,1)S(1)}, bf16[16,64,512]{2,1,0:T(8,128)(2,1)}, u32[]{:S(2)}) copy-start(bf16[16,64,512]{2,1,0:T(8,128)(2,1)} %bases.3) | copy-start | bytes 3145732
  4.1 1.9 %copy-start.4 = (bf16[30,64,64]{2,1,0:T(8,128)(2,1)S(1)}, bf16[30,64,64]{2,1,0:T(8,128)(2,1)}, u32[]{:S(2)}) copy-start(bf16[30,64,64]{2,1,0:T(8,128)(2,1)} %tr.3) | copy-start | bytes 737284
  4.1 1.8 %collective-permute-start = (bf16[8,5120]{1,0:T(8,128)(2,1)S(1)}, bf16[8,5120]{1,0:T(8,128)(2,1)S(1)}, u32[]{:S(2)}, u32[]{:S(2)}) collective-permute-start(bf16[8,5120]{1,0:T(8,128)(2,1)S(1)} %get-tuple-element.15), channel_id=1, source_target_pairs={{0,1},{1,0},{2,3},{3,2},{4,5},{5,4},{6,7},{7,6},{8,9},{9,8},{10,11... | collective-permute-start | bytes 245768 | tf_op jit(solution)/shard_map/ppermute | solution.py:547
  4.2 3.3 %copy-start.1 = (bf16[256,64,64]{0,2,1:T(8,128)(2,1)S(1)}, bf16[256,64,64]{0,2,1:T(8,128)(2,1)}, u32[]{:S(2)}) copy-start(bf16[256,64,64]{0,2,1:T(8,128)(2,1)} %param.16) | copy-start | bytes 6291460
  4.2 3.3 %copy-start.5 = (s32[256]{0:T(256)S(1)}, s32[256]{0:T(256)}, u32[]{:S(2)}) copy-start(s32[256]{0:T(256)} %param.17) | copy-start | bytes 3076
  4.2 3.3 %copy-start.6 = (s32[256,1]{0,1:T(1,128)S(1)}, s32[256,1]{0,1:T(1,128)}, u32[]{:S(2)}) copy-start(s32[256,1]{0,1:T(1,128)} %param.18) | copy-start | bytes 3076
  4.2 3.3 %copy-start.7 = (s32[256]{0:T(256)S(1)}, s32[256]{0:T(256)}, u32[]{:S(2)}) copy-start(s32[256]{0:T(256)} %param.19) | copy-start | bytes 3076
  11.3 20.4 %all-to-all-start = ((bf16[16,32,640]{2,1,0:T(8,128)(2,1)}), bf16[16,32,640]{2,1,0:T(8,128)(2,1)S(1)}, u32[]{:S(2)}, u32[]{:S(2)}) async-start(bf16[16,32,640]{2,1,0:T(8,128)(2,1)} %bitcast.5), calls=%async_computation | async-start | bytes 1310720 | tf_op jit(solution)/shard_map/all_to_all | solution.py:577
  18.7 11.6 %copy-start.2 = (bf16[254,64,64]{0,2,1:T(8,128)(2,1)S(1)}, bf16[254,64,64]{0,2,1:T(8,128)(2,1)}, u32[]{:S(2)}) copy-start(bf16[254,64,64]{0,2,1:T(8,128)(2,1)} %param.21) | copy-start | bytes 6242308
  18.7 23.9 %collective-permute-start.1 = (bf16[24,1024]{1,0:T(8,128)(2,1)S(1)}, bf16[24,1024]{1,0:T(8,128)(2,1)S(1)}, u32[]{:S(2)}, u32[]{:S(2)}) collective-permute-start(bf16[24,1024]{1,0:T(8,128)(2,1)S(1)} %get-tuple-element.18), channel_id=1, source_target_pairs={{0,255},{255,0},{1,2},{2,1},{3,4},{4,3},{5,6},{6,5},{7,8},{8,7},{9... | collective-permute-start | bytes 147464 | tf_op jit(solution)/shard_map/ppermute | solution.py:564
  34.9 18.2 %all-to-all-start.1 = ((bf16[8,32,512]{2,1,0:T(8,128)(2,1)}), bf16[8,32,512]{2,1,0:T(8,128)(2,1)S(1)}, u32[]{:S(2)}, u32[]{:S(2)}) async-start(bf16[8,32,512]{2,1,0:T(8,128)(2,1)} %bitcast.8), calls=%async_computation.1 | async-start | bytes 524288 | tf_op jit(solution)/shard_map/all_to_all | solution.py:611
  48.2 1.4 %collective-permute-start.2 = (f32[8,4096]{1,0:T(8,128)S(1)}, f32[8,4096]{1,0:T(8,128)S(1)}, u32[]{:S(2)}, u32[]{:S(2)}) collective-permute-start(f32[8,4096]{1,0:T(8,128)S(1)} %get-tuple-element.20), channel_id=1, source_target_pairs={{0,1},{1,0},{2,3},{3,2},{4,5},{5,4},{6,7},{7,6},{8,9},{9,8},{10,11... | collective-permute-start | bytes 393224 | tf_op jit(solution)/shard_map/ppermute | solution.py:621

commit v8 on v7

--- a/solution.py
+++ b/solution.py
@@ -32,6 +32,12 @@
 
 def hot(mask):
     return jnp.where(mask, 1.0, 0.0).astype(bf16)
+
+
+def hot_rows(low, width):
+    rows = iota((256, width), 0).astype(bf16)
+    match = rows == low.astype(bf16)
+    return jnp.where(match, jnp.ones((), bf16), jnp.zeros((), bf16))
 
 
 def halves(x):
@@ -105,7 +111,7 @@
         index = perm[:, cols]
         low = index & 255
         high = jnp.broadcast_to(lax.shift_right_logical(index, 8), (8, width))
-        select = hot(iota((256, width), 0) == low)
+        select = hot_rows(low, width)
         got = dot(data_v, select)
         out = got[:8]
         for q in range(1, 32):
@@ -274,7 +280,7 @@
     acc[:, leaf_cols(t - 2)] += total
 
 
-SPLIT = 5
+SPLIT = 7
 
 
 def near_first_kernel(
@@ -380,10 +386,8 @@
     recv_in, path_in, mats_in, coup_in, send, recv, path, mats, coup, ext, xs, gain, sems
 ):
     device = lax.axis_index("leaf")
-    for copy in fetch(
-        sems, (recv_in, recv), (path_in, path), (mats_in, mats), (coup_in, coup)
-    ):
-        copy.wait()
+    copies = fetch(sems, (recv_in, recv), (mats_in, mats), (coup_in, coup), (path_in, path))
+    copies[0].wait()
     ext[...] = recv[:, 512:640].astype(f32)
 
     labels = jnp.concatenate(
@@ -399,6 +403,8 @@
         xs[8 * g : 8 * g + 8, :] = rows[:8] + rows[8:]
     first, n = 0, 16
     firsts = {3: 0}
+    for copy in copies[1:]:
+        copy.wait()
     for u in range(3, 6):
         for m in range(n // 2):
             r = 8 * (first + 2 * m)
@@ -457,7 +463,7 @@
         (other_in, near_other),
         (perm_in, perm),
     )
-    for copy in copies:
+    for copy in copies[:2]:
         copy.wait()
     device = lax.axis_index("leaf")
     core = lax.axis_index("vec")
@@ -496,6 +502,9 @@
             dn[8 * leaf : 8 * leaf + 8, :].astype(bf16), bases[leaf]
         )
 
+    for copy in copies[2:]:
+        copy.wait()
+
     @pl.when(core == 0)
     def _():
         tree[:, :HALF] += near_mine[...]
@@ -511,7 +520,7 @@
     for b in range(COLS // width):
         cols = slice(b * width, (b + 1) * width)
         index = perm[:, cols]
-        select = hot(iota((256, width), 0) == (index & 255))
+        select = hot_rows(index & 255, width)
         high = jnp.broadcast_to(lax.shift_right_logical(index, 8), (8, width))
         values = tree[:, cols]
         spread = jnp.concatenate(
@@ -592,7 +601,7 @@
     (begun,) = call(
         near_first_kernel,
         [((16, LEAF * (10 - SPLIT)), f32)],
-        buffers + [pltpu.SemaphoreType.DMA((5,))],
+        buffers + [pltpu.SemaphoreType.DMA((10 - SPLIT,))],
         (vt, pt, rec_c), "aaa>h",
         2 * 37 * 512 * 512 * 256, 1 << 20, vmem=24,
     )

time: 58.2 us -> 57.1 us (0.981); the launches traced: 57.8 us -> 56.2 us
  Pallas kernels: 32 us -> 30 us
    pallas_call x9, Pallas kernels: 32 us -> 30 us  [call(): pl.pallas_call(kernel, out_shape=[pltpu.HBM(s, d) if k == 'h' else jax.Sh...]
  transfers between devices with their start and end apart: 5 -> 5, of which waited for: 2 -> 3; matrix products, arithmetic and copies ran while one was open for 0% -> 0% of each run, Pallas kernels for 31% -> 32%
where the time goes in v8:
time: 57.1 us; the launch traced here: 56.2 us
  Pallas kernels  30 us (53%)
  starting transfers between devices  20.9 us (37%)
  waiting for transfers between devices  4.8 us (8%)
    pallas_call x9, Pallas kernels, call(): pl.pallas_call(kernel, out_shape=[pltpu.HBM(s, d) if k == 'h' else jax.Sh...  30 us
    all_to_all x2, starting transfers between devices, shards(): lax.all_to_all(send, 'leaf', split_axis=0, concat_axis=0, tiled=True, axi...  15.5 us
    ppermute x1, starting transfers between devices, shards(): halo = lax.ppermute(halo, axes, pairs_a)  5.27 us
    all_to_all x2, waiting for transfers between devices, shards(): lax.all_to_all(send, 'leaf', split_axis=0, concat_axis=0, tiled=True, axi...  3.46 us
    ppermute x1, waiting for transfers between devices, shards(): near_other = lax.ppermute(near_send, axes, pairs_c)  1.33 us
  transfers between devices with their start and end apart: 5, of which 3 were waited for; matrix products, arithmetic and copies ran while one was open for 0% of the time, Pallas kernels for 32%

profile of v8, /device:TPU:8, one launch (start us, length us, event | category | flops | bytes accessed | tf_op | source)
XLA Modules:
  0.0 56.2 jit_solution(3685524242681146456)
XLA Ops:
  0.0 2.9 %shard_map.109 = (bf16[8,8192]{1,0:T(8,128)(2,1)S(1)}, bf16[8,8192]{1,0:T(8,128)(2,1)S(1)}, bf16[8,5120]{1,0:T(8,128)(2,1)S(1)}) custom-call(bf16[3,8192]{1,0:T(4,128)(2,1)} %pts_in.1, bf16[8,8192]{1,0:T(8,128)(2,1)} %vec_in.1, s32[1,8192]{1,0:T(1,128)} %perm_in.3), custom_call_target="tpu_custom_call" | custom-call | flops 1610612736 | bytes 1048576 | tf_op jit(solution)/shard_map/pallas_call | solution.py:69
  2.9 0.0 copy-start.3
  2.9 0.0 copy-start.4
  3.0 0.1 collective-permute-start
  3.1 0.0 copy-start.1
  3.1 0.0 copy-start.5
  3.1 0.0 copy-start.6
  3.1 0.0 copy-start.7
  3.1 1.7 %shard_map.110.mats.mats_in = bf16[2560,64]{1,0:T(8,128)(2,1)S(1)} custom-call(bf16[64,64,254]{2,1,0:T(8,128)(2,1)S(1)} %bitcast.11), custom_call_target="tpu_custom_call" | custom-call | flops 83886080 | bytes 3145728 | tf_op jit(solution)/shard_map/pallas_call | solution.py:69
  4.8 1.5 %shard_map.111 = (f32[256,128]{1,0:T(8,128)S(1)}, f32[32,64]{1,0:T(8,128)S(1)}, bf16[24,1024]{1,0:T(8,128)(2,1)S(1)}) custom-call(bf16[8,8192]{1,0:T(8,128)(2,1)S(1)} %get-tuple-element.13.vt.vt_in, bf16[8,8192]{1,0:T(8,128)(2,1)S(1)} %get-tuple-element.14.pt.pt_in, bf16[8,5120]{1,0:T(8,128)(2,1)S(1)} %collective-permute-done.rec_c.c_in, ...), custom_call_target="tpu_custom_call" | custom-call | flops 134217728 | bytes 2097152 | tf_op jit(solution)/shard_map/pallas_call | solution.py:69
  6.4 0.0 copy-done.6
  6.4 3.8 %shard_map.112.seen = bf16[512,640]{1,0:T(8,128)(2,1)} custom-call(f32[256,128]{1,0:T(8,128)S(1)} %get-tuple-element.16.cf, f32[32,64]{1,0:T(8,128)S(1)} %get-tuple-element.17.path.path_in, bf16[64,64,256]{2,1,0:T(8,128)(2,1)S(1)} %bitcast.12, s32[1,256]{1,0:T(1,128)S(1)} %bitcast.15, s32[1,256]{1,0:T(1,128)S(1)} %bitcast.16, s32[1,256]{1,0:T(1,128)S(1)} %bitcast.17), custom_call_target="tpu_custom_call" | custom-call | flops 167772160 | bytes 4194304 | tf_op jit(solution)/shard_map/pallas_call | solution.py:69
  10.2 7.4 %all-to-all-start = ((bf16[16,32,640]{2,1,0:T(8,128)(2,1)}), bf16[16,32,640]{2,1,0:T(8,128)(2,1)S(1)}, u32[]{:S(2)}, u32[]{:S(2)}) async-start(bf16[16,32,640]{2,1,0:T(8,128)(2,1)} %bitcast.5), calls=%async_computation | async-start | bytes 1310720 | tf_op jit(solution)/shard_map/all_to_all | solution.py:586
  17.6 5.3 %collective-permute-start.1 = (bf16[24,1024]{1,0:T(8,128)(2,1)S(1)}, bf16[24,1024]{1,0:T(8,128)(2,1)S(1)}, u32[]{:S(2)}, u32[]{:S(2)}) collective-permute-start(bf16[24,1024]{1,0:T(8,128)(2,1)S(1)} %get-tuple-element.18), channel_id=1, source_target_pairs={{0,255},{255,0},{1,2},{2,1},{3,4},{4,3},{5,6},{6,5},{7,8},{8,7},{9... | collective-permute-start | bytes 147464 | tf_op jit(solution)/shard_map/ppermute | solution.py:573
  22.9 4.1 %shard_map.115.begun = f32[16,1536]{1,0:T(8,128)} custom-call(bf16[8,8192]{1,0:T(8,128)(2,1)S(1)} %get-tuple-element.13.vt.vt_in, bf16[8,8192]{1,0:T(8,128)(2,1)S(1)} %get-tuple-element.14.pt.pt_in, bf16[8,5120]{1,0:T(8,128)(2,1)S(1)} %collective-permute-done.rec_c.c_in), custom_call_target="tpu_custom_call" | custom-call | flops 4966055936 | bytes 1048576 | tf_op jit(solution)/shard_map/pallas_call | solution.py:69
  27.0 1.3 %shard_map.113.coup_in = bf16[512,64]{1,0:T(8,128)(2,1)S(1)} custom-call(bf16[64,64,254]{2,1,0:T(8,128)(2,1)S(1)} %bitcast.13, bf16[512,640]{1,0:T(8,128)(2,1)} %shard_map.112.seen), custom_call_target="tpu_custom_call" | custom-call | flops 16777216 | bytes 3145728 | tf_op jit(solution)/shard_map/pallas_call | solution.py:69
  28.3 2.0 %all-to-all-done = bf16[16,32,640]{2,1,0:T(8,128)(2,1)S(1)} async-done(((bf16[16,32,640]{2,1,0:T(8,128)(2,1)}), bf16[16,32,640]{2,1,0:T(8,128)(2,1)S(1)}, u32[]{:S(2)}, u32[]{:S(2)}) %all-to-all-start) | async-done | bytes 655392 | tf_op jit(solution)/shard_map/all_to_all | solution.py:586
  30.3 3.3 %shard_map.114 = bf16[256,512]{1,0:T(8,128)(2,1)} custom-call(bf16[512,640]{1,0:T(8,128)(2,1)S(1)} %bitcast.10, f32[32,64]{1,0:T(8,128)S(1)} %get-tuple-element.17.path.path_in, bf16[2560,64]{1,0:T(8,128)(2,1)S(1)} %shard_map.110.mats.mats_in, bf16[512,64]{1,0:T(8,128)(2,1)S(1)} %shard_map.113.coup_in), custom_call_target="tpu_custom_call" | custom-call | flops 134217728 | bytes 2097152 | tf_op jit(solution)/shard_map/pallas_call | solution.py:69
  33.6 8.1 %all-to-all-start.1 = ((bf16[8,32,512]{2,1,0:T(8,128)(2,1)}), bf16[8,32,512]{2,1,0:T(8,128)(2,1)S(1)}, u32[]{:S(2)}, u32[]{:S(2)}) async-start(bf16[8,32,512]{2,1,0:T(8,128)(2,1)} %bitcast.8), calls=%async_computation.1 | async-start | bytes 524288 | tf_op jit(solution)/shard_map/all_to_all | solution.py:620
  41.7 7.6 %shard_map.116 = (f32[8,4096]{1,0:T(8,128)S(1)}, f32[8,4096]{1,0:T(8,128)S(1)}) custom-call(bf16[8,8192]{1,0:T(8,128)(2,1)S(1)} %get-tuple-element.13.vt.vt_in, bf16[8,8192]{1,0:T(8,128)(2,1)S(1)} %get-tuple-element.14.pt.pt_in, bf16[8,5120]{1,0:T(8,128)(2,1)S(1)} %collective-permute-done.rec_c.c_in, bf16[24,1024]{1,0:T(8,128)(2,1)S(1)} %collective-permute-done.1.halo_in, ...), custom_call_target="tpu_custom_call" | custom-call | flops 4026531840 | bytes 1048576 | tf_op jit(solution)/shard_map/pallas_call | solution.py:69
  49.3 0.1 collective-permute-start.2
  49.4 1.3 %collective-permute-done.2.other_in = f32[8,4096]{1,0:T(8,128)S(1)} collective-permute-done((f32[8,4096]{1,0:T(8,128)S(1)}, f32[8,4096]{1,0:T(8,128)S(1)}, u32[]{:S(2)}, u32[]{:S(2)}) %collective-permute-start.2) | collective-permute-done | bytes 131104 | tf_op jit(solution)/shard_map/ppermute | solution.py:630
  50.7 1.5 %all-to-all-done.1 = bf16[8,32,512]{2,1,0:T(8,128)(2,1)S(1)} async-done(((bf16[8,32,512]{2,1,0:T(8,128)(2,1)}), bf16[8,32,512]{2,1,0:T(8,128)(2,1)S(1)}, u32[]{:S(2)}, u32[]{:S(2)}) %all-to-all-start.1) | async-done | bytes 262176 | tf_op jit(solution)/shard_map/all_to_all | solution.py:620
  52.2 3.8 %shard_map.117 = bf16[8,8192]{1,0:T(8,128)(2,1)} custom-call(bf16[256,512]{1,0:T(8,128)(2,1)S(1)} %bitcast.14, f32[8,4096]{1,0:T(8,128)S(1)} %get-tuple-element.19.mine_in, f32[8,4096]{1,0:T(8,128)S(1)} %collective-permute-done.2.other_in, bf16[2560,64]{1,0:T(8,128)(2,1)S(1)} %shard_map.110.mats.mats_in, bf16[30,64,64]{2,1,0:T(8,128)(2,1)S(1)} %copy-done.4, ...), custom_call_target="tpu_custom_call" | custom-call | flops 1073741824 | bytes 8388608 | tf_op jit(solution)/shard_map/pallas_call | solution.py:69
  (11 shorter events, 0.0 us)
Async XLA Ops:
  0.0 3.1 %copy-start = (bf16[254,64,64]{0,2,1:T(8,128)(2,1)S(1)}, bf16[254,64,64]{0,2,1:T(8,128)(2,1)}, u32[]{:S(2)}) copy-start(bf16[254,64,64]{0,2,1:T(8,128)(2,1)} %param.20) | copy-start | bytes 6242308
  2.9 1.9 %copy-start.3 = (bf16[16,64,512]{2,1,0:T(8,128)(2,1)S(1)}, bf16[16,64,512]{2,1,0:T(8,128)(2,1)}, u32[]{:S(2)}) copy-start(bf16[16,64,512]{2,1,0:T(8,128)(2,1)} %bases.3) | copy-start | bytes 3145732
  2.9 1.9 %copy-start.4 = (bf16[30,64,64]{2,1,0:T(8,128)(2,1)S(1)}, bf16[30,64,64]{2,1,0:T(8,128)(2,1)}, u32[]{:S(2)}) copy-start(bf16[30,64,64]{2,1,0:T(8,128)(2,1)} %tr.3) | copy-start | bytes 737284
  3.0 1.8 %collective-permute-start = (bf16[8,5120]{1,0:T(8,128)(2,1)S(1)}, bf16[8,5120]{1,0:T(8,128)(2,1)S(1)}, u32[]{:S(2)}, u32[]{:S(2)}) collective-permute-start(bf16[8,5120]{1,0:T(8,128)(2,1)S(1)} %get-tuple-element.15), channel_id=1, source_target_pairs={{0,1},{1,0},{2,3},{3,2},{4,5},{5,4},{6,7},{7,6},{8,9},{9,8},{10,11... | collective-permute-start | bytes 245768 | tf_op jit(solution)/shard_map/ppermute | solution.py:556
  3.1 3.3 %copy-start.1 = (bf16[256,64,64]{0,2,1:T(8,128)(2,1)S(1)}, bf16[256,64,64]{0,2,1:T(8,128)(2,1)}, u32[]{:S(2)}) copy-start(bf16[256,64,64]{0,2,1:T(8,128)(2,1)} %param.16) | copy-start | bytes 6291460
  3.1 3.3 %copy-start.5 = (s32[256]{0:T(256)S(1)}, s32[256]{0:T(256)}, u32[]{:S(2)}) copy-start(s32[256]{0:T(256)} %param.17) | copy-start | bytes 3076
  3.1 3.3 %copy-start.6 = (s32[256,1]{0,1:T(1,128)S(1)}, s32[256,1]{0,1:T(1,128)}, u32[]{:S(2)}) copy-start(s32[256,1]{0,1:T(1,128)} %param.18) | copy-start | bytes 3076
  3.1 3.3 %copy-start.7 = (s32[256]{0:T(256)S(1)}, s32[256]{0:T(256)}, u32[]{:S(2)}) copy-start(s32[256]{0:T(256)} %param.19) | copy-start | bytes 3076
  10.2 20.1 %all-to-all-start = ((bf16[16,32,640]{2,1,0:T(8,128)(2,1)}), bf16[16,32,640]{2,1,0:T(8,128)(2,1)S(1)}, u32[]{:S(2)}, u32[]{:S(2)}) async-start(bf16[16,32,640]{2,1,0:T(8,128)(2,1)} %bitcast.5), calls=%async_computation | async-start | bytes 1310720 | tf_op jit(solution)/shard_map/all_to_all | solution.py:586
  17.6 9.4 %copy-start.2 = (bf16[254,64,64]{0,2,1:T(8,128)(2,1)S(1)}, bf16[254,64,64]{0,2,1:T(8,128)(2,1)}, u32[]{:S(2)}) copy-start(bf16[254,64,64]{0,2,1:T(8,128)(2,1)} %param.21) | copy-start | bytes 6242308
  17.6 24.1 %collective-permute-start.1 = (bf16[24,1024]{1,0:T(8,128)(2,1)S(1)}, bf16[24,1024]{1,0:T(8,128)(2,1)S(1)}, u32[]{:S(2)}, u32[]{:S(2)}) collective-permute-start(bf16[24,1024]{1,0:T(8,128)(2,1)S(1)} %get-tuple-element.18), channel_id=1, source_target_pairs={{0,255},{255,0},{1,2},{2,1},{3,4},{4,3},{5,6},{6,5},{7,8},{8,7},{9... | collective-permute-start | bytes 147464 | tf_op jit(solution)/shard_map/ppermute | solution.py:573
  33.6 18.6 %all-to-all-start.1 = ((bf16[8,32,512]{2,1,0:T(8,128)(2,1)}), bf16[8,32,512]{2,1,0:T(8,128)(2,1)S(1)}, u32[]{:S(2)}, u32[]{:S(2)}) async-start(bf16[8,32,512]{2,1,0:T(8,128)(2,1)} %bitcast.8), calls=%async_computation.1 | async-start | bytes 524288 | tf_op jit(solution)/shard_map/all_to_all | solution.py:620
  49.3 1.4 %collective-permute-start.2 = (f32[8,4096]{1,0:T(8,128)S(1)}, f32[8,4096]{1,0:T(8,128)S(1)}, u32[]{:S(2)}, u32[]{:S(2)}) collective-permute-start(f32[8,4096]{1,0:T(8,128)S(1)} %get-tuple-element.20), channel_id=1, source_target_pairs={{0,1},{1,0},{2,3},{3,2},{4,5},{5,4},{6,7},{7,6},{8,9},{9,8},{10,11... | collective-permute-start | bytes 393224 | tf_op jit(solution)/shard_map/ppermute | solution.py:630

commit v9 on v8

--- a/solution.py
+++ b/solution.py
@@ -206,18 +206,18 @@
         same = jnp.where((column == row) & before, 1.0, 0.0)
         ranks.append(jnp.sum(same, axis=0, keepdims=True))
     place = owner * 4 + jnp.concatenate(ranks, axis=1).astype(i32)
-    top = path[24:32, :]
-    high = top.astype(bf16).astype(f32)
-    extra = jnp.concatenate([high, top - high, jnp.zeros((16, 64), f32)], axis=0)
-    extra = wide(extra)
+    group = lax.shift_right_logical(place, 3) & 3
+    slot_row = lax.shift_right_logical(place, 5) * 8 + (place & 7)
     payload = prod[...]
-    for part in range(2):
-        rows = slice(256 * part, 256 * part + 256)
-        slots = hot(iota((256, 256), 0) + 256 * part == place)
+    lane_group = lax.shift_right_logical(iota((128, 128), 1) - 64, 4)
+    tail = jnp.zeros((128, 128), f32)
+    for g in range(4):
+        slots = hot((iota((128, 256), 0) == slot_row) & (group == g))
         out = dot(slots, payload, NT)
-        send[rows, 0:512] = out[:, :512].astype(bf16)
-        tail = out[:, 512:].reshape(8, 32, 128) + extra[None]
-        send[rows, 512:640] = tail.reshape(256, 128).astype(bf16)
+        send[:, 512 * g : 512 * g + 512] = out[:, :512].astype(bf16)
+        tail = jnp.where(lane_group == g, out[:, 512:], tail)
+    tail = tail.reshape(16, 8, 128) + wide(path[24:32, :])[None]
+    send[:, 2048:2176] = tail.reshape(128, 128).astype(bf16)
 
 
 def split3(x):
@@ -280,7 +280,7 @@
     acc[:, leaf_cols(t - 2)] += total
 
 
-SPLIT = 7
+SPLIT = 6
 
 
 def near_first_kernel(
@@ -383,24 +383,24 @@
 
 
 def middle_kernel(
-    recv_in, path_in, mats_in, coup_in, send, recv, path, mats, coup, ext, xs, gain, sems
+    recv_in, path_in, mats_in, coup_in, send, recv, path, mats, coup, xs, gain, sems
 ):
     device = lax.axis_index("leaf")
     copies = fetch(sems, (recv_in, recv), (mats_in, mats), (coup_in, coup), (path_in, path))
     copies[0].wait()
-    ext[...] = recv[:, 512:640].astype(f32)
-
-    labels = jnp.concatenate(
-        [jnp.transpose(ext[128 * i : 128 * i + 128, :])[64:65, :] for i in range(4)], axis=1
-    )
-    row, lane = iota((256, 512), 0), iota((256, 512), 1)
+    ext = recv[:, 2048:2176].astype(f32)
+
+    turned = jnp.transpose(ext)
+    row, lane = iota((64, 128), 0), iota((64, 128), 1)
     wanted = ((row & 31) + 1).astype(f32)
-    fits = lax.shift_right_logical(row, 5) == (lax.shift_right_logical(lane, 2) & 7)
-    sums = dot(hot((labels == wanted) & fits), recv[:, 0:512])
-
-    for g in range(16):
-        rows = ext[32 * g : 32 * g + 16, :64]
-        xs[8 * g : 8 * g + 8, :] = rows[:8] + rows[8:]
+    fits = lax.shift_right_logical(row, 5) == (lax.shift_right_logical(lane, 2) & 1)
+    sums = []
+    for g in range(4):
+        label = turned[64 + 16 * g : 65 + 16 * g, :]
+        picked = dot(hot((label == wanted) & fits), recv[:, 512 * g : 512 * g + 512])
+        sums += [picked[:32], picked[32:]]
+
+    xs[0:128, :] = ext[:, :64]
     first, n = 0, 16
     firsts = {3: 0}
     for copy in copies[1:]:
@@ -443,7 +443,7 @@
         line = jnp.where(x == 0, own_line, lines[0])
         line = jnp.where(x >= 2, lines[1], line)
         line = jnp.where(x >= 4, lines[2], line)
-        block = jnp.where(last, line, sums[32 * peer : 32 * peer + 32])
+        block = jnp.where(last, line, sums[peer])
         send[32 * peer : 32 * peer + 32, :] = block.astype(bf16)
 
 
@@ -573,7 +573,7 @@
     halo = lax.ppermute(halo, axes, pairs_a)
     (send,) = call(
         product_kernel,
-        [((512, 640), bf16)],
+        [((128, 2176), bf16)],
         [pltpu.VMEM((1024, 128), f32), pltpu.VMEM((640, 256), bf16)],
         (
             cf, path, jnp.transpose(coupling_blocks, (1, 2, 0)),
@@ -609,10 +609,9 @@
         middle_kernel,
         [((256, 512), bf16)],
         [
-            pltpu.VMEM((512, 640), bf16), pltpu.VMEM((32, 64), f32),
+            pltpu.VMEM((128, 2176), bf16), pltpu.VMEM((32, 64), f32),
             pltpu.VMEM((64 * T_ROWS, 64), bf16), pltpu.VMEM((64 * C_ROWS, 64), bf16),
-            pltpu.VMEM((512, 128), f32), pltpu.VMEM((256, 64), f32), pltpu.VMEM((56, 64), f32),
-            pltpu.SemaphoreType.DMA((4,)),
+            pltpu.VMEM((256, 64), f32), pltpu.VMEM((56, 64), f32), pltpu.SemaphoreType.DMA((4,)),
         ],
         (recv, path, mats, coup), "aaaa>v",
         2 * 256 * 512 * 512, 2 << 20,

time: 57.1 us -> 55.2 us (0.967); the launches traced: 56.2 us -> 54.9 us
  waiting for transfers between devices: 4.8 us -> 3.84 us
    all_to_all x2, waiting for transfers between devices: 3.46 us -> 2.5 us  [shards(): lax.all_to_all(send, 'leaf', split_axis=0, concat_axis=0, tiled=True, axi...]
  transfers between devices with their start and end apart: 5 -> 5, of which waited for: 3 -> 2; matrix products, arithmetic and copies ran while one was open for 0% -> 0% of each run, Pallas kernels for 32% -> 32%
where the time goes in v9:
time: 55.2 us; the launch traced here: 54.9 us
  Pallas kernels  30 us (54%)
  starting transfers between devices  20.6 us (37%)
  waiting for transfers between devices  3.84 us (7%)
    pallas_call x9, Pallas kernels, call(): pl.pallas_call(kernel, out_shape=[pltpu.HBM(s, d) if k == 'h' else jax.Sh...  30 us
    all_to_all x2, starting transfers between devices, shards(): lax.all_to_all(send, 'leaf', split_axis=0, concat_axis=0, tiled=True, axi...  15.2 us
    ppermute x1, starting transfers between devices, shards(): halo = lax.ppermute(halo, axes, pairs_a)  5.27 us
    all_to_all x2, waiting for transfers between devices, shards(): lax.all_to_all(send, 'leaf', split_axis=0, concat_axis=0, tiled=True, axi...  2.5 us
    ppermute x1, waiting for transfers between devices, shards(): near_other = lax.ppermute(near_send, axes, pairs_c)  1.33 us
  transfers between devices with their start and end apart: 5, of which 2 were waited for; matrix products, arithmetic and copies ran while one was open for 0% of the time, Pallas kernels for 32%

profile of v9, /device:TPU:8, one launch (start us, length us, event | category | flops | bytes accessed | tf_op | source)
XLA Modules:
  0.0 54.9 jit_solution(2667328375494980573)
XLA Ops:
  0.0 2.9 %shard_map.109 = (bf16[8,8192]{1,0:T(8,128)(2,1)S(1)}, bf16[8,8192]{1,0:T(8,128)(2,1)S(1)}, bf16[8,5120]{1,0:T(8,128)(2,1)S(1)}) custom-call(bf16[3,8192]{1,0:T(4,128)(2,1)} %pts_in.1, bf16[8,8192]{1,0:T(8,128)(2,1)} %vec_in.1, s32[1,8192]{1,0:T(1,128)} %perm_in.3), custom_call_target="tpu_custom_call" | custom-call | flops 1610612736 | bytes 1048576 | tf_op jit(solution)/shard_map/pallas_call | solution.py:69
  2.9 0.0 copy-start.3
  2.9 0.0 copy-start.4
  3.0 0.1 collective-permute-start
  3.1 0.0 copy-start.1
  3.1 0.0 copy-start.5
  3.1 0.0 copy-start.6
  3.1 0.0 copy-start.7
  3.1 1.7 %shard_map.110.mats.mats_in = bf16[2560,64]{1,0:T(8,128)(2,1)S(1)} custom-call(bf16[64,64,254]{2,1,0:T(8,128)(2,1)S(1)} %bitcast.11), custom_call_target="tpu_custom_call" | custom-call | flops 83886080 | bytes 3145728 | tf_op jit(solution)/shard_map/pallas_call | solution.py:69
  4.8 1.5 %shard_map.111 = (f32[256,128]{1,0:T(8,128)S(1)}, f32[32,64]{1,0:T(8,128)S(1)}, bf16[24,1024]{1,0:T(8,128)(2,1)S(1)}) custom-call(bf16[8,8192]{1,0:T(8,128)(2,1)S(1)} %get-tuple-element.13.vt.vt_in, bf16[8,8192]{1,0:T(8,128)(2,1)S(1)} %get-tuple-element.14.pt.pt_in, bf16[8,5120]{1,0:T(8,128)(2,1)S(1)} %collective-permute-done.rec_c.c_in, ...), custom_call_target="tpu_custom_call" | custom-call | flops 134217728 | bytes 2097152 | tf_op jit(solution)/shard_map/pallas_call | solution.py:69
  6.4 0.0 copy-done.6
  6.4 3.9 %shard_map.112.seen = bf16[128,2176]{1,0:T(8,128)(2,1)} custom-call(f32[256,128]{1,0:T(8,128)S(1)} %get-tuple-element.16.cf, f32[32,64]{1,0:T(8,128)S(1)} %get-tuple-element.17.path.path_in, bf16[64,64,256]{2,1,0:T(8,128)(2,1)S(1)} %bitcast.12, s32[1,256]{1,0:T(1,128)S(1)} %bitcast.15, s32[1,256]{1,0:T(1,128)S(1)} %bitcast.16, s32[1,256]{1,0:T(1,128)S(1)} %bitcast.17), custom_call_target="tpu_custom_call" | custom-call | flops 167772160 | bytes 4194304 | tf_op jit(solution)/shard_map/pallas_call | solution.py:69
  10.3 7.4 %all-to-all-start = ((bf16[16,8,2176]{2,1,0:T(8,128)(2,1)}), bf16[16,8,2176]{2,1,0:T(8,128)(2,1)S(1)}, u32[]{:S(2)}, u32[]{:S(2)}) async-start(bf16[16,8,2176]{2,1,0:T(8,128)(2,1)} %bitcast.5), calls=%async_computation | async-start | bytes 1114112 | tf_op jit(solution)/shard_map/all_to_all | solution.py:586
  17.7 5.3 %collective-permute-start.1 = (bf16[24,1024]{1,0:T(8,128)(2,1)S(1)}, bf16[24,1024]{1,0:T(8,128)(2,1)S(1)}, u32[]{:S(2)}, u32[]{:S(2)}) collective-permute-start(bf16[24,1024]{1,0:T(8,128)(2,1)S(1)} %get-tuple-element.18), channel_id=1, source_target_pairs={{0,255},{255,0},{1,2},{2,1},{3,4},{4,3},{5,6},{6,5},{7,8},{8,7},{9... | collective-permute-start | bytes 147464 | tf_op jit(solution)/shard_map/ppermute | solution.py:573
  23.0 5.1 %shard_map.115.begun = f32[16,2048]{1,0:T(8,128)} custom-call(bf16[8,8192]{1,0:T(8,128)(2,1)S(1)} %get-tuple-element.13.vt.vt_in, bf16[8,8192]{1,0:T(8,128)(2,1)S(1)} %get-tuple-element.14.pt.pt_in, bf16[8,5120]{1,0:T(8,128)(2,1)S(1)} %collective-permute-done.rec_c.c_in), custom_call_target="tpu_custom_call" | custom-call | flops 4966055936 | bytes 1048576 | tf_op jit(solution)/shard_map/pallas_call | solution.py:69
  28.1 1.3 %shard_map.113.coup_in = bf16[512,64]{1,0:T(8,128)(2,1)S(1)} custom-call(bf16[64,64,254]{2,1,0:T(8,128)(2,1)S(1)} %bitcast.13, bf16[128,2176]{1,0:T(8,128)(2,1)} %shard_map.112.seen), custom_call_target="tpu_custom_call" | custom-call | flops 16777216 | bytes 3145728 | tf_op jit(solution)/shard_map/pallas_call | solution.py:69
  29.5 0.0 all-to-all-done
  29.5 3.1 %shard_map.114 = bf16[256,512]{1,0:T(8,128)(2,1)} custom-call(bf16[128,2176]{1,0:T(8,128)(2,1)S(1)} %bitcast.10, f32[32,64]{1,0:T(8,128)S(1)} %get-tuple-element.17.path.path_in, bf16[2560,64]{1,0:T(8,128)(2,1)S(1)} %shard_map.110.mats.mats_in, bf16[512,64]{1,0:T(8,128)(2,1)S(1)} %shard_map.113.coup_in), custom_call_target="tpu_custom_call" | custom-call | flops 134217728 | bytes 2097152 | tf_op jit(solution)/shard_map/pallas_call | solution.py:69
  32.6 7.8 %all-to-all-start.1 = ((bf16[8,32,512]{2,1,0:T(8,128)(2,1)}), bf16[8,32,512]{2,1,0:T(8,128)(2,1)S(1)}, u32[]{:S(2)}, u32[]{:S(2)}) async-start(bf16[8,32,512]{2,1,0:T(8,128)(2,1)} %bitcast.8), calls=%async_computation.1 | async-start | bytes 524288 | tf_op jit(solution)/shard_map/all_to_all | solution.py:619
  40.4 6.5 %shard_map.116 = (f32[8,4096]{1,0:T(8,128)S(1)}, f32[8,4096]{1,0:T(8,128)S(1)}) custom-call(bf16[8,8192]{1,0:T(8,128)(2,1)S(1)} %get-tuple-element.13.vt.vt_in, bf16[8,8192]{1,0:T(8,128)(2,1)S(1)} %get-tuple-element.14.pt.pt_in, bf16[8,5120]{1,0:T(8,128)(2,1)S(1)} %collective-permute-done.rec_c.c_in, bf16[24,1024]{1,0:T(8,128)(2,1)S(1)} %collective-permute-done.1.halo_in, ...), custom_call_target="tpu_custom_call" | custom-call | flops 4026531840 | bytes 1048576 | tf_op jit(solution)/shard_map/pallas_call | solution.py:69
  47.0 0.1 collective-permute-start.2
  47.1 1.3 %collective-permute-done.2.other_in = f32[8,4096]{1,0:T(8,128)S(1)} collective-permute-done((f32[8,4096]{1,0:T(8,128)S(1)}, f32[8,4096]{1,0:T(8,128)S(1)}, u32[]{:S(2)}, u32[]{:S(2)}) %collective-permute-start.2) | collective-permute-done | bytes 131104 | tf_op jit(solution)/shard_map/ppermute | solution.py:629
  48.4 2.5 %all-to-all-done.1 = bf16[8,32,512]{2,1,0:T(8,128)(2,1)S(1)} async-done(((bf16[8,32,512]{2,1,0:T(8,128)(2,1)}), bf16[8,32,512]{2,1,0:T(8,128)(2,1)S(1)}, u32[]{:S(2)}, u32[]{:S(2)}) %all-to-all-start.1) | async-done | bytes 262176 | tf_op jit(solution)/shard_map/all_to_all | solution.py:619
  50.9 3.8 %shard_map.117 = bf16[8,8192]{1,0:T(8,128)(2,1)} custom-call(bf16[256,512]{1,0:T(8,128)(2,1)S(1)} %bitcast.14, f32[8,4096]{1,0:T(8,128)S(1)} %get-tuple-element.19.mine_in, f32[8,4096]{1,0:T(8,128)S(1)} %collective-permute-done.2.other_in, bf16[2560,64]{1,0:T(8,128)(2,1)S(1)} %shard_map.110.mats.mats_in, bf16[30,64,64]{2,1,0:T(8,128)(2,1)S(1)} %copy-done.4, ...), custom_call_target="tpu_custom_call" | custom-call | flops 1073741824 | bytes 8388608 | tf_op jit(solution)/shard_map/pallas_call | solution.py:69
  (11 shorter events, 0.0 us)
Async XLA Ops:
  0.0 3.1 %copy-start = (bf16[254,64,64]{0,2,1:T(8,128)(2,1)S(1)}, bf16[254,64,64]{0,2,1:T(8,128)(2,1)}, u32[]{:S(2)}) copy-start(bf16[254,64,64]{0,2,1:T(8,128)(2,1)} %param.20) | copy-start | bytes 6242308
  2.9 1.9 %copy-start.3 = (bf16[16,64,512]{2,1,0:T(8,128)(2,1)S(1)}, bf16[16,64,512]{2,1,0:T(8,128)(2,1)}, u32[]{:S(2)}) copy-start(bf16[16,64,512]{2,1,0:T(8,128)(2,1)} %bases.3) | copy-start | bytes 3145732
  2.9 1.9 %copy-start.4 = (bf16[30,64,64]{2,1,0:T(8,128)(2,1)S(1)}, bf16[30,64,64]{2,1,0:T(8,128)(2,1)}, u32[]{:S(2)}) copy-start(bf16[30,64,64]{2,1,0:T(8,128)(2,1)} %tr.3) | copy-start | bytes 737284
  3.0 1.8 %collective-permute-start = (bf16[8,5120]{1,0:T(8,128)(2,1)S(1)}, bf16[8,5120]{1,0:T(8,128)(2,1)S(1)}, u32[]{:S(2)}, u32[]{:S(2)}) collective-permute-start(bf16[8,5120]{1,0:T(8,128)(2,1)S(1)} %get-tuple-element.15), channel_id=1, source_target_pairs={{0,1},{1,0},{2,3},{3,2},{4,5},{5,4},{6,7},{7,6},{8,9},{9,8},{10,11... | collective-permute-start | bytes 245768 | tf_op jit(solution)/shard_map/ppermute | solution.py:556
  3.1 3.3 %copy-start.1 = (bf16[256,64,64]{0,2,1:T(8,128)(2,1)S(1)}, bf16[256,64,64]{0,2,1:T(8,128)(2,1)}, u32[]{:S(2)}) copy-start(bf16[256,64,64]{0,2,1:T(8,128)(2,1)} %param.16) | copy-start | bytes 6291460
  3.1 3.3 %copy-start.5 = (s32[256]{0:T(256)S(1)}, s32[256]{0:T(256)}, u32[]{:S(2)}) copy-start(s32[256]{0:T(256)} %param.17) | copy-start | bytes 3076
  3.1 3.3 %copy-start.6 = (s32[256,1]{0,1:T(1,128)S(1)}, s32[256,1]{0,1:T(1,128)}, u32[]{:S(2)}) copy-start(s32[256,1]{0,1:T(1,128)} %param.18) | copy-start | bytes 3076
  3.1 3.3 %copy-start.7 = (s32[256]{0:T(256)S(1)}, s32[256]{0:T(256)}, u32[]{:S(2)}) copy-start(s32[256]{0:T(256)} %param.19) | copy-start | bytes 3076
  10.3 19.2 %all-to-all-start = ((bf16[16,8,2176]{2,1,0:T(8,128)(2,1)}), bf16[16,8,2176]{2,1,0:T(8,128)(2,1)S(1)}, u32[]{:S(2)}, u32[]{:S(2)}) async-start(bf16[16,8,2176]{2,1,0:T(8,128)(2,1)} %bitcast.5), calls=%async_computation | async-start | bytes 1114112 | tf_op jit(solution)/shard_map/all_to_all | solution.py:586
  17.7 10.4 %copy-start.2 = (bf16[254,64,64]{0,2,1:T(8,128)(2,1)S(1)}, bf16[254,64,64]{0,2,1:T(8,128)(2,1)}, u32[]{:S(2)}) copy-start(bf16[254,64,64]{0,2,1:T(8,128)(2,1)} %param.21) | copy-start | bytes 6242308
  17.7 22.7 %collective-permute-start.1 = (bf16[24,1024]{1,0:T(8,128)(2,1)S(1)}, bf16[24,1024]{1,0:T(8,128)(2,1)S(1)}, u32[]{:S(2)}, u32[]{:S(2)}) collective-permute-start(bf16[24,1024]{1,0:T(8,128)(2,1)S(1)} %get-tuple-element.18), channel_id=1, source_target_pairs={{0,255},{255,0},{1,2},{2,1},{3,4},{4,3},{5,6},{6,5},{7,8},{8,7},{9... | collective-permute-start | bytes 147464 | tf_op jit(solution)/shard_map/ppermute | solution.py:573
  32.6 18.3 %all-to-all-start.1 = ((bf16[8,32,512]{2,1,0:T(8,128)(2,1)}), bf16[8,32,512]{2,1,0:T(8,128)(2,1)S(1)}, u32[]{:S(2)}, u32[]{:S(2)}) async-start(bf16[8,32,512]{2,1,0:T(8,128)(2,1)} %bitcast.8), calls=%async_computation.1 | async-start | bytes 524288 | tf_op jit(solution)/shard_map/all_to_all | solution.py:619
  47.0 1.4 %collective-permute-start.2 = (f32[8,4096]{1,0:T(8,128)S(1)}, f32[8,4096]{1,0:T(8,128)S(1)}, u32[]{:S(2)}, u32[]{:S(2)}) collective-permute-start(f32[8,4096]{1,0:T(8,128)S(1)} %get-tuple-element.20), channel_id=1, source_target_pairs={{0,1},{1,0},{2,3},{3,2},{4,5},{5,4},{6,7},{7,6},{8,9},{9,8},{10,11... | collective-permute-start | bytes 393224 | tf_op jit(solution)/shard_map/ppermute | solution.py:629

commit v10 on v9

--- a/solution.py
+++ b/solution.py
@@ -134,24 +134,24 @@
         send_c[...] = vt[:, :LOCAL]
 
 
-def coeff_kernel(vt, pt, rec_c, bases, tr, mats, cf, path, halo):
-    core = lax.axis_index("vec")
-    ends = ((slice(0, HALO), slice(0, HALO)), (slice(COLS - HALO, COLS), slice(LOCAL - HALO, LOCAL)))
-    for which, (cols, other) in enumerate(ends):
-
-        @pl.when(core == which)
-        def _():
-            halo[0:8, :] = vt[:, cols]
-            halo[8:16, :] = rec_c[:, other]
-            halo[16:24, :] = pt[:, cols]
-
+def coeff_kernel(vt, bases, tr, ut, bown, cf, path, mats, place, buf):
     cf[248:256, :] = jnp.zeros((8, 128), f32)
+    pick = transfers_wanted()
+
+    def pick_steps(steps):
+        for g in steps:
+            out = dot(pick, ut[4 * g : 4 * g + 4].reshape(256, 254), NT)
+            for j in range(4):
+                at = (4 * g + j) * T_ROWS
+                buf[at : at + T_ROWS, :64] = out[:, 64 * j : 64 * j + 64]
+
     for leaf in range(16):
         cf[8 * leaf : 8 * leaf + 8, :64] = dot(
             vt[:, LEAF * leaf : LEAF * leaf + LEAF], bases[leaf], NT
         )
+    pick_steps(range(0, 4))
     off, n = 0, 16
-    while n > 1:
+    for level in range(4):
         for m in range(n // 2):
             r = 8 * (off + 2 * m)
             pair = jnp.concatenate([cf[r : r + 8, :64], cf[r + 8 : r + 16, :64]], axis=1)
@@ -160,11 +160,24 @@
             cf[t : t + 8, :64] = dot_pair(pair, w)
         off += n
         n //= 2
+        pick_steps(range(4 + 3 * level, 7 + 3 * level))
+    for m in list(range(OWN, OWN + 3)) + list(range(OWN)) + list(range(OWN + 3, 39)):
+        mats[64 * m : 64 * m + 64, :] = buf[pl.ds(m, 64, stride=T_ROWS), :][:, :64].astype(bf16)
     value = cf[240:248, :64]
     for u in range(3):
         path[8 * u : 8 * u + 8, :] = value
         value = dot_pair(value, own_matrix(mats, OWN + u))
     path[24:32, :] = value
+    owner = bown[...]
+    owner_f = owner.astype(f32)
+    column = jnp.transpose(jnp.broadcast_to(owner_f, (128, 256)))
+    ranks = []
+    for half in range(2):
+        row = owner_f[:, 128 * half : 128 * half + 128]
+        before = iota((256, 128), 0) < iota((256, 128), 1) + 128 * half
+        same = jnp.where((column == row) & before, 1.0, 0.0)
+        ranks.append(jnp.sum(same, axis=0, keepdims=True))
+    place[...] = owner * 4 + jnp.concatenate(ranks, axis=1).astype(i32)
 
 
 def own_matrix(mats, row, count=1):
@@ -172,8 +185,18 @@
 
 
 def product_kernel(
-    cf, path, cp, bsrc, bown, btgt, send, pick, prod
+    cf, path, cp, bsrc, place_in, btgt, vt, pt, rec_c, send, halo, pick, prod
 ):
+    core = lax.axis_index("vec")
+    ends = ((slice(0, HALO), slice(0, HALO)), (slice(COLS - HALO, COLS), slice(LOCAL - HALO, LOCAL)))
+    for which, (cols, other) in enumerate(ends):
+
+        @pl.when(core == which)
+        def _():
+            halo[0:8, :] = vt[:, cols]
+            halo[8:16, :] = rec_c[:, other]
+            halo[16:24, :] = pt[:, cols]
+
     source = hot(iota((32, 256), 0) == bsrc[...])
     for v in range(8):
         mine = cf[pl.ds(v, 32, stride=8), :][:, :64].astype(bf16)
@@ -196,16 +219,7 @@
                 prod[top : top + 16, lanes] = acc[v].astype(bf16)
     prod[512:576, :] = jnp.zeros((64, 256), bf16)
     prod[576:640, :] = jnp.broadcast_to((btgt[...] + 1).astype(f32), (64, 256)).astype(bf16)
-    owner = bown[...]
-    owner_f = owner.astype(f32)
-    column = jnp.transpose(jnp.broadcast_to(owner_f, (128, 256)))
-    ranks = []
-    for half in range(2):
-        row = owner_f[:, 128 * half : 128 * half + 128]
-        before = iota((256, 128), 0) < iota((256, 128), 1) + 128 * half
-        same = jnp.where((column == row) & before, 1.0, 0.0)
-        ranks.append(jnp.sum(same, axis=0, keepdims=True))
-    place = owner * 4 + jnp.concatenate(ranks, axis=1).astype(i32)
+    place = place_in[...]
     group = lax.shift_right_logical(place, 3) & 3
     slot_row = lax.shift_right_logical(place, 5) * 8 + (place & 7)
     payload = prod[...]
@@ -364,14 +378,14 @@
         mats[64 * m : 64 * m + 64, :] = buf[pl.ds(m, 64, stride=rows), :][:, :64].astype(bf16)
 
 
-def transfers_kernel(ut, mats, buf):
+def transfers_wanted():
     row = iota((T_ROWS, 254), 0)
     want = jnp.where(row < 30, row + UPPER, -1)
     for u in range(3):
         want = jnp.where(row == OWN + u, node(u), want)
         want = jnp.where(row == SIBLING + u, node(u, True), want)
         want = jnp.where(row == OWN_UPPER + u, node(u + 3), want)
-    pick_matrices(ut, want, T_ROWS, 39, mats, buf)
+    return hot(iota((T_ROWS, 254), 1) == want)
 
 
 def couplings_kernel(uc, seen, mats, buf):
@@ -556,31 +570,24 @@
     rec_c = lax.ppermute(send_c, axes, pairs_c)
     ut = jnp.transpose(up_transfer, (1, 2, 0))
     uc = jnp.transpose(up_coupling, (1, 2, 0))
-    (mats,) = call(
-        transfers_kernel,
-        [((64 * T_ROWS, 64), bf16)],
+    cf, path, mats, place = call(
+        coeff_kernel,
+        [((256, 128), f32), ((32, 64), f32), ((64 * T_ROWS, 64), bf16), ((1, 256), i32)],
         [pltpu.VMEM((64 * T_ROWS, 128), f32)],
-        (ut,), "v>v",
-        2 * 4096 * 256 * 40, 3 << 20,
-    )
-    cf, path, halo = call(
-        coeff_kernel,
-        [((256, 128), f32), ((32, 64), f32), ((24, HALO), bf16)],
-        [],
-        (vt, pt, rec_c, leaf_bases, transfers, mats), "vvvvvv>vvv",
-        2 * 512 * 512 * 256, 2 << 20,
-    )
-    halo = lax.ppermute(halo, axes, pairs_a)
-    (send,) = call(
+        (vt, leaf_bases, transfers, ut, block_owner.reshape(1, -1)), "vvvvv>vvvv",
+        2 * 4096 * 256 * 40, 5 << 20,
+    )
+    send, halo = call(
         product_kernel,
-        [((128, 2176), bf16)],
+        [((128, 2176), bf16), ((24, HALO), bf16)],
         [pltpu.VMEM((1024, 128), f32), pltpu.VMEM((640, 256), bf16)],
         (
             cf, path, jnp.transpose(coupling_blocks, (1, 2, 0)),
-            block_source.reshape(1, -1), block_owner.reshape(1, -1), block_target.reshape(1, -1),
-        ), "vvvvvv>v",
+            block_source.reshape(1, -1), place, block_target.reshape(1, -1), vt, pt, rec_c,
+        ), "vvvvvvvvv>vv",
         2 * 512 * 256 * 640, 4 << 20,
     )
+    halo = lax.ppermute(halo, axes, pairs_a)
     near_groups = [[xy * 8 + z for z in range(8)] for xy in range(peers // 8)]
     far_groups = [[xy * 8 + z for xy in range(peers // 8)] for z in range(8)]
     recv = lax.all_to_all(

time: 55.2 us -> 53.8 us (0.975)
  Pallas kernels: 30 us -> 28.6 us
    pallas_call x9 -> x8, Pallas kernels: 30 us -> 28.6 us  [call(): pl.pallas_call(kernel, out_shape=[pltpu.HBM(s, d) if k == 'h' else jax.Sh...]
  transfers between devices with their start and end apart: 5 -> 5, of which waited for: 2 -> 2; matrix products, arithmetic and copies ran while one was open for 0% -> 0% of each run, Pallas kernels for 32% -> 34%
where the time goes in v10:
time: 53.8 us; the launch traced here: 53.5 us
  Pallas kernels  28.6 us (53%)
  starting transfers between devices  20.6 us (38%)
  waiting for transfers between devices  3.84 us (7%)
    pallas_call x8, Pallas kernels, call(): pl.pallas_call(kernel, out_shape=[pltpu.HBM(s, d) if k == 'h' else jax.Sh...  28.6 us
    all_to_all x2, starting transfers between devices, shards(): lax.all_to_all(send, 'leaf', split_axis=0, concat_axis=0, tiled=True, axi...  15.2 us
    ppermute x1, starting transfers between devices, shards(): halo = lax.ppermute(halo, axes, pairs_a)  5.28 us
    all_to_all x2, waiting for transfers between devices, shards(): lax.all_to_all(send, 'leaf', split_axis=0, concat_axis=0, tiled=True, axi...  2.5 us
    ppermute x1, waiting for transfers between devices, shards(): near_other = lax.ppermute(near_send, axes, pairs_c)  1.33 us
  transfers between devices with their start and end apart: 5, of which 2 were waited for; matrix products, arithmetic and copies ran while one was open for 0% of the time, Pallas kernels for 34%

profile of v10, /device:TPU:8, one launch (start us, length us, event | category | flops | bytes accessed | tf_op | source)
XLA Modules:
  0.0 53.5 jit_solution(6595399552050042283)
XLA Ops:
  0.0 0.0 copy-start.4
  0.0 2.9 %shard_map.109 = (bf16[8,8192]{1,0:T(8,128)(2,1)S(1)}, bf16[8,8192]{1,0:T(8,128)(2,1)S(1)}, bf16[8,5120]{1,0:T(8,128)(2,1)S(1)}) custom-call(bf16[3,8192]{1,0:T(4,128)(2,1)} %pts_in.1, bf16[8,8192]{1,0:T(8,128)(2,1)} %vec_in.1, s32[1,8192]{1,0:T(1,128)} %perm_in.3), custom_call_target="tpu_custom_call" | custom-call | flops 1610612736 | bytes 1048576 | tf_op jit(solution)/shard_map/pallas_call | solution.py:69
  3.0 0.0 copy-start.1
  3.0 0.0 copy-start.5
  3.0 0.0 copy-start.6
  3.0 0.1 collective-permute-start
  3.1 0.0 copy-done
  3.1 1.9 %shard_map.110 = (f32[256,128]{1,0:T(8,128)S(1)}, f32[32,64]{1,0:T(8,128)S(1)}, bf16[2560,64]{1,0:T(8,128)(2,1)S(1)}, s32[1,256]{1,0:T(1,128)S(1)}) custom-call(bf16[8,8192]{1,0:T(8,128)(2,1)S(1)} %get-tuple-element.16.vt.vt_in, bf16[16,64,512]{2,1,0:T(8,128)(2,1)S(1)} %copy-done.3, bf16[30,64,64]{2,1,0:T(8,128)(2,1)S(1)} %copy-done.4, ...), custom_call_target="tpu_custom_call" | custom-call | flops 83886080 | bytes 5242880 | tf_op jit(solution)/shard_map/pallas_call | solution.py:69
  5.0 0.0 collective-permute-done.rec_c.c_in
  5.0 0.0 copy-done.5
  5.0 3.9 %shard_map.111 = (bf16[128,2176]{1,0:T(8,128)(2,1)}, bf16[24,1024]{1,0:T(8,128)(2,1)S(1)}) custom-call(f32[256,128]{1,0:T(8,128)S(1)} %get-tuple-element.17.cf, f32[32,64]{1,0:T(8,128)S(1)} %get-tuple-element.18.path.path_in, bf16[64,64,256]{2,1,0:T(8,128)(2,1)S(1)} %bitcast.12, s32[1,256]{1,0:T(1,128)S(1)} %bitcast.15, ...), custom_call_target="tpu_custom_call" | custom-call | flops 167772160 | bytes 4194304 | tf_op jit(solution)/shard_map/pallas_call | solution.py:69
  8.9 7.4 %all-to-all-start = ((bf16[16,8,2176]{2,1,0:T(8,128)(2,1)}), bf16[16,8,2176]{2,1,0:T(8,128)(2,1)S(1)}, u32[]{:S(2)}, u32[]{:S(2)}) async-start(bf16[16,8,2176]{2,1,0:T(8,128)(2,1)} %bitcast.5), calls=%async_computation | async-start | bytes 1114112 | tf_op jit(solution)/shard_map/all_to_all | solution.py:593
  16.3 5.3 %collective-permute-start.1 = (bf16[24,1024]{1,0:T(8,128)(2,1)S(1)}, bf16[24,1024]{1,0:T(8,128)(2,1)S(1)}, u32[]{:S(2)}, u32[]{:S(2)}) collective-permute-start(bf16[24,1024]{1,0:T(8,128)(2,1)S(1)} %get-tuple-element.24), channel_id=1, source_target_pairs={{0,255},{255,0},{1,2},{2,1},{3,4},{4,3},{5,6},{6,5},{7,8},{8,7},{9... | collective-permute-start | bytes 147464 | tf_op jit(solution)/shard_map/ppermute | solution.py:590
  21.6 5.1 %shard_map.114.begun = f32[16,2048]{1,0:T(8,128)} custom-call(bf16[8,8192]{1,0:T(8,128)(2,1)S(1)} %get-tuple-element.16.vt.vt_in, bf16[8,8192]{1,0:T(8,128)(2,1)S(1)} %get-tuple-element.20.pt.pt_in, bf16[8,5120]{1,0:T(8,128)(2,1)S(1)} %collective-permute-done.rec_c.c_in), custom_call_target="tpu_custom_call" | custom-call | flops 4966055936 | bytes 1048576 | tf_op jit(solution)/shard_map/pallas_call | solution.py:69
  26.7 1.3 %shard_map.112.coup_in = bf16[512,64]{1,0:T(8,128)(2,1)S(1)} custom-call(bf16[64,64,254]{2,1,0:T(8,128)(2,1)S(1)} %bitcast.13, bf16[128,2176]{1,0:T(8,128)(2,1)} %get-tuple-element.22.seen), custom_call_target="tpu_custom_call" | custom-call | flops 16777216 | bytes 3145728 | tf_op jit(solution)/shard_map/pallas_call | solution.py:69
  28.1 0.0 all-to-all-done
  28.1 3.1 %shard_map.113 = bf16[256,512]{1,0:T(8,128)(2,1)} custom-call(bf16[128,2176]{1,0:T(8,128)(2,1)S(1)} %bitcast.10, f32[32,64]{1,0:T(8,128)S(1)} %get-tuple-element.18.path.path_in, bf16[2560,64]{1,0:T(8,128)(2,1)S(1)} %get-tuple-element.23.mats_in, bf16[512,64]{1,0:T(8,128)(2,1)S(1)} %shard_map.112.coup_in), custom_call_target="tpu_custom_call" | custom-call | flops 134217728 | bytes 2097152 | tf_op jit(solution)/shard_map/pallas_call | solution.py:69
  31.2 7.8 %all-to-all-start.1 = ((bf16[8,32,512]{2,1,0:T(8,128)(2,1)}), bf16[8,32,512]{2,1,0:T(8,128)(2,1)S(1)}, u32[]{:S(2)}, u32[]{:S(2)}) async-start(bf16[8,32,512]{2,1,0:T(8,128)(2,1)} %bitcast.8), calls=%async_computation.1 | async-start | bytes 524288 | tf_op jit(solution)/shard_map/all_to_all | solution.py:626
  39.0 0.0 collective-permute-done.1.halo_in
  39.0 6.5 %shard_map.115 = (f32[8,4096]{1,0:T(8,128)S(1)}, f32[8,4096]{1,0:T(8,128)S(1)}) custom-call(bf16[8,8192]{1,0:T(8,128)(2,1)S(1)} %get-tuple-element.16.vt.vt_in, bf16[8,8192]{1,0:T(8,128)(2,1)S(1)} %get-tuple-element.20.pt.pt_in, bf16[8,5120]{1,0:T(8,128)(2,1)S(1)} %collective-permute-done.rec_c.c_in, bf16[24,1024]{1,0:T(8,128)(2,1)S(1)} %collective-permute-done.1.halo_in, ...), custom_call_target="tpu_custom_call" | custom-call | flops 4026531840 | bytes 1048576 | tf_op jit(solution)/shard_map/pallas_call | solution.py:69
  45.6 0.1 collective-permute-start.2
  45.7 1.3 %collective-permute-done.2.other_in = f32[8,4096]{1,0:T(8,128)S(1)} collective-permute-done((f32[8,4096]{1,0:T(8,128)S(1)}, f32[8,4096]{1,0:T(8,128)S(1)}, u32[]{:S(2)}, u32[]{:S(2)}) %collective-permute-start.2) | collective-permute-done | bytes 131104 | tf_op jit(solution)/shard_map/ppermute | solution.py:636
  47.0 2.5 %all-to-all-done.1 = bf16[8,32,512]{2,1,0:T(8,128)(2,1)S(1)} async-done(((bf16[8,32,512]{2,1,0:T(8,128)(2,1)}), bf16[8,32,512]{2,1,0:T(8,128)(2,1)S(1)}, u32[]{:S(2)}, u32[]{:S(2)}) %all-to-all-start.1) | async-done | bytes 262176 | tf_op jit(solution)/shard_map/all_to_all | solution.py:626
  49.5 3.8 %shard_map.116 = bf16[8,8192]{1,0:T(8,128)(2,1)} custom-call(bf16[256,512]{1,0:T(8,128)(2,1)S(1)} %bitcast.14, f32[8,4096]{1,0:T(8,128)S(1)} %get-tuple-element.25.mine_in, f32[8,4096]{1,0:T(8,128)S(1)} %collective-permute-done.2.other_in, bf16[2560,64]{1,0:T(8,128)(2,1)S(1)} %get-tuple-element.23.mats_in, bf16[30,64,64]{2,1,0:T(8,128)(2,1)S(1)} %copy-done.4, ...), custom_call_target="tpu_custom_call" | custom-call | flops 1073741824 | bytes 8388608 | tf_op jit(solution)/shard_map/pallas_call | solution.py:69
  (10 shorter events, 0.0 us)
Async XLA Ops:
  0.0 3.1 %copy-start = (bf16[254,64,64]{0,2,1:T(8,128)(2,1)S(1)}, bf16[254,64,64]{0,2,1:T(8,128)(2,1)}, u32[]{:S(2)}) copy-start(bf16[254,64,64]{0,2,1:T(8,128)(2,1)} %param.20) | copy-start | bytes 6242308
  0.0 3.1 %copy-start.7 = (s32[256,1]{0,1:T(1,128)S(1)}, s32[256,1]{0,1:T(1,128)}, u32[]{:S(2)}) copy-start(s32[256,1]{0,1:T(1,128)} %param.18) | copy-start | bytes 3076
  0.0 3.1 %copy-start.3 = (bf16[16,64,512]{2,1,0:T(8,128)(2,1)S(1)}, bf16[16,64,512]{2,1,0:T(8,128)(2,1)}, u32[]{:S(2)}) copy-start(bf16[16,64,512]{2,1,0:T(8,128)(2,1)} %bases.3) | copy-start | bytes 3145732
  0.0 3.1 %copy-start.4 = (bf16[30,64,64]{2,1,0:T(8,128)(2,1)S(1)}, bf16[30,64,64]{2,1,0:T(8,128)(2,1)}, u32[]{:S(2)}) copy-start(bf16[30,64,64]{2,1,0:T(8,128)(2,1)} %tr.3) | copy-start | bytes 737284
  3.0 2.0 %copy-start.1 = (bf16[256,64,64]{0,2,1:T(8,128)(2,1)S(1)}, bf16[256,64,64]{0,2,1:T(8,128)(2,1)}, u32[]{:S(2)}) copy-start(bf16[256,64,64]{0,2,1:T(8,128)(2,1)} %param.16) | copy-start | bytes 6291460
  3.0 2.0 %copy-start.5 = (s32[256]{0:T(256)S(1)}, s32[256]{0:T(256)}, u32[]{:S(2)}) copy-start(s32[256]{0:T(256)} %param.17) | copy-start | bytes 3076
  3.0 2.0 %copy-start.6 = (s32[256]{0:T(256)S(1)}, s32[256]{0:T(256)}, u32[]{:S(2)}) copy-start(s32[256]{0:T(256)} %param.19) | copy-start | bytes 3076
  3.0 2.0 %collective-permute-start = (bf16[8,5120]{1,0:T(8,128)(2,1)S(1)}, bf16[8,5120]{1,0:T(8,128)(2,1)S(1)}, u32[]{:S(2)}, u32[]{:S(2)}) collective-permute-start(bf16[8,5120]{1,0:T(8,128)(2,1)S(1)} %get-tuple-element.21), channel_id=1, source_target_pairs={{0,1},{1,0},{2,3},{3,2},{4,5},{5,4},{6,7},{7,6},{8,9},{9,8},{10,11... | collective-permute-start | bytes 245768 | tf_op jit(solution)/shard_map/ppermute | solution.py:570
  8.9 19.2 %all-to-all-start = ((bf16[16,8,2176]{2,1,0:T(8,128)(2,1)}), bf16[16,8,2176]{2,1,0:T(8,128)(2,1)S(1)}, u32[]{:S(2)}, u32[]{:S(2)}) async-start(bf16[16,8,2176]{2,1,0:T(8,128)(2,1)} %bitcast.5), calls=%async_computation | async-start | bytes 1114112 | tf_op jit(solution)/shard_map/all_to_all | solution.py:593
  16.3 10.4 %copy-start.2 = (bf16[254,64,64]{0,2,1:T(8,128)(2,1)S(1)}, bf16[254,64,64]{0,2,1:T(8,128)(2,1)}, u32[]{:S(2)}) copy-start(bf16[254,64,64]{0,2,1:T(8,128)(2,1)} %param.21) | copy-start | bytes 6242308
  16.3 22.7 %collective-permute-start.1 = (bf16[24,1024]{1,0:T(8,128)(2,1)S(1)}, bf16[24,1024]{1,0:T(8,128)(2,1)S(1)}, u32[]{:S(2)}, u32[]{:S(2)}) collective-permute-start(bf16[24,1024]{1,0:T(8,128)(2,1)S(1)} %get-tuple-element.24), channel_id=1, source_target_pairs={{0,255},{255,0},{1,2},{2,1},{3,4},{4,3},{5,6},{6,5},{7,8},{8,7},{9... | collective-permute-start | bytes 147464 | tf_op jit(solution)/shard_map/ppermute | solution.py:590
  31.2 18.3 %all-to-all-start.1 = ((bf16[8,32,512]{2,1,0:T(8,128)(2,1)}), bf16[8,32,512]{2,1,0:T(8,128)(2,1)S(1)}, u32[]{:S(2)}, u32[]{:S(2)}) async-start(bf16[8,32,512]{2,1,0:T(8,128)(2,1)} %bitcast.8), calls=%async_computation.1 | async-start | bytes 524288 | tf_op jit(solution)/shard_map/all_to_all | solution.py:626
  45.6 1.4 %collective-permute-start.2 = (f32[8,4096]{1,0:T(8,128)S(1)}, f32[8,4096]{1,0:T(8,128)S(1)}, u32[]{:S(2)}, u32[]{:S(2)}) collective-permute-start(f32[8,4096]{1,0:T(8,128)S(1)} %get-tuple-element.26), channel_id=1, source_target_pairs={{0,1},{1,0},{2,3},{3,2},{4,5},{5,4},{6,7},{7,6},{8,9},{9,8},{10,11... | collective-permute-start | bytes 393224 | tf_op jit(solution)/shard_map/ppermute | solution.py:636

commit v11 on v10

--- a/solution.py
+++ b/solution.py
@@ -298,19 +298,34 @@
 
 
 def near_first_kernel(
-    vt_in, pt_in, c_in, begun, vt, pt, rec_c, vw, fs, ft, pw, acc, sems, out_sems
+    vt_in, pt_in, c_in, uc_in, begun, coup,
+    vt, pt, rec_c, vw, fs, ft, pw, acc, sems, out_sems, buf, uc,
 ):
-    for copy in fetch(sems, (vt_in, vt), (pt_in, pt), (c_in, rec_c)):
+    pick = couplings_wanted()
+
+    def pick_steps(steps):
+        for g in steps:
+            out = dot(pick, uc[4 * g : 4 * g + 4].reshape(256, 254), NT)
+            for j in range(4):
+                at = (4 * g + j) * C_ROWS
+                buf[at : at + C_ROWS, :64] = out[:, 64 * j : 64 * j + 64]
+
+    loads = fetch(sems, (vt_in, vt), (pt_in, pt), (c_in, rec_c), (uc_in, uc))
+    for copy in loads[:3]:
         copy.wait()
     load_window(vt, pt, rec_c, None, range(SPLIT, 12), vw, pw)
     features(range(SPLIT, 12), pw, fs, ft)
     acc[...] = jnp.zeros_like(acc)
+    loads[3].wait()
     copies = []
     for t in range(SPLIT, 10):
+        pick_steps(range(4 * (t - SPLIT), 4 * (t - SPLIT) + 4))
         near_target(t, vw, fs, ft, acc)
         src, dst = acc.at[:, leaf_cols(t - 2)], begun.at[:, leaf_cols(t - SPLIT)]
         copies += [pltpu.make_async_copy(src, dst, out_sems.at[t - SPLIT])]
         copies[-1].start()
+    for m in range(7):
+        coup[64 * m : 64 * m + 64, :] = buf[pl.ds(m, 64, stride=C_ROWS), :][:, :64].astype(bf16)
     for copy in copies:
         copy.wait()
 
@@ -363,21 +378,6 @@
     return LEVEL_START[u] + (lax.bitwise_xor(n, 1) if other else n)
 
 
-def pick_matrices(table, want, rows, count, mats, buf):
-    pick = hot(iota((rows, 254), 1) == want)
-
-    def step(g, carry):
-        out = dot(pick, table[pl.ds(4 * g, 4)].reshape(256, 254), NT)
-        for j in range(4):
-            at = pl.multiple_of((4 * g + j) * rows, 8)
-            buf[pl.ds(at, rows), :64] = out[:, 64 * j : 64 * j + 64]
-        return carry
-
-    lax.fori_loop(0, 16, step, 0, unroll=4)
-    for m in range(count):
-        mats[64 * m : 64 * m + 64, :] = buf[pl.ds(m, 64, stride=rows), :][:, :64].astype(bf16)
-
-
 def transfers_wanted():
     row = iota((T_ROWS, 254), 0)
     want = jnp.where(row < 30, row + UPPER, -1)
@@ -388,12 +388,12 @@
     return hot(iota((T_ROWS, 254), 1) == want)
 
 
-def couplings_kernel(uc, seen, mats, buf):
+def couplings_wanted():
     row = iota((C_ROWS, 254), 0)
     want = jnp.zeros((C_ROWS, 254), i32) - 1
     for u in range(7):
         want = jnp.where(row == u, node(u, u < 3), want)
-    pick_matrices(uc, want, C_ROWS, 7, mats, buf)
+    return hot(iota((C_ROWS, 254), 1) == want)
 
 
 def middle_kernel(
@@ -598,19 +598,16 @@
         pltpu.VMEM((16, 6144), bf16), pltpu.VMEM((6144, 16), bf16), pltpu.VMEM((16, 6144), bf16),
         pltpu.VMEM((8, 6144), f32), pltpu.VMEM((16, HALF), f32), pltpu.SemaphoreType.DMA((6,)),
     ]
-    (coup,) = call(
-        couplings_kernel,
-        [((64 * C_ROWS, 64), bf16)],
-        [pltpu.VMEM((64 * C_ROWS, 128), f32)],
-        (uc, send), "va>v",
-        2 * 4096 * 256 * 8, 3 << 20,
-    )
-    (begun,) = call(
+    begun, coup = call(
         near_first_kernel,
-        [((16, LEAF * (10 - SPLIT)), f32)],
-        buffers + [pltpu.SemaphoreType.DMA((10 - SPLIT,))],
-        (vt, pt, rec_c), "aaa>h",
-        2 * 37 * 512 * 512 * 256, 1 << 20, vmem=24,
+        [((16, LEAF * (10 - SPLIT)), f32), ((64 * C_ROWS, 64), bf16)],
+        buffers
+        + [
+            pltpu.SemaphoreType.DMA((10 - SPLIT,)), pltpu.VMEM((64 * C_ROWS, 128), f32),
+            pltpu.VMEM((64, 64, 254), bf16),
+        ],
+        (vt, pt, rec_c, uc), "aaah>hv",
+        2 * 33 * 512 * 512 * 256, 3 << 20, vmem=24,
     )
     (send,) = call(
         middle_kernel,

time: 53.8 us -> 53.8 us (level)
  Pallas kernels: 28.6 us -> 29.3 us
  starting transfers between devices: 20.6 us -> 20 us
    pallas_call x8 -> x7, Pallas kernels: 28.6 us -> 29.3 us  [call(): pl.pallas_call(kernel, out_shape=[pltpu.HBM(s, d) if k == 'h' else jax.Sh...]
    all_to_all x2, starting transfers between devices: 15.2 us -> 14.5 us  [shards(): lax.all_to_all(send, 'leaf', split_axis=0, concat_axis=0, tiled=True, axi...]
  transfers between devices with their start and end apart: 5 -> 5, of which waited for: 2 -> 2; matrix products, arithmetic and copies ran while one was open for 0% -> 0% of each run, Pallas kernels for 34% -> 35%
where the time goes in v11:
time: 53.8 us; the launch traced here: 53.5 us
  Pallas kernels  29.3 us (54%)
  starting transfers between devices  20 us (37%)
  waiting for transfers between devices  3.84 us (7%)
    pallas_call x7, Pallas kernels, call(): pl.pallas_call(kernel, out_shape=[pltpu.HBM(s, d) if k == 'h' else jax.Sh...  29.3 us
    all_to_all x2, starting transfers between devices, shards(): lax.all_to_all(send, 'leaf', split_axis=0, concat_axis=0, tiled=True, axi...  14.5 us
    ppermute x1, starting transfers between devices, shards(): halo = lax.ppermute(halo, axes, pairs_a)  5.28 us
    all_to_all x2, waiting for transfers between devices, shards(): lax.all_to_all(send, 'leaf', split_axis=0, concat_axis=0, tiled=True, axi...  2.5 us
    ppermute x1, waiting for transfers between devices, shards(): near_other = lax.ppermute(near_send, axes, pairs_c)  1.33 us
  transfers between devices with their start and end apart: 5, of which 2 were waited for; matrix products, arithmetic and copies ran while one was open for 0% of the time, Pallas kernels for 35%

profile of v11, /device:TPU:8, one launch (start us, length us, event | category | flops | bytes accessed | tf_op | source)
XLA Modules:
  0.0 53.5 jit_solution(1085350811162042204)
XLA Ops:
  0.0 0.0 copy-start.3
  0.0 2.9 %shard_map.109 = (bf16[8,8192]{1,0:T(8,128)(2,1)S(1)}, bf16[8,8192]{1,0:T(8,128)(2,1)S(1)}, bf16[8,5120]{1,0:T(8,128)(2,1)S(1)}) custom-call(bf16[3,8192]{1,0:T(4,128)(2,1)} %pts_in.1, bf16[8,8192]{1,0:T(8,128)(2,1)} %vec_in.1, s32[1,8192]{1,0:T(1,128)} %perm_in.3), custom_call_target="tpu_custom_call" | custom-call | flops 1610612736 | bytes 1048576 | tf_op jit(solution)/shard_map/pallas_call | solution.py:69
  3.0 0.0 copy-start.1
  3.0 0.0 copy-start.4
  3.0 0.0 copy-start.5
  3.0 0.1 collective-permute-start
  3.1 0.0 copy-done
  3.1 0.0 copy-done.6
  3.1 1.9 %shard_map.110 = (f32[256,128]{1,0:T(8,128)S(1)}, f32[32,64]{1,0:T(8,128)S(1)}, bf16[2560,64]{1,0:T(8,128)(2,1)S(1)}, s32[1,256]{1,0:T(1,128)S(1)}) custom-call(bf16[8,8192]{1,0:T(8,128)(2,1)S(1)} %get-tuple-element.18.vt.vt_in, bf16[16,64,512]{2,1,0:T(8,128)(2,1)S(1)} %copy-done.2, bf16[30,64,64]{2,1,0:T(8,128)(2,1)S(1)} %copy-done.3, ...), custom_call_target="tpu_custom_call" | custom-call | flops 83886080 | bytes 5242880 | tf_op jit(solution)/shard_map/pallas_call | solution.py:69
  5.0 0.0 collective-permute-done.rec_c.c_in
  5.0 0.0 copy-done.4
  5.0 3.9 %shard_map.111 = (bf16[128,2176]{1,0:T(8,128)(2,1)}, bf16[24,1024]{1,0:T(8,128)(2,1)S(1)}) custom-call(f32[256,128]{1,0:T(8,128)S(1)} %get-tuple-element.19.cf, f32[32,64]{1,0:T(8,128)S(1)} %get-tuple-element.20.path.path_in, bf16[64,64,256]{2,1,0:T(8,128)(2,1)S(1)} %bitcast.12, s32[1,256]{1,0:T(1,128)S(1)} %bitcast.14, ...), custom_call_target="tpu_custom_call" | custom-call | flops 167772160 | bytes 4194304 | tf_op jit(solution)/shard_map/pallas_call | solution.py:69
  8.9 7.4 %all-to-all-start = ((bf16[16,8,2176]{2,1,0:T(8,128)(2,1)}), bf16[16,8,2176]{2,1,0:T(8,128)(2,1)S(1)}, u32[]{:S(2)}, u32[]{:S(2)}) async-start(bf16[16,8,2176]{2,1,0:T(8,128)(2,1)} %bitcast.5), calls=%async_computation | async-start | bytes 1114112 | tf_op jit(solution)/shard_map/all_to_all | solution.py:593
  16.3 5.3 %collective-permute-start.1 = (bf16[24,1024]{1,0:T(8,128)(2,1)S(1)}, bf16[24,1024]{1,0:T(8,128)(2,1)S(1)}, u32[]{:S(2)}, u32[]{:S(2)}) collective-permute-start(bf16[24,1024]{1,0:T(8,128)(2,1)S(1)} %get-tuple-element.27), channel_id=1, source_target_pairs={{0,255},{255,0},{1,2},{2,1},{3,4},{4,3},{5,6},{6,5},{7,8},{8,7},{9... | collective-permute-start | bytes 147464 | tf_op jit(solution)/shard_map/ppermute | solution.py:590
  21.6 7.1 %shard_map.112 = (f32[16,2048]{1,0:T(8,128)}, bf16[512,64]{1,0:T(8,128)(2,1)S(1)}) custom-call(bf16[8,8192]{1,0:T(8,128)(2,1)S(1)} %get-tuple-element.18.vt.vt_in, bf16[8,8192]{1,0:T(8,128)(2,1)S(1)} %get-tuple-element.22.pt.pt_in, bf16[8,5120]{1,0:T(8,128)(2,1)S(1)} %collective-permute-done.rec_c.c_in, bf16[64,64,254]{2,1,0:T(8,128)(2,1)} %bitcast.17), custom_call_target="tpu_custom_call" | custom-call | flops 4429185024 | bytes 3145728 | tf_op jit(solution)/shard_map/pallas_call | solution.py:69
  28.7 0.0 all-to-all-done
  28.8 3.1 %shard_map.113 = bf16[256,512]{1,0:T(8,128)(2,1)} custom-call(bf16[128,2176]{1,0:T(8,128)(2,1)S(1)} %bitcast.10, f32[32,64]{1,0:T(8,128)S(1)} %get-tuple-element.20.path.path_in, bf16[2560,64]{1,0:T(8,128)(2,1)S(1)} %get-tuple-element.25.mats_in, bf16[512,64]{1,0:T(8,128)(2,1)S(1)} %get-tuple-element.26.coup_in), custom_call_target="tpu_custom_call" | custom-call | flops 134217728 | bytes 2097152 | tf_op jit(solution)/shard_map/pallas_call | solution.py:69
  31.9 7.1 %all-to-all-start.1 = ((bf16[8,32,512]{2,1,0:T(8,128)(2,1)}), bf16[8,32,512]{2,1,0:T(8,128)(2,1)S(1)}, u32[]{:S(2)}, u32[]{:S(2)}) async-start(bf16[8,32,512]{2,1,0:T(8,128)(2,1)} %bitcast.8), calls=%async_computation.1 | async-start | bytes 524288 | tf_op jit(solution)/shard_map/all_to_all | solution.py:623
  39.0 0.0 collective-permute-done.1.halo_in
  39.0 6.5 %shard_map.114 = (f32[8,4096]{1,0:T(8,128)S(1)}, f32[8,4096]{1,0:T(8,128)S(1)}) custom-call(bf16[8,8192]{1,0:T(8,128)(2,1)S(1)} %get-tuple-element.18.vt.vt_in, bf16[8,8192]{1,0:T(8,128)(2,1)S(1)} %get-tuple-element.22.pt.pt_in, bf16[8,5120]{1,0:T(8,128)(2,1)S(1)} %collective-permute-done.rec_c.c_in, bf16[24,1024]{1,0:T(8,128)(2,1)S(1)} %collective-permute-done.1.halo_in, ...), custom_call_target="tpu_custom_call" | custom-call | flops 4026531840 | bytes 1048576 | tf_op jit(solution)/shard_map/pallas_call | solution.py:69
  45.6 0.1 collective-permute-start.2
  45.7 1.3 %collective-permute-done.2.other_in = f32[8,4096]{1,0:T(8,128)S(1)} collective-permute-done((f32[8,4096]{1,0:T(8,128)S(1)}, f32[8,4096]{1,0:T(8,128)S(1)}, u32[]{:S(2)}, u32[]{:S(2)}) %collective-permute-start.2) | collective-permute-done | bytes 131104 | tf_op jit(solution)/shard_map/ppermute | solution.py:633
  47.0 2.5 %all-to-all-done.1 = bf16[8,32,512]{2,1,0:T(8,128)(2,1)S(1)} async-done(((bf16[8,32,512]{2,1,0:T(8,128)(2,1)}), bf16[8,32,512]{2,1,0:T(8,128)(2,1)S(1)}, u32[]{:S(2)}, u32[]{:S(2)}) %all-to-all-start.1) | async-done | bytes 262176 | tf_op jit(solution)/shard_map/all_to_all | solution.py:623
  49.5 3.8 %shard_map.115 = bf16[8,8192]{1,0:T(8,128)(2,1)} custom-call(bf16[256,512]{1,0:T(8,128)(2,1)S(1)} %bitcast.13, f32[8,4096]{1,0:T(8,128)S(1)} %get-tuple-element.29.mine_in, f32[8,4096]{1,0:T(8,128)S(1)} %collective-permute-done.2.other_in, bf16[2560,64]{1,0:T(8,128)(2,1)S(1)} %get-tuple-element.25.mats_in, bf16[30,64,64]{2,1,0:T(8,128)(2,1)S(1)} %copy-done.3, ...), custom_call_target="tpu_custom_call" | custom-call | flops 1073741824 | bytes 8388608 | tf_op jit(solution)/shard_map/pallas_call | solution.py:69
  (7 shorter events, 0.0 us)
Async XLA Ops:
  0.0 3.1 %copy-start = (bf16[254,64,64]{0,2,1:T(8,128)(2,1)S(1)}, bf16[254,64,64]{0,2,1:T(8,128)(2,1)}, u32[]{:S(2)}) copy-start(bf16[254,64,64]{0,2,1:T(8,128)(2,1)} %param.20) | copy-start | bytes 6242308
  0.0 3.1 %copy-start.6 = (s32[256,1]{0,1:T(1,128)S(1)}, s32[256,1]{0,1:T(1,128)}, u32[]{:S(2)}) copy-start(s32[256,1]{0,1:T(1,128)} %param.18) | copy-start | bytes 3076
  0.0 3.1 %copy-start.2 = (bf16[16,64,512]{2,1,0:T(8,128)(2,1)S(1)}, bf16[16,64,512]{2,1,0:T(8,128)(2,1)}, u32[]{:S(2)}) copy-start(bf16[16,64,512]{2,1,0:T(8,128)(2,1)} %bases.3) | copy-start | bytes 3145732
  0.0 3.1 %copy-start.3 = (bf16[30,64,64]{2,1,0:T(8,128)(2,1)S(1)}, bf16[30,64,64]{2,1,0:T(8,128)(2,1)}, u32[]{:S(2)}) copy-start(bf16[30,64,64]{2,1,0:T(8,128)(2,1)} %tr.3) | copy-start | bytes 737284
  3.0 2.0 %copy-start.1 = (bf16[256,64,64]{0,2,1:T(8,128)(2,1)S(1)}, bf16[256,64,64]{0,2,1:T(8,128)(2,1)}, u32[]{:S(2)}) copy-start(bf16[256,64,64]{0,2,1:T(8,128)(2,1)} %param.16) | copy-start | bytes 6291460
  3.0 2.0 %copy-start.4 = (s32[256]{0:T(256)S(1)}, s32[256]{0:T(256)}, u32[]{:S(2)}) copy-start(s32[256]{0:T(256)} %param.17) | copy-start | bytes 3076
  3.0 2.0 %copy-start.5 = (s32[256]{0:T(256)S(1)}, s32[256]{0:T(256)}, u32[]{:S(2)}) copy-start(s32[256]{0:T(256)} %param.19) | copy-start | bytes 3076
  3.0 2.0 %collective-permute-start = (bf16[8,5120]{1,0:T(8,128)(2,1)S(1)}, bf16[8,5120]{1,0:T(8,128)(2,1)S(1)}, u32[]{:S(2)}, u32[]{:S(2)}) collective-permute-start(bf16[8,5120]{1,0:T(8,128)(2,1)S(1)} %get-tuple-element.23), channel_id=1, source_target_pairs={{0,1},{1,0},{2,3},{3,2},{4,5},{5,4},{6,7},{7,6},{8,9},{9,8},{10,11... | collective-permute-start | bytes 245768 | tf_op jit(solution)/shard_map/ppermute | solution.py:570
  8.9 19.8 %all-to-all-start = ((bf16[16,8,2176]{2,1,0:T(8,128)(2,1)}), bf16[16,8,2176]{2,1,0:T(8,128)(2,1)S(1)}, u32[]{:S(2)}, u32[]{:S(2)}) async-start(bf16[16,8,2176]{2,1,0:T(8,128)(2,1)} %bitcast.5), calls=%async_computation | async-start | bytes 1114112 | tf_op jit(solution)/shard_map/all_to_all | solution.py:593
  16.3 22.7 %collective-permute-start.1 = (bf16[24,1024]{1,0:T(8,128)(2,1)S(1)}, bf16[24,1024]{1,0:T(8,128)(2,1)S(1)}, u32[]{:S(2)}, u32[]{:S(2)}) collective-permute-start(bf16[24,1024]{1,0:T(8,128)(2,1)S(1)} %get-tuple-element.27), channel_id=1, source_target_pairs={{0,255},{255,0},{1,2},{2,1},{3,4},{4,3},{5,6},{6,5},{7,8},{8,7},{9... | collective-permute-start | bytes 147464 | tf_op jit(solution)/shard_map/ppermute | solution.py:590
  31.9 17.6 %all-to-all-start.1 = ((bf16[8,32,512]{2,1,0:T(8,128)(2,1)}), bf16[8,32,512]{2,1,0:T(8,128)(2,1)S(1)}, u32[]{:S(2)}, u32[]{:S(2)}) async-start(bf16[8,32,512]{2,1,0:T(8,128)(2,1)} %bitcast.8), calls=%async_computation.1 | async-start | bytes 524288 | tf_op jit(solution)/shard_map/all_to_all | solution.py:623
  45.6 1.4 %collective-permute-start.2 = (f32[8,4096]{1,0:T(8,128)S(1)}, f32[8,4096]{1,0:T(8,128)S(1)}, u32[]{:S(2)}, u32[]{:S(2)}) collective-permute-start(f32[8,4096]{1,0:T(8,128)S(1)} %get-tuple-element.30), channel_id=1, source_target_pairs={{0,1},{1,0},{2,3},{3,2},{4,5},{5,4},{6,7},{7,6},{8,9},{9,8},{10,11... | collective-permute-start | bytes 393224 | tf_op jit(solution)/shard_map/ppermute | solution.py:633

commit v12 on v10

--- a/solution.py
+++ b/solution.py
@@ -401,7 +401,8 @@
 ):
     device = lax.axis_index("leaf")
     copies = fetch(sems, (recv_in, recv), (mats_in, mats), (coup_in, coup), (path_in, path))
-    copies[0].wait()
+    for copy in copies:
+        copy.wait()
     ext = recv[:, 2048:2176].astype(f32)
 
     turned = jnp.transpose(ext)
@@ -417,8 +418,6 @@
     xs[0:128, :] = ext[:, :64]
     first, n = 0, 16
     firsts = {3: 0}
-    for copy in copies[1:]:
-        copy.wait()
     for u in range(3, 6):
         for m in range(n // 2):
             r = 8 * (first + 2 * m)
@@ -477,7 +476,7 @@
         (other_in, near_other),
         (perm_in, perm),
     )
-    for copy in copies[:2]:
+    for copy in copies:
         copy.wait()
     device = lax.axis_index("leaf")
     core = lax.axis_index("vec")
@@ -516,9 +515,6 @@
             dn[8 * leaf : 8 * leaf + 8, :].astype(bf16), bases[leaf]
         )
 
-    for copy in copies[2:]:
-        copy.wait()
-
     @pl.when(core == 0)
     def _():
         tree[:, :HALF] += near_mine[...]

time: 53.8 us -> 54.4 us (1.011)
  Pallas kernels: 28.6 us -> 29.2 us
    pallas_call x8, Pallas kernels: 28.6 us -> 29.2 us  [call(): pl.pallas_call(kernel, out_shape=[pltpu.HBM(s, d) if k == 'h' else jax.Sh...]
  transfers between devices with their start and end apart: 5 -> 5, of which waited for: 2 -> 2; matrix products, arithmetic and copies ran while one was open for 0% -> 0% of each run, Pallas kernels for 34% -> 33%
where the time goes in v12:
time: 54.4 us; the launch traced here: 54 us
  Pallas kernels  29.2 us (54%)
  starting transfers between devices  20.6 us (38%)
  waiting for transfers between devices  3.84 us (7%)
    pallas_call x8, Pallas kernels, call(): pl.pallas_call(kernel, out_shape=[pltpu.HBM(s, d) if k == 'h' else jax.Sh...  29.2 us
    all_to_all x2, starting transfers between devices, shards(): lax.all_to_all(send, 'leaf', split_axis=0, concat_axis=0, tiled=True, axi...  15.2 us
    ppermute x1, starting transfers between devices, shards(): halo = lax.ppermute(halo, axes, pairs_a)  5.28 us
    all_to_all x2, waiting for transfers between devices, shards(): lax.all_to_all(send, 'leaf', split_axis=0, concat_axis=0, tiled=True, axi...  2.5 us
    ppermute x1, waiting for transfers between devices, shards(): near_other = lax.ppermute(near_send, axes, pairs_c)  1.33 us
  transfers between devices with their start and end apart: 5, of which 2 were waited for; matrix products, arithmetic and copies ran while one was open for 0% of the time, Pallas kernels for 33%

profile of v12, /device:TPU:8, one launch (start us, length us, event | category | flops | bytes accessed | tf_op | source)
XLA Modules:
  0.0 54.0 jit_solution(14002992642620487518)
XLA Ops:
  0.0 0.0 copy-start.4
  0.0 2.9 %shard_map.109 = (bf16[8,8192]{1,0:T(8,128)(2,1)S(1)}, bf16[8,8192]{1,0:T(8,128)(2,1)S(1)}, bf16[8,5120]{1,0:T(8,128)(2,1)S(1)}) custom-call(bf16[3,8192]{1,0:T(4,128)(2,1)} %pts_in.1, bf16[8,8192]{1,0:T(8,128)(2,1)} %vec_in.1, s32[1,8192]{1,0:T(1,128)} %perm_in.3), custom_call_target="tpu_custom_call" | custom-call | flops 1610612736 | bytes 1048576 | tf_op jit(solution)/shard_map/pallas_call | solution.py:69
  3.0 0.0 copy-start.1
  3.0 0.0 copy-start.5
  3.0 0.0 copy-start.6
  3.0 0.1 collective-permute-start
  3.1 1.9 %shard_map.110 = (f32[256,128]{1,0:T(8,128)S(1)}, f32[32,64]{1,0:T(8,128)S(1)}, bf16[2560,64]{1,0:T(8,128)(2,1)S(1)}, s32[1,256]{1,0:T(1,128)S(1)}) custom-call(bf16[8,8192]{1,0:T(8,128)(2,1)S(1)} %get-tuple-element.16.vt.vt_in, bf16[16,64,512]{2,1,0:T(8,128)(2,1)S(1)} %copy-done.3, bf16[30,64,64]{2,1,0:T(8,128)(2,1)S(1)} %copy-done.4, ...), custom_call_target="tpu_custom_call" | custom-call | flops 83886080 | bytes 5242880 | tf_op jit(solution)/shard_map/pallas_call | solution.py:69
  5.0 0.0 collective-permute-done.rec_c.c_in
  5.0 0.0 copy-done.1
  5.0 0.0 copy-done.5
  5.0 3.9 %shard_map.111 = (bf16[128,2176]{1,0:T(8,128)(2,1)}, bf16[24,1024]{1,0:T(8,128)(2,1)S(1)}) custom-call(f32[256,128]{1,0:T(8,128)S(1)} %get-tuple-element.17.cf, f32[32,64]{1,0:T(8,128)S(1)} %get-tuple-element.18.path.path_in, bf16[64,64,256]{2,1,0:T(8,128)(2,1)S(1)} %bitcast.12, s32[1,256]{1,0:T(1,128)S(1)} %bitcast.15, ...), custom_call_target="tpu_custom_call" | custom-call | flops 167772160 | bytes 4194304 | tf_op jit(solution)/shard_map/pallas_call | solution.py:69
  8.9 7.4 %all-to-all-start = ((bf16[16,8,2176]{2,1,0:T(8,128)(2,1)}), bf16[16,8,2176]{2,1,0:T(8,128)(2,1)S(1)}, u32[]{:S(2)}, u32[]{:S(2)}) async-start(bf16[16,8,2176]{2,1,0:T(8,128)(2,1)} %bitcast.5), calls=%async_computation | async-start | bytes 1114112 | tf_op jit(solution)/shard_map/all_to_all | solution.py:589
  16.3 5.3 %collective-permute-start.1 = (bf16[24,1024]{1,0:T(8,128)(2,1)S(1)}, bf16[24,1024]{1,0:T(8,128)(2,1)S(1)}, u32[]{:S(2)}, u32[]{:S(2)}) collective-permute-start(bf16[24,1024]{1,0:T(8,128)(2,1)S(1)} %get-tuple-element.24), channel_id=1, source_target_pairs={{0,255},{255,0},{1,2},{2,1},{3,4},{4,3},{5,6},{6,5},{7,8},{8,7},{9... | collective-permute-start | bytes 147464 | tf_op jit(solution)/shard_map/ppermute | solution.py:586
  21.6 5.1 %shard_map.114.begun = f32[16,2048]{1,0:T(8,128)} custom-call(bf16[8,8192]{1,0:T(8,128)(2,1)S(1)} %get-tuple-element.16.vt.vt_in, bf16[8,8192]{1,0:T(8,128)(2,1)S(1)} %get-tuple-element.20.pt.pt_in, bf16[8,5120]{1,0:T(8,128)(2,1)S(1)} %collective-permute-done.rec_c.c_in), custom_call_target="tpu_custom_call" | custom-call | flops 4966055936 | bytes 1048576 | tf_op jit(solution)/shard_map/pallas_call | solution.py:69
  26.7 1.3 %shard_map.112.coup_in = bf16[512,64]{1,0:T(8,128)(2,1)S(1)} custom-call(bf16[64,64,254]{2,1,0:T(8,128)(2,1)S(1)} %bitcast.13, bf16[128,2176]{1,0:T(8,128)(2,1)} %get-tuple-element.22.seen), custom_call_target="tpu_custom_call" | custom-call | flops 16777216 | bytes 3145728 | tf_op jit(solution)/shard_map/pallas_call | solution.py:69
  28.1 0.0 all-to-all-done
  28.1 3.0 %shard_map.113 = bf16[256,512]{1,0:T(8,128)(2,1)} custom-call(bf16[128,2176]{1,0:T(8,128)(2,1)S(1)} %bitcast.10, f32[32,64]{1,0:T(8,128)S(1)} %get-tuple-element.18.path.path_in, bf16[2560,64]{1,0:T(8,128)(2,1)S(1)} %get-tuple-element.23.mats_in, bf16[512,64]{1,0:T(8,128)(2,1)S(1)} %shard_map.112.coup_in), custom_call_target="tpu_custom_call" | custom-call | flops 134217728 | bytes 2097152 | tf_op jit(solution)/shard_map/pallas_call | solution.py:69
  31.1 7.8 %all-to-all-start.1 = ((bf16[8,32,512]{2,1,0:T(8,128)(2,1)}), bf16[8,32,512]{2,1,0:T(8,128)(2,1)S(1)}, u32[]{:S(2)}, u32[]{:S(2)}) async-start(bf16[8,32,512]{2,1,0:T(8,128)(2,1)} %bitcast.8), calls=%async_computation.1 | async-start | bytes 524288 | tf_op jit(solution)/shard_map/all_to_all | solution.py:622
  38.9 0.0 collective-permute-done.1.halo_in
  38.9 6.5 %shard_map.115 = (f32[8,4096]{1,0:T(8,128)S(1)}, f32[8,4096]{1,0:T(8,128)S(1)}) custom-call(bf16[8,8192]{1,0:T(8,128)(2,1)S(1)} %get-tuple-element.16.vt.vt_in, bf16[8,8192]{1,0:T(8,128)(2,1)S(1)} %get-tuple-element.20.pt.pt_in, bf16[8,5120]{1,0:T(8,128)(2,1)S(1)} %collective-permute-done.rec_c.c_in, bf16[24,1024]{1,0:T(8,128)(2,1)S(1)} %collective-permute-done.1.halo_in, ...), custom_call_target="tpu_custom_call" | custom-call | flops 4026531840 | bytes 1048576 | tf_op jit(solution)/shard_map/pallas_call | solution.py:69
  45.4 0.1 collective-permute-start.2
  45.5 1.3 %collective-permute-done.2.other_in = f32[8,4096]{1,0:T(8,128)S(1)} collective-permute-done((f32[8,4096]{1,0:T(8,128)S(1)}, f32[8,4096]{1,0:T(8,128)S(1)}, u32[]{:S(2)}, u32[]{:S(2)}) %collective-permute-start.2) | collective-permute-done | bytes 131104 | tf_op jit(solution)/shard_map/ppermute | solution.py:632
  46.8 2.5 %all-to-all-done.1 = bf16[8,32,512]{2,1,0:T(8,128)(2,1)S(1)} async-done(((bf16[8,32,512]{2,1,0:T(8,128)(2,1)}), bf16[8,32,512]{2,1,0:T(8,128)(2,1)S(1)}, u32[]{:S(2)}, u32[]{:S(2)}) %all-to-all-start.1) | async-done | bytes 262176 | tf_op jit(solution)/shard_map/all_to_all | solution.py:622
  49.3 4.5 %shard_map.116 = bf16[8,8192]{1,0:T(8,128)(2,1)} custom-call(bf16[256,512]{1,0:T(8,128)(2,1)S(1)} %bitcast.14, f32[8,4096]{1,0:T(8,128)S(1)} %get-tuple-element.25.mine_in, f32[8,4096]{1,0:T(8,128)S(1)} %collective-permute-done.2.other_in, bf16[2560,64]{1,0:T(8,128)(2,1)S(1)} %get-tuple-element.23.mats_in, bf16[30,64,64]{2,1,0:T(8,128)(2,1)S(1)} %copy-done.4, ...), custom_call_target="tpu_custom_call" | custom-call | flops 1073741824 | bytes 8388608 | tf_op jit(solution)/shard_map/pallas_call | solution.py:69
  (10 shorter events, 0.0 us)
Async XLA Ops:
  0.0 3.1 %copy-start = (bf16[254,64,64]{0,2,1:T(8,128)(2,1)S(1)}, bf16[254,64,64]{0,2,1:T(8,128)(2,1)}, u32[]{:S(2)}) copy-start(bf16[254,64,64]{0,2,1:T(8,128)(2,1)} %param.20) | copy-start | bytes 6242308
  0.0 3.1 %copy-start.7 = (s32[256,1]{0,1:T(1,128)S(1)}, s32[256,1]{0,1:T(1,128)}, u32[]{:S(2)}) copy-start(s32[256,1]{0,1:T(1,128)} %param.18) | copy-start | bytes 3076
  0.0 3.1 %copy-start.3 = (bf16[16,64,512]{2,1,0:T(8,128)(2,1)S(1)}, bf16[16,64,512]{2,1,0:T(8,128)(2,1)}, u32[]{:S(2)}) copy-start(bf16[16,64,512]{2,1,0:T(8,128)(2,1)} %bases.3) | copy-start | bytes 3145732
  0.0 3.1 %copy-start.4 = (bf16[30,64,64]{2,1,0:T(8,128)(2,1)S(1)}, bf16[30,64,64]{2,1,0:T(8,128)(2,1)}, u32[]{:S(2)}) copy-start(bf16[30,64,64]{2,1,0:T(8,128)(2,1)} %tr.3) | copy-start | bytes 737284
  3.0 2.0 %copy-start.1 = (bf16[256,64,64]{0,2,1:T(8,128)(2,1)S(1)}, bf16[256,64,64]{0,2,1:T(8,128)(2,1)}, u32[]{:S(2)}) copy-start(bf16[256,64,64]{0,2,1:T(8,128)(2,1)} %param.16) | copy-start | bytes 6291460
  3.0 2.0 %copy-start.5 = (s32[256]{0:T(256)S(1)}, s32[256]{0:T(256)}, u32[]{:S(2)}) copy-start(s32[256]{0:T(256)} %param.17) | copy-start | bytes 3076
  3.0 2.0 %copy-start.6 = (s32[256]{0:T(256)S(1)}, s32[256]{0:T(256)}, u32[]{:S(2)}) copy-start(s32[256]{0:T(256)} %param.19) | copy-start | bytes 3076
  3.0 2.0 %collective-permute-start = (bf16[8,5120]{1,0:T(8,128)(2,1)S(1)}, bf16[8,5120]{1,0:T(8,128)(2,1)S(1)}, u32[]{:S(2)}, u32[]{:S(2)}) collective-permute-start(bf16[8,5120]{1,0:T(8,128)(2,1)S(1)} %get-tuple-element.21), channel_id=1, source_target_pairs={{0,1},{1,0},{2,3},{3,2},{4,5},{5,4},{6,7},{7,6},{8,9},{9,8},{10,11... | collective-permute-start | bytes 245768 | tf_op jit(solution)/shard_map/ppermute | solution.py:566
  8.9 19.2 %all-to-all-start = ((bf16[16,8,2176]{2,1,0:T(8,128)(2,1)}), bf16[16,8,2176]{2,1,0:T(8,128)(2,1)S(1)}, u32[]{:S(2)}, u32[]{:S(2)}) async-start(bf16[16,8,2176]{2,1,0:T(8,128)(2,1)} %bitcast.5), calls=%async_computation | async-start | bytes 1114112 | tf_op jit(solution)/shard_map/all_to_all | solution.py:589
  16.3 10.4 %copy-start.2 = (bf16[254,64,64]{0,2,1:T(8,128)(2,1)S(1)}, bf16[254,64,64]{0,2,1:T(8,128)(2,1)}, u32[]{:S(2)}) copy-start(bf16[254,64,64]{0,2,1:T(8,128)(2,1)} %param.21) | copy-start | bytes 6242308
  16.3 22.5 %collective-permute-start.1 = (bf16[24,1024]{1,0:T(8,128)(2,1)S(1)}, bf16[24,1024]{1,0:T(8,128)(2,1)S(1)}, u32[]{:S(2)}, u32[]{:S(2)}) collective-permute-start(bf16[24,1024]{1,0:T(8,128)(2,1)S(1)} %get-tuple-element.24), channel_id=1, source_target_pairs={{0,255},{255,0},{1,2},{2,1},{3,4},{4,3},{5,6},{6,5},{7,8},{8,7},{9... | collective-permute-start | bytes 147464 | tf_op jit(solution)/shard_map/ppermute | solution.py:586
  31.1 18.3 %all-to-all-start.1 = ((bf16[8,32,512]{2,1,0:T(8,128)(2,1)}), bf16[8,32,512]{2,1,0:T(8,128)(2,1)S(1)}, u32[]{:S(2)}, u32[]{:S(2)}) async-start(bf16[8,32,512]{2,1,0:T(8,128)(2,1)} %bitcast.8), calls=%async_computation.1 | async-start | bytes 524288 | tf_op jit(solution)/shard_map/all_to_all | solution.py:622
  45.4 1.4 %collective-permute-start.2 = (f32[8,4096]{1,0:T(8,128)S(1)}, f32[8,4096]{1,0:T(8,128)S(1)}, u32[]{:S(2)}, u32[]{:S(2)}) collective-permute-start(f32[8,4096]{1,0:T(8,128)S(1)} %get-tuple-element.26), channel_id=1, source_target_pairs={{0,1},{1,0},{2,3},{3,2},{4,5},{5,4},{6,7},{7,6},{8,9},{9,8},{10,11... | collective-permute-start | bytes 393224 | tf_op jit(solution)/shard_map/ppermute | solution.py:632
